TPU v7x, 32 devices: a whole 2x2x4 slice. The times are simulated.
32 devices in a mesh: wide: 8 (over z, x), narrow: 4 (over y, core).
Axes of the slice: x: 2, y: 2, z: 4, core: 2. Of those that a mesh axis runs over, the one named last changes fastest.
Arguments:
- tokens: bfloat16 [32, 512, 768], P(('wide', 'narrow')), may hold values from -6 to 6
- lengths: int32 [32, 2], P(('wide', 'narrow')), may hold values from 8 to 504, as said below
- buckets: int32 [1023], replicated, may hold values from 0 to 255
- query_weight: bfloat16 [768, 768], P(('wide', 'narrow')), may hold values from -0.21875 to 0.21875
- query_bias: bfloat16 [768], P(('wide', 'narrow')), may hold values from -3 to 3
- key_weight: bfloat16 [768, 768], P(('wide', 'narrow')), may hold values from -0.21875 to 0.21875
- key_bias: bfloat16 [768], P(('wide', 'narrow')), may hold values from -3 to 3
- value_weight: bfloat16 [768, 768], P(('wide', 'narrow')), may hold values from -0.21875 to 0.21875
- value_bias: bfloat16 [768], P(('wide', 'narrow')), may hold values from -3 to 3
- output_weight: bfloat16 [768, 768], P(('wide', 'narrow')), may hold values from -0.875 to 0.875
- output_bias: bfloat16 [768], P(('wide', 'narrow')), may hold values from -3 to 3
- relative_table: bfloat16 [256, 768], P(('wide', 'narrow')), may hold values from -6 to 6
- first_gain: bfloat16 [768], P(('wide', 'narrow')), may hold values from 0.5 to 1.5
- first_shift: bfloat16 [768], P(('wide', 'narrow')), may hold values from -3 to 3
- inner_weight: bfloat16 [768, 3072], P(('wide', 'narrow')), may hold values from -0.21875 to 0.21875
- inner_bias: bfloat16 [3072], P(('wide', 'narrow')), may hold values from -3 to 3
- outer_weight: bfloat16 [3072, 768], P(('wide', 'narrow')), may hold values from -0.109375 to 0.109375
- outer_bias: bfloat16 [768], P(('wide', 'narrow')), may hold values from -3 to 3
- second_gain: bfloat16 [768], P(('wide', 'narrow')), may hold values from 0.5 to 1.5
- second_shift: bfloat16 [768], P(('wide', 'narrow')), may hold values from -3 to 3
- cotangent: bfloat16 [32, 512, 768], P(('wide', 'narrow')), may hold values from -6 to 6
Outputs:
- layer_out: bfloat16 [32, 512, 768], P(('wide', 'narrow'))
- tokens_grad: float32 [32, 512, 768], P(('wide', 'narrow'))
- query_weight_grad: float32 [768, 768], P(('wide', 'narrow'))
- query_bias_grad: float32 [768], P(('wide', 'narrow'))
- key_weight_grad: float32 [768, 768], P(('wide', 'narrow'))
- key_bias_grad: float32 [768], P(('wide', 'narrow'))
- value_weight_grad: float32 [768, 768], P(('wide', 'narrow'))
- value_bias_grad: float32 [768], P(('wide', 'narrow'))
- output_weight_grad: float32 [768, 768], P(('wide', 'narrow'))
- output_bias_grad: float32 [768], P(('wide', 'narrow'))
- relative_table_grad: float32 [256, 768], P(('wide', 'narrow'))
- first_gain_grad: float32 [768], P(('wide', 'narrow'))
- first_shift_grad: float32 [768], P(('wide', 'narrow'))
- inner_weight_grad: float32 [768, 3072], P(('wide', 'narrow'))
- inner_bias_grad: float32 [3072], P(('wide', 'narrow'))
- outer_weight_grad: float32 [3072, 768], P(('wide', 'narrow'))
- outer_bias_grad: float32 [768], P(('wide', 'narrow'))
- second_gain_grad: float32 [768], P(('wide', 'narrow'))
- second_shift_grad: float32 [768], P(('wide', 'narrow'))
Inputs may be any that keep to these rules, and one draw needn't show every extreme that they name: lengths[p, 0] is pair p's query length, 8 to 64; lengths[p, 1] is its passage length, 112 or more; the two sum to at most 512, and to exactly 512 in some pair of every draw, whose query length is 8.
All inputs are finite; a program needn't handle non-finite values.
Results may differ from a plain program's by a relative error of at most 0.025.
Values may be sent and summed in bfloat16 or wider, within the bound.
No kernel may reach another device: no remote copies, remote signals or barrier semaphores. Data moves between devices by JAX's collectives and lax.ppermute only.
A program may use at most 256 MiB of HBM per device.

v0:
```python
import jax
import jax.numpy as jnp
from jax import lax
from jax.experimental import pallas as pl
from jax.experimental.pallas import tpu as pltpu
from jax.sharding import PartitionSpec as P

HD = 64
EPSILON = 1e-05
MASKED = -1000000000.0
AXES = ("wide", "narrow")
BF = jnp.bfloat16
F32 = jnp.float32
NT = (((1,), (1,)), ((), ()))
NN = (((1,), (0,)), ((), ()))
TN = (((0,), (0,)), ((), ()))


def dot(left, right, dims):
    return lax.dot_general(left, right, dims, preferred_element_type=F32)


def half_lanes(block):
    first = lax.broadcasted_iota(jnp.int32, (1, 128), 1) < HD
    return jnp.where(first, block, 0).astype(BF), jnp.where(first, 0, block).astype(BF)


def stacked(block):
    return jnp.concatenate(half_lanes(block), axis=0)


def attend_kernel(tot_ref, q_ref, k_ref, v_ref, kr_ref, qr_ref, c_ref, p_ref, t_ref, *, rows, tile):
    span = rows + tile
    scale = (3.0 * HD) ** (-0.5) * 1.4426950408889634
    column = lax.broadcasted_iota(jnp.int32, (1, rows), 1)
    valid = column < tot_ref[0]

    def skewed(grid_scores):
        return pltpu.roll(grid_scores, span - (tile - 1), 1, stride=1, stride_axis=0)[:, :rows]

    values = stacked(v_ref[...])
    for b in range(rows // tile):
        sl = slice(b * tile, (b + 1) * tile)
        low = rows - tile - b * tile
        grid_scores = dot(stacked(k_ref[sl, :]), qr_ref[low : low + span, :], NT)
        for head in range(2):
            t_ref[head, sl, :] = skewed(grid_scores[head * tile : (head + 1) * tile])
    for b in range(rows // tile):
        sl = slice(b * tile, (b + 1) * tile)
        low = rows - tile - b * tile
        q = stacked(q_ref[sl, :])
        grid_scores = dot(q, kr_ref[low : low + span, :], NT)
        raw = (
            dot(q, k_ref[...], NT)
            + jnp.concatenate([skewed(grid_scores[:tile]), skewed(grid_scores[tile:])], axis=0)
            + jnp.concatenate([t_ref[0, :, sl].T, t_ref[1, :, sl].T], axis=0)
        )
        scores = jnp.where(valid, raw * scale, MASKED)
        top = jnp.max(scores, axis=-1, keepdims=True)
        expd = jnp.exp2(scores - top)
        probs = (expd * (1.0 / jnp.sum(expd, axis=-1, keepdims=True))).astype(BF)
        p_ref[0, sl, :] = probs[:tile]
        p_ref[1, sl, :] = probs[tile:]
        both = jnp.concatenate([probs[:tile], probs[tile:]], axis=1)
        c_ref[sl, :] = dot(both, values, NN).astype(BF)


def attend(total, q, k, v, kr, qr):
    rows, width = q.shape
    groups = width // 128
    cols = lambda r: pl.BlockSpec((r, 128), lambda p: (0, p))
    return pl.pallas_call(
        lambda *refs: attend_kernel(*refs, rows=rows, tile=rows // 2),
        grid=(groups,),
        in_specs=[pl.BlockSpec(memory_space=pltpu.SMEM)]
        + [cols(rows)] * 3
        + [cols(2 * rows)] * 2,
        out_specs=[cols(rows), pl.BlockSpec((2, rows, rows), lambda p: (p, 0, 0))],
        out_shape=[
            jax.ShapeDtypeStruct((rows, width), BF),
            jax.ShapeDtypeStruct((2 * groups, rows, rows), BF),
        ],
        scratch_shapes=[pltpu.VMEM((2, rows, rows), F32)],
        compiler_params=pltpu.CompilerParams(vmem_limit_bytes=60 << 20),
        cost_estimate=pl.CostEstimate(
            flops=25 << 30, bytes_accessed=12 << 20, transcendentals=12 * rows * rows
        ),
        name="attend",
    )(total, q, k, v, kr, qr)


def attend_back_kernel(
    q_ref, k_ref, v_ref, kr_ref, qr_ref, dc_ref, p_ref, onehot_ref, *refs, rows, tile,
):
    d_ref, pos_ref, ds_ref, dqr_ref, dkr_ref = refs[-5:]
    dq_ref, dk_ref, dv_ref = d_ref.at[0], d_ref.at[1], d_ref.at[2]
    span = rows + tile
    scale = (3.0 * HD) ** (-0.5)
    upper = lax.broadcasted_iota(jnp.int32, (128, 1), 0) < HD
    flip = (
        lax.broadcasted_iota(jnp.int32, (tile, tile), 0)
        + lax.broadcasted_iota(jnp.int32, (tile, tile), 1)
        == tile - 1
    ).astype(BF)
    dkr_ref[...] = jnp.zeros_like(dkr_ref)
    dqr_ref[...] = jnp.zeros_like(dqr_ref)
    zeros = jnp.zeros((tile, tile), F32)
    beside = lambda *parts: jnp.concatenate(parts, axis=1)
    above = lambda *parts: jnp.concatenate(parts, axis=0)

    def unskewed(flipped):
        return pltpu.roll(beside(flipped, zeros), 0, 1, stride=1, stride_axis=0).astype(BF)

    def turned(block):
        across = block.T
        return beside(jnp.where(upper, across, 0), jnp.where(upper, 0, across)).astype(BF)

    keys, queries = stacked(k_ref[...]), stacked(q_ref[...])
    kr, qr = half_lanes(kr_ref[...]), half_lanes(qr_ref[...])
    dvt = jnp.zeros((128, rows), F32)
    for b in range(rows // tile):
        sl = slice(b * tile, (b + 1) * tile)
        low = rows - tile - b * tile
        high = low + span
        dc = dc_ref[sl, :]
        dp = dot(stacked(dc), v_ref[...], NT)
        pb = above(p_ref[0, sl, :], p_ref[1, sl, :])
        p = pb.astype(F32)
        pdp = p * dp
        delta = jnp.sum(pdp, axis=-1, keepdims=True)
        ds = ((pdp - p * delta) * scale).astype(BF)
        dsa, dsb = ds[:tile], ds[tile:]
        ds_ref[0, sl, :] = dsa
        ds_ref[1, sl, :] = dsb
        dvt = dvt + dot(turned(dc.astype(F32)), pb, NN)
        da, db = unskewed(dot(flip, dsa, NN)), unskewed(dot(flip, dsb, NN))
        rel = dot(beside(da, db), above(kr[0][low:high], kr[1][low:high]), NN).astype(BF)
        dq_ref[sl, :] = (dot(beside(dsa, dsb), keys, NN) + dot(flip, rel, NN)).astype(BF)
        dkr_ref[:, low:high] += dot(turned(dot(flip, q_ref[sl, :], NN)), above(da, db), NN)
    dv_ref[...] = dvt.T.astype(BF)
    for b in range(rows // tile):
        sl = slice(b * tile, (b + 1) * tile)
        low = rows - tile - b * tile
        high = low + span
        ta, tb = dot(flip, ds_ref[0, :, sl], NT), dot(flip, ds_ref[1, :, sl], NT)
        da, db = unskewed(ta), unskewed(tb)
        dk = dot(
            beside(ta.astype(BF), tb.astype(BF), da, db),
            above(queries, qr[0][low:high], qr[1][low:high]),
            NN,
        )
        dk_ref[sl, :] = dot(flip, dk.astype(BF), NN).astype(BF)
        dqr_ref[:, low:high] += dot(turned(dot(flip, k_ref[sl, :], NN)), above(da, db), NN)
    pos_ref[0] = dot(dqr_ref[...].astype(BF), onehot_ref[...], NN)
    pos_ref[1] = dot(dkr_ref[...].astype(BF), onehot_ref[...], NN)


def attend_back(q, k, v, kr, qr, dc, probs, onehot, first, groups, before):
    rows, width = q.shape
    buckets = onehot.shape[1]
    cols = lambda r: pl.BlockSpec((r, 128), lambda p: (0, first + p))
    skip = [pl.BlockSpec(memory_space=pl.ANY)] * len(before)
    share = groups / (width // 128)
    return pl.pallas_call(
        lambda *refs: attend_back_kernel(*refs, rows=rows, tile=rows // 2),
        grid=(groups,),
        in_specs=[cols(rows)] * 3
        + [cols(2 * rows)] * 2
        + [cols(rows), pl.BlockSpec((2, rows, rows), lambda p: (first + p, 0, 0)),
           pl.BlockSpec((2 * rows, buckets), lambda p: (0, 0))]
        + skip,
        out_specs=[
            pl.BlockSpec((3, rows, 128), lambda p: (0, 0, first + p)),
            pl.BlockSpec((2, 128, buckets), lambda p: (0, first + p, 0)),
        ],
        out_shape=[
            jax.ShapeDtypeStruct((3, rows, width), BF),
            jax.ShapeDtypeStruct((2, width, buckets), F32),
        ],
        scratch_shapes=[pltpu.VMEM((2, rows, rows), BF)] + [pltpu.VMEM((128, 2 * rows), F32)] * 2,
        compiler_params=pltpu.CompilerParams(vmem_limit_bytes=60 << 20),
        input_output_aliases={8 + i: i for i in range(len(before))},
        cost_estimate=pl.CostEstimate(
            flops=int(40e9 * share), bytes_accessed=int(18e6 * share), transcendentals=0
        ),
        name="attend_back",
    )(q, k, v, kr, qr, dc, probs, onehot, *before)


STRIPES = 32
VECTORS = 10


def cost(flops, moved, transcendentals=0):
    return pl.CostEstimate(flops=flops, bytes_accessed=moved, transcendentals=transcendentals)


def big(megabytes=60):
    return pltpu.CompilerParams(vmem_limit_bytes=megabytes << 20)


def stripe_marks(width, dtype):
    part = width // STRIPES
    column = lax.broadcasted_iota(jnp.int32, (STRIPES, width), 1)
    stripe = lax.broadcasted_iota(jnp.int32, (STRIPES, width), 0)
    owner = (column >= stripe * part) & (column < stripe * part + part)
    place = lax.broadcasted_iota(jnp.int32, (128, width), 0)
    spot = (lax.broadcasted_iota(jnp.int32, (128, width), 1) % part == place).astype(dtype)
    return owner, spot


def pack_kernel(*refs, mats, vectors, fan):
    first_ref, second_ref = refs[-2:]
    at = 0
    for ref in refs[:mats]:
        first_ref[at : at + ref.shape[0], :] = ref[...]
        at += ref.shape[0]
    first_ref[at:, :] = jnp.zeros_like(first_ref[at:, :])
    for i, ref in enumerate(refs[mats : mats + vectors]):
        lane = 0 if i < 8 else 128
        first_ref[at + i % 8 : at + i % 8 + 1, lane : lane + ref.shape[0]] = ref[...].reshape(1, -1)
    outer_ref, inner_ref, output_ref = refs[mats + vectors : mats + vectors + 3]
    width = outer_ref.shape[1]
    at = outer_ref.shape[0]
    second_ref[:at, :] = outer_ref[...]
    for f in range(fan):
        rows = inner_ref.shape[0]
        second_ref[at : at + rows, :] = inner_ref[:, f * width : (f + 1) * width]
        at += rows
    second_ref[at:, :] = output_ref[...]


def pack(mats, vectors, outer, inner, output, fan):
    width = outer.shape[1]
    first = sum(m.shape[0] for m in mats) + 8
    second = outer.shape[0] + fan * inner.shape[0] + output.shape[0]
    return pl.pallas_call(
        lambda *refs: pack_kernel(*refs, mats=len(mats), vectors=len(vectors), fan=fan),
        out_shape=[jax.ShapeDtypeStruct((first, width), BF), jax.ShapeDtypeStruct((second, width), BF)],
        name="pack",
    )(*mats, *vectors, outer, inner, output)


def project_kernel(where_ref, *refs, fan):
    blocks, (x_ref, bucket_ref) = refs[:10], refs[10:12]
    q_ref, k_ref, v_ref, kr_ref, qr_ref, vecs_ref, w_ref, onehot_ref, xt_ref, tt_ref = refs[12:22]
    table_ref, vec_ref = refs[22:]
    step = pl.program_id(0)
    width = x_ref.shape[1]
    span = q_ref.shape[1]
    buckets = onehot_ref.shape[1]
    me = where_ref[0]

    def place(out, near, far):
        for r in range(STRIPES // 2):
            for ref, core in ((near, 0), (far, 1)):
                out[me ^ ((r // 4) * 2 + (r % 4) * 8 + core)] = ref[r]

    for i in range(3):
        place(w_ref.at[i], blocks[2 * i], blocks[2 * i + 1])

    @pl.when(step == 0)
    def _():
        place(table_ref, blocks[6], blocks[7])
        place(vec_ref, blocks[8], blocks[9])
        xt_ref[...] = x_ref[...].T
        tt_ref[...] = table_ref.reshape(buckets, width)[...].T
        index = lax.broadcasted_iota(jnp.int32, onehot_ref.shape, 1)
        onehot_ref[...] = (bucket_ref[...] == index).astype(F32).astype(BF)
        owner, spot = stripe_marks(width, BF)
        vecs_ref[...] = jnp.zeros_like(vecs_ref)

        def spread(block, marks, mine):
            return jnp.sum(jnp.where(mine, dot(block, marks, NN), 0.0), axis=0, keepdims=True)

        for i in range(VECTORS - 1):
            lanes = slice(0, 128) if i < 8 else slice(128, 256)
            vecs_ref[i : i + 1, :] = spread(vec_ref[:, i % 8, lanes], spot, owner)
        block = vec_ref[:, (VECTORS - 1) % 8, 128:256]
        part = width * fan // STRIPES
        for f in range(fan):
            column = lax.broadcasted_iota(jnp.int32, (STRIPES, width), 1) + f * width
            stripe = lax.broadcasted_iota(jnp.int32, (STRIPES, width), 0)
            mine = (column >= stripe * part) & (column < stripe * part + part)
            place_at = lax.broadcasted_iota(jnp.int32, (128, width), 0)
            marks = lax.broadcasted_iota(jnp.int32, (128, width), 1) + f * width
            marks = (marks % part == place_at).astype(BF)
            row = VECTORS - 1 + f
            vecs_ref[row : row + 1, :] = spread(block, marks, mine)

    x = x_ref[...]
    table = table_ref.reshape(buckets, width)[...]
    columns = pl.ds(pl.multiple_of(step * span, 128), span)
    bias = [vecs_ref[i : i + 1, columns] for i in range(3)]
    mats = [w_ref.at[i].reshape(width, span)[...] for i in range(3)]
    for i, out in enumerate((q_ref, k_ref, v_ref)):
        out[...] = (dot(x, mats[i], NN) + bias[i]).astype(BF)
    for i, out in ((0, qr_ref), (1, kr_ref)):
        pos = (dot(table, mats[i], NN) + bias[i]).astype(BF)
        out[...] = dot(onehot_ref[...], pos, NN).astype(BF)


def project_all(where, near, far, x, bucket_column, fan):
    rows, width = x.shape
    part = width // STRIPES
    span = 256
    weight = lambda i: [pl.BlockSpec((STRIPES // 2, part, span), lambda p: (0, i, p))] * 2
    small = lambda i: [pl.BlockSpec((STRIPES // 2, 8, width), lambda p: (0, i, 0))] * 2
    buckets = 8 * STRIPES
    whole = lambda shape: pl.BlockSpec(shape, lambda p: (0,) * len(shape))
    cols = lambda r: pl.BlockSpec((r, span), lambda p: (0, p))
    shape = jax.ShapeDtypeStruct
    out = lambda r: shape((r, width), BF)
    return pl.pallas_call(
        lambda *refs: project_kernel(*refs, fan=fan),
        grid=(width // span,),
        in_specs=[pl.BlockSpec(memory_space=pltpu.SMEM)] + weight(0) + weight(1) + weight(2)
        + small(3 * part // 8) + small(3 * part // 8 + 1)
        + [whole((rows, width)), whole((2 * rows, 1))],
        out_specs=[cols(rows)] * 3 + [cols(2 * rows)] * 2
        + [whole((16, width)), pl.BlockSpec((3, STRIPES, part, span), lambda p: (0, 0, 0, p)),
           whole((2 * rows, buckets)), whole((width, rows)), whole((width, buckets))],
        out_shape=[out(rows)] * 3 + [out(2 * rows)] * 2
        + [shape((16, width), F32), shape((3, STRIPES, part, width), BF), shape((2 * rows, buckets), BF),
           shape((width, rows), BF), shape((width, buckets), BF)],
        scratch_shapes=[pltpu.VMEM((STRIPES, 8, width), BF)] * 2,
        compiler_params=big(),
        cost_estimate=cost(4 << 30, 12 << 20),
        name="project",
    )(where, *([near, far] * 5), x, bucket_column)


def normal_parts(hidden):
    centered = hidden - jnp.mean(hidden, axis=-1, keepdims=True)
    inverse = lax.rsqrt(jnp.mean(centered * centered, axis=-1, keepdims=True) + EPSILON)
    return centered * inverse, inverse


def normal_back(upstream, normed, inverse, gain):
    scaled = upstream * gain
    return inverse * (
        scaled
        - jnp.mean(scaled, axis=-1, keepdims=True)
        - normed * jnp.mean(scaled * normed, axis=-1, keepdims=True)
    )


def halves_to(keep_ref, send_ref, grad, own):
    part = keep_ref.shape[1]
    blocks = grad.reshape((grad.shape[0] // (2 * part), 2, part, grad.shape[1]))
    even, odd = blocks[:, 0].astype(BF), blocks[:, 1].astype(BF)

    @pl.when(own == 0)
    def _():
        keep_ref[...] = even
        send_ref[...] = odd

    @pl.when(own != 0)
    def _():
        keep_ref[...] = odd
        send_ref[...] = even


def feed_kernel(where_ref, vecs_ref, ctx_hbm, x_hbm, cot_hbm, packed_hbm,
                out_hbm, outer_hbm, keep_hbm, send_hbm, cg_hbm, fg_hbm, vg_ref,
                ctx, x, cot, wo, wi, w2, act, slope, low, turned, og, n1, inv, acc, first,
                stage, keep, send, fetch, chunk_fetch, flush, outer_flush, keep_flush, *, fan):
    rows, width = ctx.shape
    part = width // STRIPES
    own = where_ref[1]
    vec = lambda i: vecs_ref[i : i + 1, :]
    column = lambda a: jnp.sum(a, axis=0, keepdims=True)
    copy = pltpu.make_async_copy
    ins = [copy(ctx_hbm, ctx, fetch.at[0]),
           copy(packed_hbm.at[:, pl.ds(2 * fan * part, part), :], wo, fetch.at[1]),
           copy(x_hbm, x, fetch.at[2]), copy(cot_hbm, cot, fetch.at[3])]

    def chunk_copies(f):
        inner = pl.ds(pl.multiple_of((fan + f) * part, 8), part)
        outer = pl.ds(f * (STRIPES // fan), STRIPES // fan)
        return (copy(packed_hbm.at[:, inner, :], wi.at[f], chunk_fetch.at[0, f]),
                copy(packed_hbm.at[outer, pl.ds(0, fan * part), :], w2.at[f], chunk_fetch.at[1, f]))

    for one in ins[:3]:
        one.start()
    for f in range(fan):
        for one in chunk_copies(f):
            one.start()
    ins[3].start()
    vg_ref[...] = jnp.zeros_like(vg_ref)
    ins[0].wait()
    ins[1].wait()
    attended = dot(ctx[...], wo.reshape(width, width)[...], NN) + vec(3)
    ins[2].wait()
    normed, inverse = normal_parts(x[...].astype(F32) + attended)
    n1[...] = normed
    inv[...] = jnp.broadcast_to(inverse, inv.shape)
    start = normed * vec(4) + vec(5)
    low[...] = start.astype(BF)
    acc[...] = start + vec(6)

    def forward(f, carry):
        for one in chunk_copies(f):
            one.wait()
        pre = dot(low[...], wi.at[f].reshape(width, width)[...], NN) + vecs_ref[pl.ds(9 + f, 1), :]
        half = 0.5 + 0.5 * lax.erf(pre * 0.7071067811865476)
        active = (pre * half).astype(BF)
        act[f] = active
        slope[f] = (half + pre * (jnp.exp(-0.5 * pre * pre) * 0.3989422804014327)).astype(BF)
        acc[...] += dot(active, w2.at[f].reshape(width, width)[...], NN)
        return carry

    lax.fori_loop(0, fan, forward, 0)
    turned[...] = low[...].T
    normed, inverse = normal_parts(acc[...])
    low[...] = (normed * vec(7) + vec(8)).astype(BF)
    outs = [copy(low, out_hbm, flush.at[0]), copy(cot, cg_hbm, flush.at[1]), copy(first, fg_hbm, flush.at[2])]
    outs[0].start()
    ins[3].wait()
    upstream = cot[...].astype(F32)
    vg_ref[8:9, :] = column(upstream * normed)
    vg_ref[9:10, :] = column(upstream)
    second = normal_back(upstream, normed, inverse, vec(7))
    acc[...] = second
    og[...] = second.astype(BF)
    vg_ref[10:11, :] = column(og[...].astype(F32))

    def outer_copy(f):
        return copy(stage.at[f % 2], outer_hbm.at[pl.ds(pl.multiple_of(f * width, 8), width), :],
                    outer_flush.at[f % 2])

    def outer_grad(f, carry):
        @pl.when(f >= 2)
        def _():
            outer_copy(f - 2).wait()

        stage[f % 2] = dot(act[f], og[...], TN).astype(BF)
        outer_copy(f).start()
        return carry

    lax.fori_loop(0, fan, outer_grad, 0)

    def keep_copies(f):
        place = pl.ds(pl.multiple_of(f * part, 8), part)
        return (copy(keep.at[f % 2], keep_hbm.at[:, place, :], keep_flush.at[0, f % 2]),
                copy(send.at[f % 2], send_hbm.at[:, place, :], keep_flush.at[1, f % 2]))

    def leave(f, grad):
        @pl.when(f >= 2)
        def _():
            for one in keep_copies(f - 2):
                one.wait()

        halves_to(keep.at[f % 2], send.at[f % 2], grad, own)
        for one in keep_copies(f):
            one.start()

    def backward(f, carry):
        grad = dot(og[...], w2.at[f].reshape(width, width)[...], NT) * slope[f].astype(F32)
        ig = grad.astype(BF)
        acc[...] += dot(ig, wi.at[f].reshape(width, width)[...], NT)
        vg_ref[pl.ds(f, 1), :] = column(ig.astype(F32))
        leave(f, dot(turned[...], ig, NN))
        return carry

    lax.fori_loop(0, fan, backward, 0)
    total = acc[...]
    normed = n1[...]
    vg_ref[4:5, :] = column(total * normed)
    vg_ref[5:6, :] = column(total)
    grad = normal_back(total, normed, inv[:, 0:1], vec(4))
    first[...] = grad
    outs[2].start()
    ag = grad.astype(BF)
    vg_ref[6:7, :] = column(ag.astype(F32))
    leave(fan, dot(ctx[...], ag, TN))
    cot[...] = dot(ag, wo.reshape(width, width)[...], NT).astype(BF)
    outs[1].start()
    for one in outs:
        one.wait()
    for f in (fan - 2, fan - 1):
        outer_copy(f).wait()
    for f in (fan - 1, fan):
        for one in keep_copies(f):
            one.wait()


def feed(where, vecs, ctx, x, cot, packed, fan):
    rows, width = x.shape
    part = width // STRIPES
    shape = jax.ShapeDtypeStruct
    hbm = pl.BlockSpec(memory_space=pl.ANY)
    half = shape((STRIPES // 2, part * (fan + 1), width), BF)
    low, high = pltpu.VMEM((rows, width), BF), pltpu.VMEM((rows, width), F32)
    sem = pltpu.SemaphoreType.DMA
    return pl.pallas_call(
        lambda *refs: feed_kernel(*refs, fan=fan),
        in_specs=[pl.BlockSpec(memory_space=pltpu.SMEM), pl.BlockSpec(memory_space=pltpu.VMEM)] + [hbm] * 4,
        out_specs=[hbm] * 6 + [pl.BlockSpec(memory_space=pltpu.VMEM)],
        out_shape=[shape((rows, width), BF), shape((fan * width, width), BF), half, half,
                   shape((rows, width), BF), shape((rows, width), F32), shape((16, width), F32)],
        scratch_shapes=[low, low, low, pltpu.VMEM((STRIPES, part, width), BF),
                        pltpu.VMEM((fan, STRIPES, part, width), BF),
                        pltpu.VMEM((fan, STRIPES // fan, part * fan, width), BF),
                        pltpu.VMEM((fan, rows, width), BF), pltpu.VMEM((fan, rows, width), BF), low,
                        pltpu.VMEM((width, rows), BF), low, high, pltpu.VMEM((rows, 128), F32), high, high,
                        pltpu.VMEM((2, width, width), BF)]
        + [pltpu.VMEM((2, STRIPES // 2, part, width), BF)] * 2
        + [sem((4,)), sem((2, fan)), sem((3,)), sem((2,)), sem((2, 2))],
        compiler_params=big(),
        name="feed",
    )(where, vecs, ctx, x, cot, packed)


def project_back_kernel(own_ref, d_ref, pos_ref, w_ref, xt_ref, tt_ref, vg2_ref,
                        keep_ref, send_ref, vec_ref, tab_ref, bias_ref, *, fan):
    step = pl.program_id(0)
    width, rows = xt_ref.shape
    buckets = tt_ref.shape[1]
    part = width // STRIPES
    own = own_ref[1]

    @pl.when(step == 0)
    def _():
        tab_ref[...] = jnp.zeros_like(tab_ref)

    @pl.when(step < 3)
    def _():
        d = d_ref[0]
        ones = jnp.ones((8, rows), BF)
        bias_ref[step] = dot(ones, d, NN)

        @pl.when(step < 2)
        def _():
            pos = pos_ref[0].astype(BF)
            tab_ref[...] += dot(w_ref.at[0].reshape(width, width)[...], pos, NN)
            bias_ref[step] += dot(jnp.ones((8, buckets), BF), pos, NT)
            grad = dot(xt_ref[...], d, NN) + dot(tt_ref[...], pos, NT)
            halves_to(keep_ref, send_ref, grad, own)

        @pl.when(step == 2)
        def _():
            halves_to(keep_ref, send_ref, dot(xt_ref[...], d, NN), own)

    @pl.when(step == 3)
    def _():
        vec_ref[...] = jnp.zeros_like(vec_ref)
        owner, spot = stripe_marks(width, BF)

        def cut(row, marks, mine):
            return dot(jnp.where(mine, jnp.broadcast_to(row, mine.shape), 0.0).astype(BF), marks, NT)

        bias = [bias_ref[i, 0:1, :] for i in range(3)]
        grads = bias + [vg2_ref[6:7, :], vg2_ref[4:5, :],
                        vg2_ref[5:6, :], vg2_ref[10:11, :], vg2_ref[8:9, :], vg2_ref[9:10, :]]
        for i, row in enumerate(grads):
            lanes = slice(0, 128) if i < 8 else slice(128, 256)
            vec_ref[:, i % 8, lanes] = cut(row, spot, owner)
        broad = width * fan // STRIPES
        total = jnp.zeros((STRIPES, 128), F32)
        for f in range(fan):
            column_at = lax.broadcasted_iota(jnp.int32, (STRIPES, width), 1) + f * width
            stripe = lax.broadcasted_iota(jnp.int32, (STRIPES, width), 0)
            mine = (column_at >= stripe * broad) & (column_at < stripe * broad + broad)
            place = lax.broadcasted_iota(jnp.int32, (128, width), 0)
            marks = lax.broadcasted_iota(jnp.int32, (128, width), 1) + f * width
            total += cut(vg2_ref[f : f + 1, :], (marks % broad == place).astype(BF), mine)
        vec_ref[:, (VECTORS - 1) % 8, 128:256] = total
        blocks = tab_ref[...].T.reshape((STRIPES // 2, 2, 8, width))
        vectors = vec_ref[...].reshape((STRIPES // 2, 2, 8, width))
        zero = jnp.zeros((STRIPES // 2, part - 16, width), BF)
        for out, pick in ((keep_ref, own == 0), (send_ref, own != 0)):
            out[:, 0:8] = jnp.where(pick, blocks[:, 0], blocks[:, 1]).astype(BF)
            out[:, 8:16] = jnp.where(pick, vectors[:, 0], vectors[:, 1]).astype(BF)
            out[:, 16:part] = zero


def project_back(own, d, pos, mats, xt, tt, vg, fan):
    width, rows = xt.shape
    part = width // STRIPES
    buckets = tt.shape[1]
    whole = lambda shape: pl.BlockSpec(shape, lambda g: (0,) * len(shape))
    block = pl.BlockSpec((STRIPES // 2, part, width), lambda g: (0, g, 0))
    shape = jax.ShapeDtypeStruct
    half = shape((STRIPES // 2, part * 4, width), BF)
    return pl.pallas_call(
        lambda *refs: project_back_kernel(*refs, fan=fan),
        grid=(4,),
        in_specs=[pl.BlockSpec(memory_space=pltpu.SMEM),
                  pl.BlockSpec((1, rows, width), lambda g: (jnp.minimum(g, 2), 0, 0)),
                  pl.BlockSpec((1, width, buckets), lambda g: (jnp.minimum(g, 1), 0, 0)),
                  pl.BlockSpec((1, STRIPES, part, width), lambda g: (jnp.minimum(g, 1), 0, 0, 0)),
                  whole((width, rows)), whole((width, buckets)), whole((16, width))],
        out_specs=[block, block],
        out_shape=[half, half],
        scratch_shapes=[pltpu.VMEM((STRIPES, 8, width), F32), pltpu.VMEM((width, buckets), F32),
                        pltpu.VMEM((3, 8, width), F32)],
        compiler_params=big(),
        cost_estimate=cost(4 << 30, 12 << 20),
        name="project_back",
    )(own, d, pos, mats, xt, tt, vg)


def token_grad_kernel(fg_ref, d_ref, w_ref, out_ref):
    width = out_ref.shape[1]

    @pl.when(pl.program_id(0) == 0)
    def _():
        out_ref[...] = fg_ref[...]

    out_ref[...] += dot(d_ref[0], w_ref.at[0].reshape(width, width)[...], NT)


def token_grads(fg, d, mats):
    rows, width = fg.shape
    full = pl.BlockSpec((rows, width), lambda g: (0, 0))
    return pl.pallas_call(
        token_grad_kernel,
        grid=(3,),
        in_specs=[full, pl.BlockSpec((1, rows, width), lambda g: (g, 0, 0)),
                  pl.BlockSpec((1,) + mats.shape[1:], lambda g: (g, 0, 0, 0))],
        out_specs=full,
        out_shape=jax.ShapeDtypeStruct((rows, width), F32),
        compiler_params=big(24),
        cost_estimate=cost(2 << 30, 10 << 20),
        name="token_grads",
    )(fg, d, mats)


def near_hop_kernel(where_ref, keep_ref, got_ref, *out_refs):
    for r, out in enumerate(out_refs):
        at = where_ref[2] ^ r
        out[0] = (keep_ref[at].astype(F32) + got_ref[at].astype(F32)).astype(BF)


def near_hop(where, keep, got):
    count, rows, width = keep.shape
    group = pl.BlockSpec((4, rows, width), lambda z: (z, 0, 0))
    return pl.pallas_call(
        near_hop_kernel,
        grid=(count // 4,),
        in_specs=[pl.BlockSpec(memory_space=pltpu.SMEM), group, group],
        out_specs=[pl.BlockSpec((1, rows, width), lambda z: (z, 0, 0))] * 4,
        out_shape=[jax.ShapeDtypeStruct((count // 4, rows, width), BF)] * 4,
        compiler_params=big(16),
        cost_estimate=cost(keep.size, 6 * keep.size),
        name="near_hop",
    )(where, keep, got)


def finish_kernel(*refs, parts, vectors):
    ins, outer_ref, mats, lines = refs[:parts], refs[parts], refs[parts + 1 : -vectors - 1], refs[-vectors - 1 : -1]
    refs[-1][...] = outer_ref[0].astype(F32)
    add = lambda rows: sum(ref[0, rows, :].astype(F32) for ref in ins)
    at = 0
    for ref in mats:
        ref[...] = add(slice(at, at + ref.shape[0]))
        at += ref.shape[0]
    tile = add(slice(at, at + 8))
    for i, ref in enumerate(lines):
        lane = 0 if i < 8 else 128
        ref[...] = tile[i % 8, lane : lane + ref.shape[0]]


def finish(parts, outer, mat_rows, sizes):
    width = parts[0].shape[2]
    return pl.pallas_call(
        lambda *refs: finish_kernel(*refs, parts=len(parts), vectors=len(sizes)),
        out_shape=[jax.ShapeDtypeStruct((rows, width), F32) for rows in mat_rows]
        + [jax.ShapeDtypeStruct((size,), F32) for size in sizes]
        + [jax.ShapeDtypeStruct(outer.shape[1:], F32)],
        compiler_params=big(16),
        name="finish",
    )(*parts, outer)


def far_hop_kernel(where_ref, *refs):
    for r, out in enumerate(refs[4:]):
        at = where_ref[3] ^ r
        out[0] = sum(ref[at].astype(F32) for ref in refs[:4]).astype(BF)


def far_hop(where, parts):
    count, rows, width = parts[0].shape
    return pl.pallas_call(
        far_hop_kernel,
        in_specs=[pl.BlockSpec(memory_space=pltpu.SMEM)] + [pl.BlockSpec(memory_space=pltpu.VMEM)] * 4,
        out_shape=[jax.ShapeDtypeStruct((1, rows, width), BF)] * 4,
        compiler_params=big(16),
        cost_estimate=cost(4 * parts[0].size, 10 * parts[0].size),
        name="far_hop",
    )(where, *parts)


def gather_rows(block):
    return lax.all_gather(block, AXES, axis=0, tiled=False)


def scatter_rows(blocks):
    return lax.psum_scatter(blocks, AXES, scatter_dimension=0, tiled=False)


def xor_permute(block, mask, count):
    return lax.ppermute(block, AXES, [(d, d ^ mask) for d in range(count)])


def in_vmem(block):
    return pltpu.with_memory_space_constraint(block, pltpu.VMEM)


class Scatter:
    def __init__(self, where, keep, send, count):
        self.where, self.keep, self.count = where, keep, count
        self.got = xor_permute(send, 1, count)

    def near(self, *after):
        got = tie(self.got, after)
        parts = near_hop(self.where, self.keep, in_vmem(got))
        self.keep, self.sent = parts[0], parts[1:]
        self.got = [xor_permute(part, 2 * r, self.count) for r, part in enumerate(self.sent, 1)]

    def far(self, *after):
        got = tie(self.got, after)
        parts = far_hop(self.where, [self.keep] + [in_vmem(part) for part in got])
        self.keep, self.sent = parts[0], parts[1:]
        self.got = [xor_permute(part, 8 * r, self.count) for r, part in enumerate(self.sent, 1)]

    def total(self):
        return sum(part[0].astype(F32) for part in [self.keep] + self.got)


def tie(value, other):
    if isinstance(other, tuple) and not other:
        return value
    return lax.optimization_barrier((value, other))[0]


def scatter_plain(keep, send, parts, count):
    blocks = jnp.stack([keep, send], axis=1).reshape((STRIPES,) + keep.shape[1:])
    sums, at = [], 0
    for part in parts:
        whole = blocks[:, at : at + part]
        rows = STRIPES * part
        flat = whole.reshape(count, rows // count, whole.shape[2])
        sums.append(lax.psum_scatter(flat.astype(F32), AXES, scatter_dimension=0, tiled=False))
        at += part
    return sums


def make_body(counts):
    count = counts[0] * counts[1]
    direct = counts == (8, 4)

    def body(
        tokens, lengths, buckets,
        query_weight, query_bias, key_weight, key_bias, value_weight, value_bias,
        output_weight, output_bias, relative_table, first_gain, first_shift,
        inner_weight, inner_bias, outer_weight, outer_bias, second_gain, second_shift,
        cotangent,
    ):
        rows, width = tokens.shape[1:]
        fan = inner_weight.shape[1] // width
        vectors = (
            query_bias, key_bias, value_bias, output_bias, first_gain, first_shift,
            outer_bias, second_gain, second_shift, inner_bias,
        )
        first_mats = (query_weight, key_weight, value_weight, relative_table)
        second_mats = [outer_weight]
        second_mats += [inner_weight[:, f * width : (f + 1) * width] for f in range(fan)]
        second_mats += [output_weight]

        def vector_rows(pieces):
            lead = pieces[0].shape[:-1]
            tile = jnp.zeros(lead + (8, width), BF)
            for i, piece in enumerate(pieces):
                lane = 0 if i < 8 else 128
                tile = tile.at[..., i % 8, lane : lane + piece.shape[-1]].set(piece)
            return tile

        me = lax.axis_index("wide") * counts[1] + lax.axis_index("narrow")
        if direct:
            first_pack, second_pack = pack(first_mats, vectors, outer_weight, inner_weight, output_weight, fan)
            second_all = gather_rows(second_pack)
            everyone = lambda block, step: jnp.concatenate(
                [block] + [xor_permute(block, step * r, count) for r in (1, 2, 3)]
            )
            near = everyone(everyone(first_pack[None], 8), 2)
            far = xor_permute(near, 1, count)
            where = jnp.stack([me, me & 1, (me >> 1) & 3, me >> 3]).astype(jnp.int32)
        else:
            whole = lambda block: lax.all_gather(block, AXES, axis=0, tiled=True)
            striped = lambda block: whole(block).reshape(STRIPES, -1, width)
            spread = [whole(v).reshape(STRIPES, -1) for v in vectors]
            first_all = jnp.concatenate(
                [striped(m) for m in first_mats] + [vector_rows(spread)], axis=1
            )
            second_all = jnp.concatenate([striped(m) for m in second_mats], axis=1)
            first_all = first_all.reshape((4, 4, 2) + first_all.shape[1:]).transpose(2, 1, 0, 3, 4)
            near, far = first_all.reshape((2, STRIPES // 2) + first_all.shape[3:])
            where = jnp.zeros((4,), jnp.int32)

        flat = tokens.reshape(rows, width)
        bucket_column = jnp.pad(buckets[::-1], (0, 1), constant_values=-1).reshape(-1, 1)
        q, k, v, kr, qr, vecs, mats, onehot, xt, tt = project_all(where, near, far, flat, bucket_column, fan)
        total = lengths[0, 0:1] + lengths[0, 1:2]
        context, probs = attend(total, q, k, v, kr, qr)
        cot = cotangent.reshape(rows, width)
        layer_out, outer_grad, inner_keep, inner_send, context_grad, fg, vg = feed(
            where, vecs, context, flat, cot, second_all, fan
        )
        outer_blocks = outer_grad.reshape(count, -1, width)
        groups = width // 128
        back = lambda dc, first, pairs, before: attend_back(
            q, k, v, kr, qr, dc, probs, onehot, first, pairs, before
        )
        if direct:
            outer_sum = scatter_rows(outer_blocks)
            inner = Scatter(where, inner_keep, inner_send, count)
            grads = back(context_grad, 0, 1, ())
            inner.near(grads[0])
            grads = back(tie(context_grad, inner.sent), 1, groups - 1, grads)
            inner.far(grads[0])
            d, pos = tie(tuple(grads), inner.sent)
        else:
            outer_out = scatter_rows(outer_blocks.astype(F32))
            grads = back(context_grad, 0, 1, ())
            d, pos = back(context_grad, 1, groups - 1, grads)
        last_keep, last_send = project_back(where, d, pos, mats, xt, tt, vg, fan)

        part = width // STRIPES
        if direct:
            last = Scatter(where, last_keep, last_send, count)
            last.near()
            tokens_grad = token_grads(fg, tie(d, last.sent), mats)
            last.far(tokens_grad)
            inner.got = tie(inner.got, tokens_grad)
            inner_sum = inner.total()
            inner_parts = [inner_sum[f * part : (f + 1) * part] for f in range(fan + 1)]
            query_out, key_out, value_out, table_out, *pieces, outer_out = finish(
                [last.keep] + [in_vmem(got) for got in last.got],
                outer_sum[None], (part, part, part, 8), [piece.shape[0] for piece in vectors],
            )
        else:
            tokens_grad = token_grads(fg, d, mats)
            inner_parts = scatter_plain(inner_keep, inner_send, (part,) * (fan + 1), count)
            query_out, key_out, value_out, table_out, _ = scatter_plain(
                last_keep, last_send, (part,) * 3 + (8, part - 8), count
            )
            blocks = jnp.stack([last_keep, last_send], axis=1).reshape(STRIPES, -1, width)
            tile = blocks[:, 3 * part + 8 : 3 * part + 16].astype(F32)
            pieces = []
            for i, piece in enumerate(vectors):
                lane = 0 if i < 8 else 128
                length = piece.shape[0] * count // STRIPES
                line = tile[:, i % 8, lane : lane + length].reshape(-1)
                pieces.append(lax.psum_scatter(line, AXES, scatter_dimension=0, tiled=True))
        inner_out = jnp.concatenate(inner_parts[:fan], axis=1)
        output_out = inner_parts[fan]
        (qb, kb, vb, ob, g1, s1, outb, g2, s2, inb) = pieces
        return (
            layer_out.reshape(tokens.shape), tokens_grad.reshape(tokens.shape),
            query_out, qb, key_out, kb, value_out, vb, output_out, ob, table_out, g1, s1,
            inner_out, inb, outer_out, outb, g2, s2,
        )

    return body


def solution(mesh):
    counts = (mesh.shape["wide"], mesh.shape["narrow"])
    rows3, rows2, rows1 = P(AXES, None, None), P(AXES, None), P(AXES)
    params = (
        rows2, rows1, rows2, rows1, rows2, rows1, rows2, rows1, rows2, rows1, rows1,
        rows2, rows1, rows2, rows1, rows1, rows1,
    )
    return jax.shard_map(
        make_body(counts),
        mesh=mesh,
        in_specs=(rows3, rows2, P()) + params + (rows3,),
        out_specs=(rows3, rows3) + params,
        check_vma=False,
    )
```

profile of v0, /device:TPU:0, one launch (start us, length us, event | category | flops | bytes accessed | tf_op | source)
XLA Modules:
  0.0 276.6 jit_solution(18363626616888145930)
XLA Ops:
  7.2 2.0 pack.1
  9.3 5.1 %collective-permute-start.2 = (bf16[1,88,768]{2,1,0:T(8,128)(2,1)}, bf16[1,88,768]{2,1,0:T(8,128)(2,1)S(1)}, u32[]{:S(2)}, u32[]{:S(2)}) collective-permute-start(bf16[1,88,768]{2,1,0:T(8,128)(2,1)} %bitcast.31), channel_id=1, source_target_pairs={{0,24},{1,25},{2,26},{3,27},{4,28},{5,29},{6,30},{7,31},{8,16},{9,... | collective-permute-start | bytes 405512 | tf_op jit(solution)/shard_map/ppermute | solution.py:704
  15.0 4.1 %collective-permute-done.2 = bf16[1,88,768]{2,1,0:T(8,128)(2,1)S(1)} collective-permute-done((bf16[1,88,768]{2,1,0:T(8,128)(2,1)}, bf16[1,88,768]{2,1,0:T(8,128)(2,1)S(1)}, u32[]{:S(2)}, u32[]{:S(2)}) %collective-permute-start.2) | collective-permute-done | bytes 135200 | tf_op jit(solution)/shard_map/ppermute | solution.py:704
  19.1 7.0 %collective-permute-done.1 = bf16[1,88,768]{2,1,0:T(8,128)(2,1)S(1)} collective-permute-done((bf16[1,88,768]{2,1,0:T(8,128)(2,1)}, bf16[1,88,768]{2,1,0:T(8,128)(2,1)S(1)}, u32[]{:S(2)}, u32[]{:S(2)}) %collective-permute-start.1) | collective-permute-done | bytes 135200 | tf_op jit(solution)/shard_map/ppermute | solution.py:704
  27.1 1.6 collective-permute-start.4
  31.7 17.3 %collective-permute-done.3 = bf16[4,88,768]{2,1,0:T(8,128)(2,1)S(1)} collective-permute-done((bf16[4,88,768]{2,1,0:T(8,128)(2,1)S(1)}, bf16[4,88,768]{2,1,0:T(8,128)(2,1)S(1)}, u32[]{:S(2)}, u32[]{:S(2)}) %collective-permute-start.3) | collective-permute-done | bytes 540704 | tf_op jit(solution)/shard_map/ppermute | solution.py:704
  49.1 13.4 %collective-permute-done.5 = bf16[4,88,768]{2,1,0:T(8,128)(2,1)S(1)} collective-permute-done((bf16[4,88,768]{2,1,0:T(8,128)(2,1)S(1)}, bf16[4,88,768]{2,1,0:T(8,128)(2,1)S(1)}, u32[]{:S(2)}, u32[]{:S(2)}) %collective-permute-start.5) | collective-permute-done | bytes 540704 | tf_op jit(solution)/shard_map/ppermute | solution.py:704
  67.0 10.2 %project.1 = (bf16[512,768]{1,0:T(8,128)(2,1)}, bf16[512,768]{1,0:T(8,128)(2,1)}, bf16[512,768]{1,0:T(8,128)(2,1)}, bf16[1024,768]{1,0:T(8,128)(2,1)}, bf16[1024...) custom-call(s32[4]{0:T(128)} %pad_add_fusion.refs_0_.where_ref, ...), custom_call_target="tpu_custom_call" | custom-call | flops 4294967296 | bytes 12582912 | tf_op jit(solution)/shard_map/project/pallas_call | solution.py:314
  77.2 23.2 %attend.1 = (bf16[512,768]{1,0:T(8,128)(2,1)}, bf16[12,512,512]{2,1,0:T(8,128)(2,1)}) custom-call(s32[1]{0:T(128)} %bitcast.7.refs_0_, bf16[512,768]{1,0:T(8,128)(2,1)} %get-tuple-element.93.refs_1_.refs_0_, bf16[512,768]{1,0:T(8,128)(2,1)} %get-tuple-element.94.refs_2_.refs_1_, bf16[512,768]{1,0:T(8,128)(2,1)} %get-tuple-element.95.refs_3_.refs_2_, ...), custom_call_target="tpu_custom_call" | custom-call | flops 26843545600 | bytes 12582912 | tf_op jit(solution)/shard_map/attend/pallas_call | solution.py:72
  100.4 8.7 %all-gather.3.cloned.1.call-done = bf16[6912,768]{1,0:T(8,128)(2,1)} async-done(((bf16[216,768]{1,0:T(8,128)(2,1)}), bf16[6912,768]{1,0:T(8,128)(2,1)}) %all-gather.3.cloned.1.call-update) | async-done | bytes 10616848 | tf_op jit(solution)/shard_map/all_gather | solution.py:696
  109.1 31.4 %feed.1 = (bf16[512,768]{1,0:T(8,128)(2,1)}, bf16[3072,768]{1,0:T(8,128)(2,1)}, bf16[16,120,768]{2,1,0:T(8,128)(2,1)}, bf16[16,120,768]{2,1,0:T(8,128)(2,1)}, bf...) custom-call(s32[4]{0:T(128)} %pad_add_fusion.refs_0_.where_ref, ...), custom_call_target="tpu_custom_call" | custom-call | tf_op jit(solution)/shard_map/feed/pallas_call | solution.py:496
  140.9 7.5 %attend_back.2 = (bf16[3,512,768]{2,1,0:T(8,128)(2,1)}, f32[2,768,256]{2,1,0:T(8,128)}) custom-call(bf16[512,768]{1,0:T(8,128)(2,1)} %get-tuple-element.93.refs_1_.refs_0_, bf16[512,768]{1,0:T(8,128)(2,1)} %get-tuple-element.94.refs_2_.refs_1_, bf16[512,768]{1,0:T(8,128)(2,1)} %get-tuple-element.95.refs_3_.refs_2_, ...), custom_call_target="tpu_custom_call" | custom-call | flops 6666666496 | bytes 3000000 | tf_op jit(solution)/shard_map/attend_back/pallas_call | solution.py:164
  148.4 4.4 %near_hop.2 = (bf16[4,120,768]{2,1,0:T(8,128)(2,1)S(1)}, bf16[4,120,768]{2,1,0:T(8,128)(2,1)}, bf16[4,120,768]{2,1,0:T(8,128)(2,1)}, bf16[4,120,768]{2,1,0:T(8,128)(2,1)}) custom-call(s32[4]{0:T(128)S(1)} %copy-done.6, bf16[16,120,768]{2,1,0:T(8,128)(2,1)S(1)} %copy-done.1, bf16[16,120,768]{2,1,0:T(8,128)(2,1)} %collective-permute-done.7.got_ref), custom_call_target="tpu_custom_call" | custom-call | flops 1474560 | bytes 8847360 | tf_op jit(solution)/shard_map/near_hop/pallas_call | solution.py:639
  156.2 27.2 %attend_back.3 = (bf16[3,512,768]{2,1,0:T(8,128)(2,1)}, f32[2,768,256]{2,1,0:T(8,128)}) custom-call(bf16[512,768]{1,0:T(8,128)(2,1)} %get-tuple-element.93.refs_1_.refs_0_, bf16[512,768]{1,0:T(8,128)(2,1)} %get-tuple-element.94.refs_2_.refs_1_, bf16[512,768]{1,0:T(8,128)(2,1)} %get-tuple-element.95.refs_3_.refs_2_, ...), custom_call_target="tpu_custom_call", output_to_operand_aliasing={{0}: (8, {}), {1}: (9, {})} | custom-call | flops 33333334016 | bytes 15000000 | tf_op jit(solution)/shard_map/attend_back/pallas_call | solution.py:164
  183.4 5.2 %collective-permute-done.10.refs_3_ = bf16[4,120,768]{2,1,0:T(8,128)(2,1)S(1)} collective-permute-done((bf16[4,120,768]{2,1,0:T(8,128)(2,1)}, bf16[4,120,768]{2,1,0:T(8,128)(2,1)S(1)}, u32[]{:S(2)}, u32[]{:S(2)}) %collective-permute-start.10) | collective-permute-done | bytes 737312 | tf_op jit(solution)/shard_map/ppermute | solution.py:704
  191.5 9.7 %project_back.1 = (bf16[16,96,768]{2,1,0:T(8,128)(2,1)}, bf16[16,96,768]{2,1,0:T(8,128)(2,1)}) custom-call(s32[4]{0:T(128)} %pad_add_fusion.refs_0_.where_ref, bf16[3,512,768]{2,1,0:T(8,128)(2,1)} %get-tuple-element.134.refs_1_.d_ref, f32[2,768,256]{2,1,0:T(8,128)} %get-tuple-element.124.refs_2_, bf16[3,32,24,768]{3,2,1,0:T(8,128)(2,1)} %get-tuple-element.125.refs_3_.w_ref, ...), custom_call_target="tpu_custom_call" | custom-call | flops 4294967296 | bytes 12582912 | tf_op jit(solution)/shard_map/project_back/pallas_call | solution.py:586
  203.6 2.1 collective-permute-start.20
  206.0 1.7 copy-done.2
  208.8 1.6 collective-permute-start.12
  210.9 4.5 %collective-permute-done.18 = bf16[1,120,768]{2,1,0:T(8,128)(2,1)S(1)} collective-permute-done((bf16[1,120,768]{2,1,0:T(8,128)(2,1)}, bf16[1,120,768]{2,1,0:T(8,128)(2,1)S(1)}, u32[]{:S(2)}, u32[]{:S(2)}) %collective-permute-start.18) | collective-permute-done | bytes 184352 | tf_op jit(solution)/shard_map/ppermute | solution.py:704
  216.9 3.8 %token_grads.1 = f32[512,768]{1,0:T(8,128)} custom-call(f32[512,768]{1,0:T(8,128)S(1)} %copy-done.4, bf16[3,512,768]{2,1,0:T(8,128)(2,1)S(1)} %copy-done.3, bf16[3,32,24,768]{3,2,1,0:T(8,128)(2,1)S(1)} %copy-done), custom_call_target="tpu_custom_call" | custom-call | flops 2147483648 | bytes 10485760 | tf_op jit(solution)/shard_map/token_grads/pallas_call | solution.py:617
  221.8 19.1 %collective-permute-done.12.refs_1_ = bf16[4,96,768]{2,1,0:T(8,128)(2,1)S(1)} collective-permute-done((bf16[4,96,768]{2,1,0:T(8,128)(2,1)S(1)}, bf16[4,96,768]{2,1,0:T(8,128)(2,1)S(1)}, u32[]{:S(2)}, u32[]{:S(2)}) %collective-permute-start.12) | collective-permute-done | bytes 589856 | tf_op jit(solution)/shard_map/ppermute | solution.py:704
  243.5 2.7 collective-permute-start.17
  246.9 21.1 %reduce-scatter.2.cloned.1.call-done.refs_4_ = bf16[1,96,768]{2,1,0:T(8,128)(2,1)} async-done(((bf16[32,96,768]{2,1,0:T(8,128)(2,1)}), bf16[1,96,768]{2,1,0:T(8,128)(2,1)}) %reduce-scatter.2.cloned.1.call-update) | async-done | bytes 147472 | tf_op jit(solution)/shard_map/reduce_scatter | solution.py:700
  (82 shorter events, 26.8 us)
Async XLA Ops:
  7.2 101.9 %all-gather.3.cloned.1.call-start = ((), (), s32[]{:S(2)}) async-start(), calls=%async_computation.2 | async-start | bytes 10948608 | tf_op jit(solution)/shard_map/all_gather | solution.py:696
  9.2 258.8 %reduce-scatter.2.cloned.1.call-start = ((), (), s32[]{:S(2)}) async-start(), calls=%async_computation.1 | async-start | bytes 4866048 | tf_op jit(solution)/shard_map/reduce_scatter | solution.py:700
  9.3 9.8 %collective-permute-start.2 = (bf16[1,88,768]{2,1,0:T(8,128)(2,1)}, bf16[1,88,768]{2,1,0:T(8,128)(2,1)S(1)}, u32[]{:S(2)}, u32[]{:S(2)}) collective-permute-start(bf16[1,88,768]{2,1,0:T(8,128)(2,1)} %bitcast.31), channel_id=1, source_target_pairs={{0,24},{1,25},{2,26},{3,27},{4,28},{5,29},{6,30},{7,31},{8,16},{9,... | collective-permute-start | bytes 405512 | tf_op jit(solution)/shard_map/ppermute | solution.py:704
  14.4 11.7 %collective-permute-start.1 = (bf16[1,88,768]{2,1,0:T(8,128)(2,1)}, bf16[1,88,768]{2,1,0:T(8,128)(2,1)S(1)}, u32[]{:S(2)}, u32[]{:S(2)}) collective-permute-start(bf16[1,88,768]{2,1,0:T(8,128)(2,1)} %bitcast.32), channel_id=1, source_target_pairs={{0,16},{1,17},{2,18},{3,19},{4,20},{5,21},{6,22},{7,23},{8,24},{9,... | collective-permute-start | bytes 405512 | tf_op jit(solution)/shard_map/ppermute | solution.py:704
  14.4 11.7 %collective-permute-start = (bf16[1,88,768]{2,1,0:T(8,128)(2,1)}, bf16[1,88,768]{2,1,0:T(8,128)(2,1)S(1)}, u32[]{:S(2)}, u32[]{:S(2)}) collective-permute-start(bf16[1,88,768]{2,1,0:T(8,128)(2,1)} %bitcast.33), channel_id=1, source_target_pairs={{0,8},{1,9},{2,10},{3,11},{4,12},{5,13},{6,14},{7,15},{8,0},{9,1},... | collective-permute-start | bytes 405512 | tf_op jit(solution)/shard_map/ppermute | solution.py:704
  27.1 35.5 %copy-start.12 = (s32[1023]{0:T(1024)S(1)}, s32[1023]{0:T(1024)}, u32[]{:S(2)}) copy-start(s32[1023]{0:T(1024)} %param.23) | copy-start | bytes 12280
  27.1 22.0 %collective-permute-start.4 = (bf16[4,88,768]{2,1,0:T(8,128)(2,1)S(1)}, bf16[4,88,768]{2,1,0:T(8,128)(2,1)S(1)}, u32[]{:S(2)}, u32[]{:S(2)}) collective-permute-start(bf16[4,88,768]{2,1,0:T(8,128)(2,1)S(1)} %pad_maximum_fusion), channel_id=1, source_target_pairs={{0,4},{1,5},{2,6},{3,7},{4,0},{5,1},{6,2},{7,3},{8,12},{9,13},{10,... | collective-permute-start | bytes 1622024 | tf_op jit(solution)/shard_map/ppermute | solution.py:704
  28.7 20.4 %collective-permute-start.3 = (bf16[4,88,768]{2,1,0:T(8,128)(2,1)S(1)}, bf16[4,88,768]{2,1,0:T(8,128)(2,1)S(1)}, u32[]{:S(2)}, u32[]{:S(2)}) collective-permute-start(bf16[4,88,768]{2,1,0:T(8,128)(2,1)S(1)} %pad_maximum_fusion), channel_id=1, source_target_pairs={{0,2},{1,3},{2,0},{3,1},{4,6},{5,7},{6,4},{7,5},{8,10},{9,11},{10,... | collective-permute-start | bytes 1622024 | tf_op jit(solution)/shard_map/ppermute | solution.py:704
  31.1 31.4 %collective-permute-start.5 = (bf16[4,88,768]{2,1,0:T(8,128)(2,1)S(1)}, bf16[4,88,768]{2,1,0:T(8,128)(2,1)S(1)}, u32[]{:S(2)}, u32[]{:S(2)}) collective-permute-start(bf16[4,88,768]{2,1,0:T(8,128)(2,1)S(1)} %pad_maximum_fusion), channel_id=1, source_target_pairs={{0,6},{1,7},{2,4},{3,5},{4,2},{5,3},{6,0},{7,1},{8,14},{9,15},{10,... | collective-permute-start | bytes 1622024 | tf_op jit(solution)/shard_map/ppermute | solution.py:704
  62.5 4.5 %collective-permute-start.6 = (bf16[16,88,768]{2,1,0:T(8,128)(2,1)S(1)}, bf16[16,88,768]{2,1,0:T(8,128)(2,1)}, u32[]{:S(2)}, u32[]{:S(2)}) collective-permute-start(bf16[16,88,768]{2,1,0:T(8,128)(2,1)S(1)} %constant_dynamic-update-slice_fusion.refs_1_.refs_3_.refs_5_.refs_7_.refs_9_), channel_id=1, source_target_pairs={{0,1},{1,0},{2,3},{3,2},{4,5},{5,4},{6,7},{7,6},{8,9},{9,8},{10,11... | collective-permute-start | bytes 6488072 | tf_op jit(solution)/shard_map/ppermute | solution.py:704
  140.5 7.9 %collective-permute-start.7 = (bf16[16,120,768]{2,1,0:T(8,128)(2,1)}, bf16[16,120,768]{2,1,0:T(8,128)(2,1)}, u32[]{:S(2)}, u32[]{:S(2)}) collective-permute-start(bf16[16,120,768]{2,1,0:T(8,128)(2,1)} %get-tuple-element.104), channel_id=1, source_target_pairs={{0,1},{1,0},{2,3},{3,2},{4,5},{5,4},{6,7},{7,6},{8,9},{9,8},{10,11... | collective-permute-start | bytes 8847368 | tf_op jit(solution)/shard_map/ppermute | solution.py:704
  152.8 30.7 %collective-permute-start.8 = (bf16[4,120,768]{2,1,0:T(8,128)(2,1)}, bf16[4,120,768]{2,1,0:T(8,128)(2,1)S(1)}, u32[]{:S(2)}, u32[]{:S(2)}) collective-permute-start(bf16[4,120,768]{2,1,0:T(8,128)(2,1)} %get-tuple-element.109), channel_id=1, source_target_pairs={{0,2},{1,3},{2,0},{3,1},{4,6},{5,7},{6,4},{7,5},{8,10},{9,11},{10,... | collective-permute-start | bytes 2211848 | tf_op jit(solution)/shard_map/ppermute | solution.py:704
  154.3 29.2 %collective-permute-start.9 = (bf16[4,120,768]{2,1,0:T(8,128)(2,1)}, bf16[4,120,768]{2,1,0:T(8,128)(2,1)S(1)}, u32[]{:S(2)}, u32[]{:S(2)}) collective-permute-start(bf16[4,120,768]{2,1,0:T(8,128)(2,1)} %get-tuple-element.110), channel_id=1, source_target_pairs={{0,4},{1,5},{2,6},{3,7},{4,0},{5,1},{6,2},{7,3},{8,12},{9,13},{10,... | collective-permute-start | bytes 2211848 | tf_op jit(solution)/shard_map/ppermute | solution.py:704
  154.8 33.8 %collective-permute-start.10 = (bf16[4,120,768]{2,1,0:T(8,128)(2,1)}, bf16[4,120,768]{2,1,0:T(8,128)(2,1)S(1)}, u32[]{:S(2)}, u32[]{:S(2)}) collective-permute-start(bf16[4,120,768]{2,1,0:T(8,128)(2,1)} %get-tuple-element.111), channel_id=1, source_target_pairs={{0,6},{1,7},{2,4},{3,5},{4,2},{5,3},{6,0},{7,1},{8,14},{9,15},{10,... | collective-permute-start | bytes 2211848 | tf_op jit(solution)/shard_map/ppermute | solution.py:704
  201.2 4.7 %collective-permute-start.11 = (bf16[16,96,768]{2,1,0:T(8,128)(2,1)}, bf16[16,96,768]{2,1,0:T(8,128)(2,1)S(1)}, u32[]{:S(2)}, u32[]{:S(2)}) collective-permute-start(bf16[16,96,768]{2,1,0:T(8,128)(2,1)} %get-tuple-element.130), channel_id=1, source_target_pairs={{0,1},{1,0},{2,3},{3,2},{4,5},{5,4},{6,7},{7,6},{8,9},{9,8},{10,11... | collective-permute-start | bytes 7077896 | tf_op jit(solution)/shard_map/ppermute | solution.py:704
  201.2 14.2 %collective-permute-start.18 = (bf16[1,120,768]{2,1,0:T(8,128)(2,1)}, bf16[1,120,768]{2,1,0:T(8,128)(2,1)S(1)}, u32[]{:S(2)}, u32[]{:S(2)}) collective-permute-start(bf16[1,120,768]{2,1,0:T(8,128)(2,1)} %copy-done.10), channel_id=1, source_target_pairs={{0,8},{1,9},{2,10},{3,11},{4,12},{5,13},{6,14},{7,15},{8,0},{9,1},... | collective-permute-start | bytes 552968 | tf_op jit(solution)/shard_map/ppermute | solution.py:704
  202.6 18.1 %collective-permute-start.19 = (bf16[1,120,768]{2,1,0:T(8,128)(2,1)}, bf16[1,120,768]{2,1,0:T(8,128)(2,1)S(1)}, u32[]{:S(2)}, u32[]{:S(2)}) collective-permute-start(bf16[1,120,768]{2,1,0:T(8,128)(2,1)} %copy-done.9), channel_id=1, source_target_pairs={{0,16},{1,17},{2,18},{3,19},{4,20},{5,21},{6,22},{7,23},{8,24},{9,... | collective-permute-start | bytes 552968 | tf_op jit(solution)/shard_map/ppermute | solution.py:704
  203.6 17.5 %collective-permute-start.20 = (bf16[1,120,768]{2,1,0:T(8,128)(2,1)}, bf16[1,120,768]{2,1,0:T(8,128)(2,1)S(1)}, u32[]{:S(2)}, u32[]{:S(2)}) collective-permute-start(bf16[1,120,768]{2,1,0:T(8,128)(2,1)} %copy-done.8), channel_id=1, source_target_pairs={{0,24},{1,25},{2,26},{3,27},{4,28},{5,29},{6,30},{7,31},{8,16},{9,... | collective-permute-start | bytes 552968 | tf_op jit(solution)/shard_map/ppermute | solution.py:704
  208.8 32.1 %collective-permute-start.12 = (bf16[4,96,768]{2,1,0:T(8,128)(2,1)S(1)}, bf16[4,96,768]{2,1,0:T(8,128)(2,1)S(1)}, u32[]{:S(2)}, u32[]{:S(2)}) collective-permute-start(bf16[4,96,768]{2,1,0:T(8,128)(2,1)S(1)} %get-tuple-element.131), channel_id=1, source_target_pairs={{0,2},{1,3},{2,0},{3,1},{4,6},{5,7},{6,4},{7,5},{8,10},{9,11},{10,... | collective-permute-start | bytes 1769480 | tf_op jit(solution)/shard_map/ppermute | solution.py:704
  210.4 30.5 %collective-permute-start.13 = (bf16[4,96,768]{2,1,0:T(8,128)(2,1)S(1)}, bf16[4,96,768]{2,1,0:T(8,128)(2,1)S(1)}, u32[]{:S(2)}, u32[]{:S(2)}) collective-permute-start(bf16[4,96,768]{2,1,0:T(8,128)(2,1)S(1)} %get-tuple-element.132), channel_id=1, source_target_pairs={{0,4},{1,5},{2,6},{3,7},{4,0},{5,1},{6,2},{7,3},{8,12},{9,13},{10,... | collective-permute-start | bytes 1769480 | tf_op jit(solution)/shard_map/ppermute | solution.py:704
  215.4 25.5 %collective-permute-start.14 = (bf16[4,96,768]{2,1,0:T(8,128)(2,1)S(1)}, bf16[4,96,768]{2,1,0:T(8,128)(2,1)S(1)}, u32[]{:S(2)}, u32[]{:S(2)}) collective-permute-start(bf16[4,96,768]{2,1,0:T(8,128)(2,1)S(1)} %get-tuple-element.133), channel_id=1, source_target_pairs={{0,6},{1,7},{2,4},{3,5},{4,2},{5,3},{6,0},{7,1},{8,14},{9,15},{10,... | collective-permute-start | bytes 1769480 | tf_op jit(solution)/shard_map/ppermute | solution.py:704
  241.8 26.2 %collective-permute-start.15 = (bf16[1,96,768]{2,1,0:T(8,128)(2,1)S(1)}, bf16[1,96,768]{2,1,0:T(8,128)(2,1)S(1)}, u32[]{:S(2)}, u32[]{:S(2)}) collective-permute-start(bf16[1,96,768]{2,1,0:T(8,128)(2,1)S(1)} %get-tuple-element.140), channel_id=1, source_target_pairs={{0,8},{1,9},{2,10},{3,11},{4,12},{5,13},{6,14},{7,15},{8,0},{9,1},... | collective-permute-start | bytes 442376 | tf_op jit(solution)/shard_map/ppermute | solution.py:704
  242.9 25.1 %collective-permute-start.16 = (bf16[1,96,768]{2,1,0:T(8,128)(2,1)S(1)}, bf16[1,96,768]{2,1,0:T(8,128)(2,1)S(1)}, u32[]{:S(2)}, u32[]{:S(2)}) collective-permute-start(bf16[1,96,768]{2,1,0:T(8,128)(2,1)S(1)} %get-tuple-element.141), channel_id=1, source_target_pairs={{0,16},{1,17},{2,18},{3,19},{4,20},{5,21},{6,22},{7,23},{8,24},{9,... | collective-permute-start | bytes 442376 | tf_op jit(solution)/shard_map/ppermute | solution.py:704
  243.5 24.5 %collective-permute-start.17 = (bf16[1,96,768]{2,1,0:T(8,128)(2,1)S(1)}, bf16[1,96,768]{2,1,0:T(8,128)(2,1)S(1)}, u32[]{:S(2)}, u32[]{:S(2)}) collective-permute-start(bf16[1,96,768]{2,1,0:T(8,128)(2,1)S(1)} %get-tuple-element.142), channel_id=1, source_target_pairs={{0,24},{1,25},{2,26},{3,27},{4,28},{5,29},{6,30},{7,31},{8,16},{9,... | collective-permute-start | bytes 442376 | tf_op jit(solution)/shard_map/ppermute | solution.py:704
  (13 other events, 130.9 us)
Sparse Core Ops, SparseCore 0:
  10.9 98.0 all-gather.2
  140.9 127.0 reduce-scatter.1
where the time goes:
time: 277 us
  Pallas kernels  123 us (44%)
  waiting for transfers between devices  102 us (37%)
  starting transfers between devices  25.8 us (9%)
  between operations  15.6 us (6%)
  local copies, waits for them, and re-layouts  8.33 us (3%)
    ppermute x21, waiting for transfers between devices, xor_permute(): return lax.ppermute(block, AXES, [(d, d ^ mask) for d in range(count)])  71.7 us
    pallas_call x2, Pallas kernels, attend_back(): pl.pallas_call(lambda *refs: attend_back_kernel(*refs, rows=rows, tile=ro...  34.7 us
    pallas_call x1, Pallas kernels, feed(): pl.pallas_call(lambda *refs: feed_kernel(*refs, fan=fan), in_specs=[pl.Bl...  31.4 us
    ppermute x21, starting transfers between devices, xor_permute(): return lax.ppermute(block, AXES, [(d, d ^ mask) for d in range(count)])  25.7 us
    pallas_call x1, Pallas kernels, attend(): pl.pallas_call(lambda *refs: attend_kernel(*refs, rows=rows, tile=rows //...  23.2 us
    reduce_scatter x1, waiting for transfers between devices, scatter_rows(): return lax.psum_scatter(blocks, AXES, scatter_dimension=0, tiled=False)  21.1 us
    pallas_call x1, Pallas kernels, project_all(): pl.pallas_call(lambda *refs: project_kernel(*refs, fan=fan), grid=(width...  10.2 us
    pallas_call x1, Pallas kernels, project_back(): pl.pallas_call(lambda *refs: project_back_kernel(*refs, fan=fan), grid=(4...  9.66 us
  transfers between devices with their start and end apart: 23, of which 12 were waited for; matrix products, arithmetic and copies ran while one was open for 2% of the time, Pallas kernels for 32%

commit v1 on v0

--- a/solution.py
+++ b/solution.py
@@ -151,8 +151,8 @@
         )
         dk_ref[sl, :] = dot(flip, dk.astype(BF), NN).astype(BF)
         dqr_ref[:, low:high] += dot(turned(dot(flip, k_ref[sl, :], NN)), above(da, db), NN)
-    pos_ref[0] = dot(dqr_ref[...].astype(BF), onehot_ref[...], NN)
-    pos_ref[1] = dot(dkr_ref[...].astype(BF), onehot_ref[...], NN)
+    pos_ref[0] = dot(dqr_ref[...].astype(BF), onehot_ref[...], NN).astype(BF)
+    pos_ref[1] = dot(dkr_ref[...].astype(BF), onehot_ref[...], NN).astype(BF)
 
 
 def attend_back(q, k, v, kr, qr, dc, probs, onehot, first, groups, before):
@@ -175,10 +175,10 @@
         ],
         out_shape=[
             jax.ShapeDtypeStruct((3, rows, width), BF),
-            jax.ShapeDtypeStruct((2, width, buckets), F32),
+            jax.ShapeDtypeStruct((2, width, buckets), BF),
         ],
         scratch_shapes=[pltpu.VMEM((2, rows, rows), BF)] + [pltpu.VMEM((128, 2 * rows), F32)] * 2,
-        compiler_params=pltpu.CompilerParams(vmem_limit_bytes=60 << 20),
+        compiler_params=pltpu.CompilerParams(vmem_limit_bytes=54 << 20),
         input_output_aliases={8 + i: i for i in range(len(before))},
         cost_estimate=pl.CostEstimate(
             flops=int(40e9 * share), bytes_accessed=int(18e6 * share), transcendentals=0
@@ -361,13 +361,12 @@
         send_ref[...] = even
 
 
-def feed_kernel(where_ref, vecs_ref, ctx_hbm, x_hbm, cot_hbm, packed_hbm,
-                out_hbm, outer_hbm, keep_hbm, send_hbm, cg_hbm, fg_hbm, vg_ref,
-                ctx, x, cot, wo, wi, w2, act, slope, low, turned, og, n1, inv, acc, first,
-                stage, keep, send, fetch, chunk_fetch, flush, outer_flush, keep_flush, *, fan):
+def feed_forward_kernel(vecs_ref, ctx_hbm, x_hbm, cot_hbm, packed_hbm,
+                        out_hbm, outer_hbm, slope_hbm, og_hbm, low_hbm, n1_hbm, inv_hbm, second_hbm, vg_ref,
+                        ctx, x, cot, wo, wi, w2, act, slope, low, og, n1, inv, acc, out, stage,
+                        fetch, chunk_fetch, flush, slope_flush, outer_flush, *, fan):
     rows, width = ctx.shape
     part = width // STRIPES
-    own = where_ref[1]
     vec = lambda i: vecs_ref[i : i + 1, :]
     column = lambda a: jnp.sum(a, axis=0, keepdims=True)
     copy = pltpu.make_async_copy
@@ -387,6 +386,8 @@
         for one in chunk_copies(f):
             one.start()
     ins[3].start()
+    outs = [copy(n1, n1_hbm, flush.at[0]), copy(inv, inv_hbm, flush.at[1]), copy(low, low_hbm, flush.at[2]),
+            copy(out, out_hbm, flush.at[3]), copy(acc, second_hbm, flush.at[4]), copy(og, og_hbm, flush.at[5])]
     vg_ref[...] = jnp.zeros_like(vg_ref)
     ins[0].wait()
     ins[1].wait()
@@ -398,6 +399,11 @@
     start = normed * vec(4) + vec(5)
     low[...] = start.astype(BF)
     acc[...] = start + vec(6)
+    for one in outs[:3]:
+        one.start()
+
+    def slope_copy(f):
+        return copy(slope.at[f], slope_hbm.at[f], slope_flush.at[f])
 
     def forward(f, carry):
         for one in chunk_copies(f):
@@ -407,22 +413,23 @@
         active = (pre * half).astype(BF)
         act[f] = active
         slope[f] = (half + pre * (jnp.exp(-0.5 * pre * pre) * 0.3989422804014327)).astype(BF)
+        slope_copy(f).start()
         acc[...] += dot(active, w2.at[f].reshape(width, width)[...], NN)
         return carry
 
     lax.fori_loop(0, fan, forward, 0)
-    turned[...] = low[...].T
     normed, inverse = normal_parts(acc[...])
-    low[...] = (normed * vec(7) + vec(8)).astype(BF)
-    outs = [copy(low, out_hbm, flush.at[0]), copy(cot, cg_hbm, flush.at[1]), copy(first, fg_hbm, flush.at[2])]
-    outs[0].start()
+    out[...] = (normed * vec(7) + vec(8)).astype(BF)
+    outs[3].start()
     ins[3].wait()
     upstream = cot[...].astype(F32)
     vg_ref[8:9, :] = column(upstream * normed)
     vg_ref[9:10, :] = column(upstream)
     second = normal_back(upstream, normed, inverse, vec(7))
     acc[...] = second
+    outs[4].start()
     og[...] = second.astype(BF)
+    outs[5].start()
     vg_ref[10:11, :] = column(og[...].astype(F32))
 
     def outer_copy(f):
@@ -439,6 +446,72 @@
         return carry
 
     lax.fori_loop(0, fan, outer_grad, 0)
+    for one in outs:
+        one.wait()
+    for f in range(fan):
+        slope_copy(f).wait()
+    for f in (fan - 2, fan - 1):
+        outer_copy(f).wait()
+
+
+def feed_forward(vecs, ctx, x, cot, packed, fan):
+    rows, width = x.shape
+    part = width // STRIPES
+    shape = jax.ShapeDtypeStruct
+    hbm = pl.BlockSpec(memory_space=pl.ANY)
+    vmem = pl.BlockSpec(memory_space=pltpu.VMEM)
+    low, high = pltpu.VMEM((rows, width), BF), pltpu.VMEM((rows, width), F32)
+    sem = pltpu.SemaphoreType.DMA
+    return pl.pallas_call(
+        lambda *refs: feed_forward_kernel(*refs, fan=fan),
+        in_specs=[vmem] + [hbm] * 4,
+        out_specs=[hbm] * 8 + [vmem],
+        out_shape=[shape((rows, width), BF), shape((fan * width, width), BF), shape((fan, rows, width), BF),
+                   shape((rows, width), BF), shape((rows, width), BF), shape((rows, width), F32),
+                   shape((rows, 128), F32), shape((rows, width), F32), shape((16, width), F32)],
+        scratch_shapes=[low, low, low, pltpu.VMEM((STRIPES, part, width), BF),
+                        pltpu.VMEM((fan, STRIPES, part, width), BF),
+                        pltpu.VMEM((fan, STRIPES // fan, part * fan, width), BF),
+                        pltpu.VMEM((fan, rows, width), BF), pltpu.VMEM((fan, rows, width), BF), low, low,
+                        high, pltpu.VMEM((rows, 128), F32), high, low, pltpu.VMEM((2, width, width), BF),
+                        sem((4,)), sem((2, fan)), sem((6,)), sem((fan,)), sem((2,))],
+        compiler_params=big(),
+        name="feed_forward",
+    )(vecs, ctx, x, cot, packed)
+
+
+def feed_back_kernel(where_ref, vecs_ref, vg_in_ref, og_hbm, low_hbm, slope_hbm, second_hbm, n1_hbm, inv_hbm,
+                     ctx_hbm, packed_hbm, keep_hbm, send_hbm, cg_hbm, fg_hbm, vg_ref,
+                     og, low, slope, acc, n1, inv, ctx, wo, wi, w2, turned, cg, fg, keep, send,
+                     fetch, chunk_fetch, flush, keep_flush, *, fan):
+    rows, width = ctx.shape
+    part = width // STRIPES
+    own = where_ref[1]
+    column = lambda a: jnp.sum(a, axis=0, keepdims=True)
+    copy = pltpu.make_async_copy
+
+    def chunk_copies(f):
+        inner = pl.ds(pl.multiple_of((fan + f) * part, 8), part)
+        outer = pl.ds(f * (STRIPES // fan), STRIPES // fan)
+        return (copy(packed_hbm.at[outer, pl.ds(0, fan * part), :], w2.at[f], chunk_fetch.at[0, f]),
+                copy(slope_hbm.at[f], slope.at[f], chunk_fetch.at[1, f]),
+                copy(packed_hbm.at[:, inner, :], wi.at[f], chunk_fetch.at[2, f]))
+
+    ins = [copy(og_hbm, og, fetch.at[0]), copy(low_hbm, low, fetch.at[1]), copy(second_hbm, acc, fetch.at[2]),
+           copy(ctx_hbm, ctx, fetch.at[3]), copy(n1_hbm, n1, fetch.at[4]), copy(inv_hbm, inv, fetch.at[5]),
+           copy(packed_hbm.at[:, pl.ds(2 * fan * part, part), :], wo, fetch.at[6])]
+    for one in [ins[0], *chunk_copies(0), ins[1], ins[2]]:
+        one.start()
+    for f in range(1, fan):
+        for one in chunk_copies(f):
+            one.start()
+    for one in ins[3:]:
+        one.start()
+    vg_ref[...] = vg_in_ref[...]
+    ins[1].wait()
+    turned[...] = low[...].T
+    ins[0].wait()
+    ins[2].wait()
 
     def keep_copies(f):
         place = pl.ds(pl.multiple_of(f * part, 8), part)
@@ -456,6 +529,8 @@
             one.start()
 
     def backward(f, carry):
+        for one in chunk_copies(f):
+            one.wait()
         grad = dot(og[...], w2.at[f].reshape(width, width)[...], NT) * slope[f].astype(F32)
         ig = grad.astype(BF)
         acc[...] += dot(ig, wi.at[f].reshape(width, width)[...], NT)
@@ -464,141 +539,148 @@
         return carry
 
     lax.fori_loop(0, fan, backward, 0)
-    total = acc[...]
-    normed = n1[...]
+    for one in ins[3:]:
+        one.wait()
+    total, normed = acc[...], n1[...]
+    grad = normal_back(total, normed, inv[:, 0:1], vecs_ref[4:5, :])
+    ag = grad.astype(BF)
+    leave(fan, dot(ctx[...], ag, TN))
+    cg[...] = dot(ag, wo.reshape(width, width)[...], NT).astype(BF)
+    fg[...] = grad
+    outs = [copy(cg, cg_hbm, flush.at[0]), copy(fg, fg_hbm, flush.at[1])]
+    for one in outs:
+        one.start()
     vg_ref[4:5, :] = column(total * normed)
     vg_ref[5:6, :] = column(total)
-    grad = normal_back(total, normed, inv[:, 0:1], vec(4))
-    first[...] = grad
-    outs[2].start()
-    ag = grad.astype(BF)
     vg_ref[6:7, :] = column(ag.astype(F32))
-    leave(fan, dot(ctx[...], ag, TN))
-    cot[...] = dot(ag, wo.reshape(width, width)[...], NT).astype(BF)
-    outs[1].start()
     for one in outs:
         one.wait()
-    for f in (fan - 2, fan - 1):
-        outer_copy(f).wait()
     for f in (fan - 1, fan):
         for one in keep_copies(f):
             one.wait()
 
 
-def feed(where, vecs, ctx, x, cot, packed, fan):
-    rows, width = x.shape
+def feed_back(where, vecs, vg, og, low, slope, second, n1, inv, ctx, packed, fan):
+    rows, width = ctx.shape
     part = width // STRIPES
     shape = jax.ShapeDtypeStruct
     hbm = pl.BlockSpec(memory_space=pl.ANY)
+    vmem = pl.BlockSpec(memory_space=pltpu.VMEM)
     half = shape((STRIPES // 2, part * (fan + 1), width), BF)
-    low, high = pltpu.VMEM((rows, width), BF), pltpu.VMEM((rows, width), F32)
+    thin, wide = pltpu.VMEM((rows, width), BF), pltpu.VMEM((rows, width), F32)
     sem = pltpu.SemaphoreType.DMA
     return pl.pallas_call(
-        lambda *refs: feed_kernel(*refs, fan=fan),
-        in_specs=[pl.BlockSpec(memory_space=pltpu.SMEM), pl.BlockSpec(memory_space=pltpu.VMEM)] + [hbm] * 4,
-        out_specs=[hbm] * 6 + [pl.BlockSpec(memory_space=pltpu.VMEM)],
-        out_shape=[shape((rows, width), BF), shape((fan * width, width), BF), half, half,
-                   shape((rows, width), BF), shape((rows, width), F32), shape((16, width), F32)],
-        scratch_shapes=[low, low, low, pltpu.VMEM((STRIPES, part, width), BF),
+        lambda *refs: feed_back_kernel(*refs, fan=fan),
+        in_specs=[pl.BlockSpec(memory_space=pltpu.SMEM), vmem, vmem] + [hbm] * 8,
+        out_specs=[hbm] * 4 + [vmem],
+        out_shape=[half, half, shape((rows, width), BF), shape((rows, width), F32), shape(vg.shape, F32)],
+        scratch_shapes=[thin, thin, pltpu.VMEM((fan, rows, width), BF), wide, wide,
+                        pltpu.VMEM((rows, 128), F32), thin, pltpu.VMEM((STRIPES, part, width), BF),
                         pltpu.VMEM((fan, STRIPES, part, width), BF),
                         pltpu.VMEM((fan, STRIPES // fan, part * fan, width), BF),
-                        pltpu.VMEM((fan, rows, width), BF), pltpu.VMEM((fan, rows, width), BF), low,
-                        pltpu.VMEM((width, rows), BF), low, high, pltpu.VMEM((rows, 128), F32), high, high,
-                        pltpu.VMEM((2, width, width), BF)]
+                        pltpu.VMEM((width, rows), BF), thin, wide]
         + [pltpu.VMEM((2, STRIPES // 2, part, width), BF)] * 2
-        + [sem((4,)), sem((2, fan)), sem((3,)), sem((2,)), sem((2, 2))],
+        + [sem((7,)), sem((3, fan)), sem((2,)), sem((2, 2))],
         compiler_params=big(),
-        name="feed",
-    )(where, vecs, ctx, x, cot, packed)
-
-
-def project_back_kernel(own_ref, d_ref, pos_ref, w_ref, xt_ref, tt_ref, vg2_ref,
-                        keep_ref, send_ref, vec_ref, tab_ref, bias_ref, *, fan):
-    step = pl.program_id(0)
-    width, rows = xt_ref.shape
-    buckets = tt_ref.shape[1]
+        name="feed_back",
+    )(where, vecs, vg, og, low, slope, second, n1, inv, ctx, packed)
+
+
+def cut(row, mine, marks):
+    return dot(jnp.where(mine, jnp.broadcast_to(row, mine.shape), 0.0).astype(BF), marks, NT)
+
+
+def cut_vectors_kernel(vg_ref, vec_ref, *, fan):
+    width = vg_ref.shape[1]
+    vec_ref[...] = jnp.zeros_like(vec_ref)
+    whole = stripe_marks(width, BF)
+    for i, at in enumerate((6, 4, 5, 10, 8, 9), 3):
+        lanes = slice(0, 128) if i < 8 else slice(128, 256)
+        vec_ref[:, i % 8, lanes] = cut(vg_ref[at : at + 1, :], *whole)
+    broad = width * fan // STRIPES
+    total = jnp.zeros((STRIPES, 128), F32)
+    for f in range(fan):
+        column_at = lax.broadcasted_iota(jnp.int32, (STRIPES, width), 1) + f * width
+        stripe = lax.broadcasted_iota(jnp.int32, (STRIPES, width), 0)
+        mine = (column_at >= stripe * broad) & (column_at < stripe * broad + broad)
+        place = lax.broadcasted_iota(jnp.int32, (128, width), 0)
+        marks = lax.broadcasted_iota(jnp.int32, (128, width), 1) + f * width
+        total += cut(vg_ref[f : f + 1, :], mine, (marks % broad == place).astype(BF))
+    vec_ref[:, (VECTORS - 1) % 8, 128:256] = total
+
+
+def cut_vectors(vg, fan):
+    return pl.pallas_call(
+        lambda *refs: cut_vectors_kernel(*refs, fan=fan),
+        out_shape=jax.ShapeDtypeStruct((STRIPES, 8, vg.shape[1]), F32),
+        compiler_params=big(24),
+        cost_estimate=pl.CostEstimate(flops=100000000000, bytes_accessed=1000000, transcendentals=0),
+        name="cut_vectors",
+    )(vg)
+
+
+def project_back_kernel(where_ref, vec_in_ref, w, xt, tt, d_hbm, pos_hbm, *refs, fan, hops):
+    keep_ref, send_ref = refs[hops : hops + 2]
+    d, pos, vec_ref, chunk_fetch = refs[-4:]
+    width, rows = xt.shape
+    buckets = tt.shape[1]
     part = width // STRIPES
-    own = own_ref[1]
-
-    @pl.when(step == 0)
-    def _():
-        tab_ref[...] = jnp.zeros_like(tab_ref)
-
-    @pl.when(step < 3)
-    def _():
-        d = d_ref[0]
-        ones = jnp.ones((8, rows), BF)
-        bias_ref[step] = dot(ones, d, NN)
-
-        @pl.when(step < 2)
-        def _():
-            pos = pos_ref[0].astype(BF)
-            tab_ref[...] += dot(w_ref.at[0].reshape(width, width)[...], pos, NN)
-            bias_ref[step] += dot(jnp.ones((8, buckets), BF), pos, NT)
-            grad = dot(xt_ref[...], d, NN) + dot(tt_ref[...], pos, NT)
-            halves_to(keep_ref, send_ref, grad, own)
-
-        @pl.when(step == 2)
-        def _():
-            halves_to(keep_ref, send_ref, dot(xt_ref[...], d, NN), own)
-
-    @pl.when(step == 3)
-    def _():
-        vec_ref[...] = jnp.zeros_like(vec_ref)
-        owner, spot = stripe_marks(width, BF)
-
-        def cut(row, marks, mine):
-            return dot(jnp.where(mine, jnp.broadcast_to(row, mine.shape), 0.0).astype(BF), marks, NT)
-
-        bias = [bias_ref[i, 0:1, :] for i in range(3)]
-        grads = bias + [vg2_ref[6:7, :], vg2_ref[4:5, :],
-                        vg2_ref[5:6, :], vg2_ref[10:11, :], vg2_ref[8:9, :], vg2_ref[9:10, :]]
-        for i, row in enumerate(grads):
-            lanes = slice(0, 128) if i < 8 else slice(128, 256)
-            vec_ref[:, i % 8, lanes] = cut(row, spot, owner)
-        broad = width * fan // STRIPES
-        total = jnp.zeros((STRIPES, 128), F32)
-        for f in range(fan):
-            column_at = lax.broadcasted_iota(jnp.int32, (STRIPES, width), 1) + f * width
-            stripe = lax.broadcasted_iota(jnp.int32, (STRIPES, width), 0)
-            mine = (column_at >= stripe * broad) & (column_at < stripe * broad + broad)
-            place = lax.broadcasted_iota(jnp.int32, (128, width), 0)
-            marks = lax.broadcasted_iota(jnp.int32, (128, width), 1) + f * width
-            total += cut(vg2_ref[f : f + 1, :], (marks % broad == place).astype(BF), mine)
-        vec_ref[:, (VECTORS - 1) % 8, 128:256] = total
-        blocks = tab_ref[...].T.reshape((STRIPES // 2, 2, 8, width))
-        vectors = vec_ref[...].reshape((STRIPES // 2, 2, 8, width))
-        zero = jnp.zeros((STRIPES // 2, part - 16, width), BF)
-        for out, pick in ((keep_ref, own == 0), (send_ref, own != 0)):
-            out[:, 0:8] = jnp.where(pick, blocks[:, 0], blocks[:, 1]).astype(BF)
-            out[:, 8:16] = jnp.where(pick, vectors[:, 0], vectors[:, 1]).astype(BF)
-            out[:, 16:part] = zero
-
-
-def project_back(own, d, pos, mats, xt, tt, vg, fan):
+    own = where_ref[1]
+    copy = pltpu.make_async_copy
+
+    def chunk(i):
+        some = [copy(d_hbm.at[i], d.at[i], chunk_fetch.at[0, i])]
+        if i < 2:
+            some += [copy(pos_hbm.at[i], pos.at[i], chunk_fetch.at[1, i])]
+        return some
+
+    for one in chunk(0) + chunk(1) + chunk(2):
+        one.start()
+    for r, out in enumerate(refs[hops + 2 : -4]):
+        at = where_ref[3] ^ r
+        out[0] = sum(ref[at].astype(F32) for ref in refs[:hops]).astype(BF)
+    vec_ref[...] = vec_in_ref[...]
+    marks = stripe_marks(width, BF)
+    table = jnp.zeros((width, buckets), F32)
+    ones = jnp.ones((8, rows), BF)
+    for i in range(3):
+        for one in chunk(i):
+            one.wait()
+        line = dot(ones, d[i], NN)
+        grad = dot(xt[...], d[i], NN)
+        if i < 2:
+            low = pos[i]
+            table = table + dot(w.at[i].reshape(width, width)[...], low, NN)
+            line = line + dot(jnp.ones((8, buckets), BF), low, NT)
+            grad = grad + dot(tt[...], low, NT)
+        place = slice(i * part, (i + 1) * part)
+        halves_to(keep_ref.at[:, place], send_ref.at[:, place], grad, own)
+        vec_ref[:, i, 0:128] = cut(line[0:1], *marks)
+    table_at, vector_at = slice(3 * part, 3 * part + 8), slice(3 * part + 8, 3 * part + 16)
+    halves_to(keep_ref.at[:, table_at], send_ref.at[:, table_at], table.T, own)
+    halves_to(keep_ref.at[:, vector_at], send_ref.at[:, vector_at], vec_ref[...].reshape(STRIPES * 8, width), own)
+
+
+def project_back(where, d, pos, mats, xt, tt, vec, fan, parts=()):
     width, rows = xt.shape
     part = width // STRIPES
     buckets = tt.shape[1]
-    whole = lambda shape: pl.BlockSpec(shape, lambda g: (0,) * len(shape))
-    block = pl.BlockSpec((STRIPES // 2, part, width), lambda g: (0, g, 0))
-    shape = jax.ShapeDtypeStruct
-    half = shape((STRIPES // 2, part * 4, width), BF)
-    return pl.pallas_call(
-        lambda *refs: project_back_kernel(*refs, fan=fan),
-        grid=(4,),
-        in_specs=[pl.BlockSpec(memory_space=pltpu.SMEM),
-                  pl.BlockSpec((1, rows, width), lambda g: (jnp.minimum(g, 2), 0, 0)),
-                  pl.BlockSpec((1, width, buckets), lambda g: (jnp.minimum(g, 1), 0, 0)),
-                  pl.BlockSpec((1, STRIPES, part, width), lambda g: (jnp.minimum(g, 1), 0, 0, 0)),
-                  whole((width, rows)), whole((width, buckets)), whole((16, width))],
-        out_specs=[block, block],
-        out_shape=[half, half],
-        scratch_shapes=[pltpu.VMEM((STRIPES, 8, width), F32), pltpu.VMEM((width, buckets), F32),
-                        pltpu.VMEM((3, 8, width), F32)],
-        compiler_params=big(),
-        cost_estimate=cost(4 << 30, 12 << 20),
+    hbm = pl.BlockSpec(memory_space=pl.ANY)
+    vmem = pl.BlockSpec(memory_space=pltpu.VMEM)
+    half = jax.ShapeDtypeStruct((STRIPES // 2, part * 3 + 16, width), BF)
+    sem = pltpu.SemaphoreType.DMA
+    return pl.pallas_call(
+        lambda *refs: project_back_kernel(*refs, fan=fan, hops=len(parts)),
+        in_specs=[pl.BlockSpec(memory_space=pltpu.SMEM)] + [vmem] * 4 + [hbm] * 2 + [vmem] * len(parts),
+        out_specs=[vmem, vmem] + [vmem] * len(parts),
+        out_shape=[pltpu.VMEM(half.shape, half.dtype), pltpu.VMEM(half.shape, half.dtype)]
+        + [jax.ShapeDtypeStruct((1,) + part_.shape[1:], BF) for part_ in parts],
+        scratch_shapes=[pltpu.VMEM((3, rows, width), BF), pltpu.VMEM((2, width, buckets), BF),
+                        pltpu.VMEM((STRIPES, 8, width), F32), sem((2, 3))],
+        compiler_params=big(32),
         name="project_back",
-    )(own, d, pos, mats, xt, tt, vg)
+    )(where, vec, *[pltpu.with_memory_space_constraint(a, pltpu.VMEM) for a in (mats, xt, tt)],
+      *[pltpu.with_memory_space_constraint(a, pltpu.HBM) for a in (d, pos)], *parts)
 
 
 def token_grad_kernel(fg_ref, d_ref, w_ref, out_ref):
@@ -627,25 +709,30 @@
     )(fg, d, mats)
 
 
-def near_hop_kernel(where_ref, keep_ref, got_ref, *out_refs):
-    for r, out in enumerate(out_refs):
+def near_hop_kernel(where_ref, *refs, groups):
+    keeps, gots, outs = refs[:groups], refs[groups : 2 * groups], refs[2 * groups :]
+    for r, out in enumerate(outs):
         at = where_ref[2] ^ r
-        out[0] = (keep_ref[at].astype(F32) + got_ref[at].astype(F32)).astype(BF)
+        row = 0
+        for keep_ref, got_ref in zip(keeps, gots):
+            rows = keep_ref.shape[1]
+            out[0, row : row + rows] = (keep_ref[at].astype(F32) + got_ref[at].astype(F32)).astype(BF)
+            row += rows
 
 
 def near_hop(where, keep, got):
-    count, rows, width = keep.shape
-    group = pl.BlockSpec((4, rows, width), lambda z: (z, 0, 0))
-    return pl.pallas_call(
-        near_hop_kernel,
+    count, _, width = keep[0].shape
+    group = lambda block: pl.BlockSpec((4,) + block.shape[1:], lambda z: (z, 0, 0))
+    rows = sum(block.shape[1] for block in keep)
+    return pl.pallas_call(
+        lambda *refs: near_hop_kernel(*refs, groups=len(keep)),
         grid=(count // 4,),
-        in_specs=[pl.BlockSpec(memory_space=pltpu.SMEM), group, group],
+        in_specs=[pl.BlockSpec(memory_space=pltpu.SMEM)] + [group(block) for block in keep] * 2,
         out_specs=[pl.BlockSpec((1, rows, width), lambda z: (z, 0, 0))] * 4,
         out_shape=[jax.ShapeDtypeStruct((count // 4, rows, width), BF)] * 4,
         compiler_params=big(16),
-        cost_estimate=cost(keep.size, 6 * keep.size),
         name="near_hop",
-    )(where, keep, got)
+    )(where, *keep, *got)
 
 
 def finish_kernel(*refs, parts, vectors):
@@ -709,13 +796,18 @@
 
 
 class Scatter:
-    def __init__(self, where, keep, send, count):
-        self.where, self.keep, self.count = where, keep, count
-        self.got = xor_permute(send, 1, count)
+    def __init__(self, where, count, space):
+        self.where, self.count, self.space = where, count, space
+        self.keep, self.got = [], []
+
+    def add(self, keep, send):
+        self.keep.append(keep)
+        self.got.append(xor_permute(send, 1, self.count))
 
     def near(self, *after):
         got = tie(self.got, after)
-        parts = near_hop(self.where, self.keep, in_vmem(got))
+        keep = [pltpu.with_memory_space_constraint(part, self.space) for part in self.keep]
+        parts = near_hop(self.where, keep, [in_vmem(part) for part in got])
         self.keep, self.sent = parts[0], parts[1:]
         self.got = [xor_permute(part, 2 * r, self.count) for r, part in enumerate(self.sent, 1)]
 
@@ -805,37 +897,43 @@
         total = lengths[0, 0:1] + lengths[0, 1:2]
         context, probs = attend(total, q, k, v, kr, qr)
         cot = cotangent.reshape(rows, width)
-        layer_out, outer_grad, inner_keep, inner_send, context_grad, fg, vg = feed(
-            where, vecs, context, flat, cot, second_all, fan
+        layer_out, outer_grad, slope, og, low, n1, inv, second, vg = feed_forward(
+            vecs, context, flat, cot, second_all, fan
         )
         outer_blocks = outer_grad.reshape(count, -1, width)
-        groups = width // 128
-        back = lambda dc, first, pairs, before: attend_back(
-            q, k, v, kr, qr, dc, probs, onehot, first, pairs, before
-        )
         if direct:
             outer_sum = scatter_rows(outer_blocks)
-            inner = Scatter(where, inner_keep, inner_send, count)
-            grads = back(context_grad, 0, 1, ())
-            inner.near(grads[0])
-            grads = back(tie(context_grad, inner.sent), 1, groups - 1, grads)
-            inner.far(grads[0])
-            d, pos = tie(tuple(grads), inner.sent)
         else:
             outer_out = scatter_rows(outer_blocks.astype(F32))
-            grads = back(context_grad, 0, 1, ())
-            d, pos = back(context_grad, 1, groups - 1, grads)
-        last_keep, last_send = project_back(where, d, pos, mats, xt, tt, vg, fan)
+        inner_keep, inner_send, context_grad, fg, vg = feed_back(
+            where, vecs, vg, og, low, slope, second, n1, inv, context, second_all, fan
+        )
+        vec = cut_vectors(vg, fan)
+        if direct:
+            inner = Scatter(where, count, pltpu.HBM)
+            inner.add(inner_keep, inner_send)
+            inner.near(vec)
+            context_grad = tie(context_grad, inner.sent)
+        d, pos = attend_back(q, k, v, kr, qr, context_grad, probs, onehot, 0, width // 128, ())
+        if direct:
+            parts = [inner.keep] + [in_vmem(got) for got in inner.got]
+            last_keep, last_send, *parts = project_back(where, d, pos, mats, xt, tt, vec, fan, parts)
+            inner.keep = parts[0]
+            inner.got = [xor_permute(part, 8 * r, count) for r, part in enumerate(parts[1:], 1)]
+        else:
+            last_keep, last_send = project_back(where, d, pos, mats, xt, tt, vec, fan)
 
         part = width // STRIPES
         if direct:
-            last = Scatter(where, last_keep, last_send, count)
+            last = Scatter(where, count, pltpu.VMEM)
+            last.add(last_keep, last_send)
             last.near()
             tokens_grad = token_grads(fg, tie(d, last.sent), mats)
             last.far(tokens_grad)
             inner.got = tie(inner.got, tokens_grad)
             inner_sum = inner.total()
             inner_parts = [inner_sum[f * part : (f + 1) * part] for f in range(fan + 1)]
+            output_out = inner_parts[fan]
             query_out, key_out, value_out, table_out, *pieces, outer_out = finish(
                 [last.keep] + [in_vmem(got) for got in last.got],
                 outer_sum[None], (part, part, part, 8), [piece.shape[0] for piece in vectors],
@@ -843,8 +941,9 @@
         else:
             tokens_grad = token_grads(fg, d, mats)
             inner_parts = scatter_plain(inner_keep, inner_send, (part,) * (fan + 1), count)
+            output_out = inner_parts[fan]
             query_out, key_out, value_out, table_out, _ = scatter_plain(
-                last_keep, last_send, (part,) * 3 + (8, part - 8), count
+                last_keep, last_send, (part,) * 3 + (8, 8), count
             )
             blocks = jnp.stack([last_keep, last_send], axis=1).reshape(STRIPES, -1, width)
             tile = blocks[:, 3 * part + 8 : 3 * part + 16].astype(F32)
@@ -855,7 +954,6 @@
                 line = tile[:, i % 8, lane : lane + length].reshape(-1)
                 pieces.append(lax.psum_scatter(line, AXES, scatter_dimension=0, tiled=True))
         inner_out = jnp.concatenate(inner_parts[:fan], axis=1)
-        output_out = inner_parts[fan]
         (qb, kb, vb, ob, g1, s1, outb, g2, s2, inb) = pieces
         return (
             layer_out.reshape(tokens.shape), tokens_grad.reshape(tokens.shape),

time: 277 us -> 268 us (0.968)
  waiting for transfers between devices: 102 us -> 93.1 us
  Pallas kernels: 123 us -> 126 us
  local copies, waits for them, and re-layouts: 8.33 us -> 5.44 us
    reduce_scatter x1, waiting for transfers between devices: 21.1 us -> 9.34 us  [scatter_rows(): return lax.psum_scatter(blocks, AXES, scatter_dimension=0, tiled=False)]
    pallas_call x4 -> x6, Pallas kernels: 46.7 us -> 53.4 us  [the longest x1 19.4 us: feed_forward(): pl.pallas_call(lambda *refs: feed_forward_kernel(*refs, fan=fan), in_spec...]
    ppermute x21, waiting for transfers between devices: 71.7 us -> 75 us  [xor_permute(): return lax.ppermute(block, AXES, [(d, d ^ mask) for d in range(count)])]
    unnamed x36 -> x30, local copies, waits for them, and re-layouts: 5.81 us -> 2.92 us
    pallas_call x2 -> x1, Pallas kernels: 34.7 us -> 32.1 us  [attend_back(): pl.pallas_call(lambda *refs: attend_back_kernel(*refs, rows=rows, tile=ro...]
  transfers between devices with their start and end apart: 23 -> 23, of which waited for: 12 -> 13; matrix products, arithmetic and copies ran while one was open for 2% -> 2% of each run, Pallas kernels for 32% -> 39%
where the time goes in v1:
time: 268 us
  Pallas kernels  126 us (47%)
  waiting for transfers between devices  93.1 us (35%)
  starting transfers between devices  25.2 us (9%)
  between operations  15.6 us (6%)
  local copies, waits for them, and re-layouts  5.44 us (2%)
    ppermute x21, waiting for transfers between devices, xor_permute(): return lax.ppermute(block, AXES, [(d, d ^ mask) for d in range(count)])  75 us
    pallas_call x1, Pallas kernels, attend_back(): pl.pallas_call(lambda *refs: attend_back_kernel(*refs, rows=rows, tile=ro...  32.1 us
    ppermute x21, starting transfers between devices, xor_permute(): return lax.ppermute(block, AXES, [(d, d ^ mask) for d in range(count)])  25.1 us
    pallas_call x1, Pallas kernels, attend(): pl.pallas_call(lambda *refs: attend_kernel(*refs, rows=rows, tile=rows //...  23.2 us
    pallas_call x1, Pallas kernels, feed_forward(): pl.pallas_call(lambda *refs: feed_forward_kernel(*refs, fan=fan), in_spec...  19.4 us
    pallas_call x1, Pallas kernels, feed_back(): pl.pallas_call(lambda *refs: feed_back_kernel(*refs, fan=fan), in_specs=[...  19.3 us
    pallas_call x1, Pallas kernels, project_all(): pl.pallas_call(lambda *refs: project_kernel(*refs, fan=fan), grid=(width...  10.1 us
    reduce_scatter x1, waiting for transfers between devices, scatter_rows(): return lax.psum_scatter(blocks, AXES, scatter_dimension=0, tiled=False)  9.34 us
  transfers between devices with their start and end apart: 23, of which 13 were waited for; matrix products, arithmetic and copies ran while one was open for 2% of the time, Pallas kernels for 39%

profile of v1, /device:TPU:0, one launch (start us, length us, event | category | flops | bytes accessed | tf_op | source)
XLA Modules:
  0.0 267.8 jit_solution(16185008886814476524)
XLA Ops:
  7.2 2.0 pack.1
  9.3 5.1 %collective-permute-start.2 = (bf16[1,88,768]{2,1,0:T(8,128)(2,1)}, bf16[1,88,768]{2,1,0:T(8,128)(2,1)S(1)}, u32[]{:S(2)}, u32[]{:S(2)}) collective-permute-start(bf16[1,88,768]{2,1,0:T(8,128)(2,1)} %bitcast.32), channel_id=1, source_target_pairs={{0,24},{1,25},{2,26},{3,27},{4,28},{5,29},{6,30},{7,31},{8,16},{9,... | collective-permute-start | bytes 405512 | tf_op jit(solution)/shard_map/ppermute | solution.py:791
  15.1 4.1 %collective-permute-done.2 = bf16[1,88,768]{2,1,0:T(8,128)(2,1)S(1)} collective-permute-done((bf16[1,88,768]{2,1,0:T(8,128)(2,1)}, bf16[1,88,768]{2,1,0:T(8,128)(2,1)S(1)}, u32[]{:S(2)}, u32[]{:S(2)}) %collective-permute-start.2) | collective-permute-done | bytes 135200 | tf_op jit(solution)/shard_map/ppermute | solution.py:791
  19.1 7.0 %collective-permute-done.1 = bf16[1,88,768]{2,1,0:T(8,128)(2,1)S(1)} collective-permute-done((bf16[1,88,768]{2,1,0:T(8,128)(2,1)}, bf16[1,88,768]{2,1,0:T(8,128)(2,1)S(1)}, u32[]{:S(2)}, u32[]{:S(2)}) %collective-permute-start.1) | collective-permute-done | bytes 135200 | tf_op jit(solution)/shard_map/ppermute | solution.py:791
  31.7 17.3 %collective-permute-done.3 = bf16[4,88,768]{2,1,0:T(8,128)(2,1)S(1)} collective-permute-done((bf16[4,88,768]{2,1,0:T(8,128)(2,1)S(1)}, bf16[4,88,768]{2,1,0:T(8,128)(2,1)S(1)}, u32[]{:S(2)}, u32[]{:S(2)}) %collective-permute-start.3) | collective-permute-done | bytes 540704 | tf_op jit(solution)/shard_map/ppermute | solution.py:791
  49.1 13.4 %collective-permute-done.5 = bf16[4,88,768]{2,1,0:T(8,128)(2,1)S(1)} collective-permute-done((bf16[4,88,768]{2,1,0:T(8,128)(2,1)S(1)}, bf16[4,88,768]{2,1,0:T(8,128)(2,1)S(1)}, u32[]{:S(2)}, u32[]{:S(2)}) %collective-permute-start.5) | collective-permute-done | bytes 540704 | tf_op jit(solution)/shard_map/ppermute | solution.py:791
  67.0 10.1 %project.1 = (bf16[512,768]{1,0:T(8,128)(2,1)}, bf16[512,768]{1,0:T(8,128)(2,1)}, bf16[512,768]{1,0:T(8,128)(2,1)}, bf16[1024,768]{1,0:T(8,128)(2,1)}, bf16[1024...) custom-call(s32[4]{0:T(128)} %pad_add_fusion.refs_0_.where_ref, ...), custom_call_target="tpu_custom_call" | custom-call | flops 4294967296 | bytes 12582912 | tf_op jit(solution)/shard_map/project/pallas_call | solution.py:314
  77.1 23.2 %attend.1 = (bf16[512,768]{1,0:T(8,128)(2,1)}, bf16[12,512,512]{2,1,0:T(8,128)(2,1)}) custom-call(s32[1]{0:T(128)} %bitcast.7.refs_0_, bf16[512,768]{1,0:T(8,128)(2,1)} %get-tuple-element.93.refs_1_.refs_0_, bf16[512,768]{1,0:T(8,128)(2,1)} %get-tuple-element.94.refs_2_.refs_1_, bf16[512,768]{1,0:T(8,128)(2,1)} %get-tuple-element.95.refs_3_.refs_2_, ...), custom_call_target="tpu_custom_call" | custom-call | flops 26843545600 | bytes 12582912 | tf_op jit(solution)/shard_map/attend/pallas_call | solution.py:72
  100.3 8.8 %all-gather.3.cloned.1.call-done = bf16[6912,768]{1,0:T(8,128)(2,1)} async-done(((bf16[216,768]{1,0:T(8,128)(2,1)}), bf16[6912,768]{1,0:T(8,128)(2,1)}) %all-gather.3.cloned.1.call-update) | async-done | bytes 10616848 | tf_op jit(solution)/shard_map/all_gather | solution.py:783
  109.1 19.4 %feed_forward.1 = (bf16[512,768]{1,0:T(8,128)(2,1)}, bf16[3072,768]{1,0:T(8,128)(2,1)}, bf16[4,512,768]{2,1,0:T(8,128)(2,1)}, bf16[512,768]{1,0:T(8,128)(2,1)}, ...) custom-call(f32[16,768]{1,0:T(8,128)} %get-tuple-element.92.refs_0_., ...), custom_call_target="tpu_custom_call" | custom-call | tf_op jit(solution)/shard_map/feed_forward/pallas_call | solution.py:465
  128.5 19.3 %feed_back.1 = (bf16[16,120,768]{2,1,0:T(8,128)(2,1)}, bf16[16,120,768]{2,1,0:T(8,128)(2,1)}, bf16[512,768]{1,0:T(8,128)(2,1)}, f32[512,768]{1,0:T(8,128)}, f32[16,768]{1,0:T(8,128)}) custom-call(s32[4]{0:T(128)} %pad_add_fusion.refs_0_.where_ref, f32[16,768]{1,0:T(8,128)} %get-tuple-element.92.refs_0_.refs_1_, f32[16,768]{1,0:T(8,128)} %get-tuple-element.101.refs_2_, ...), custom_call_target="tpu_custom_call" | custom-call | tf_op jit(solution)/shard_map/feed_back/pallas_call | solution.py:572
  149.8 3.8 %collective-permute-done.7.refs_2_ = bf16[16,120,768]{2,1,0:T(8,128)(2,1)S(1)} collective-permute-done((bf16[16,120,768]{2,1,0:T(8,128)(2,1)}, bf16[16,120,768]{2,1,0:T(8,128)(2,1)S(1)}, u32[]{:S(2)}, u32[]{:S(2)}) %collective-permute-start.7) | collective-permute-done | bytes 2949152 | tf_op jit(solution)/shard_map/ppermute | solution.py:791
  153.6 3.9 %near_hop.2 = (bf16[4,120,768]{2,1,0:T(8,128)(2,1)S(1)}, bf16[4,120,768]{2,1,0:T(8,128)(2,1)}, bf16[4,120,768]{2,1,0:T(8,128)(2,1)S(1)}, bf16[4,120,768]{2,1,0:T(8,128)(2,1)S(1)}) custom-call(s32[4]{0:T(128)S(1)} %copy-done.6, bf16[16,120,768]{2,1,0:T(8,128)(2,1)} %get-tuple-element.110.refs_1_, bf16[16,120,768]{2,1,0:T(8,128)(2,1)S(1)} %collective-permute-done.7.refs_2_), custom_call_target="tpu_custom_call" | custom-call | tf_op jit(solution)/shard_map/near_hop/pallas_call | solution.py:727
  160.9 32.1 %attend_back.1 = (bf16[3,512,768]{2,1,0:T(8,128)(2,1)}, bf16[2,768,256]{2,1,0:T(8,128)(2,1)}) custom-call(bf16[512,768]{1,0:T(8,128)(2,1)} %get-tuple-element.93.refs_1_.refs_0_, bf16[512,768]{1,0:T(8,128)(2,1)} %get-tuple-element.94.refs_2_.refs_1_, bf16[512,768]{1,0:T(8,128)(2,1)} %get-tuple-element.95.refs_3_.refs_2_, ...), custom_call_target="tpu_custom_call" | custom-call | flops 40000000000 | bytes 18000000 | tf_op jit(solution)/shard_map/attend_back/pallas_call | solution.py:164
  193.0 8.5 %collective-permute-done.10.refs_10_ = bf16[4,120,768]{2,1,0:T(8,128)(2,1)S(1)} collective-permute-done((bf16[4,120,768]{2,1,0:T(8,128)(2,1)S(1)}, bf16[4,120,768]{2,1,0:T(8,128)(2,1)S(1)}, u32[]{:S(2)}, u32[]{:S(2)}) %collective-permute-start.10) | collective-permute-done | bytes 737312 | tf_op jit(solution)/shard_map/ppermute | solution.py:791
  201.5 8.8 %project_back.1 = (bf16[16,88,768]{2,1,0:T(8,128)(2,1)S(1)}, bf16[16,88,768]{2,1,0:T(8,128)(2,1)S(1)}, bf16[1,120,768]{2,1,0:T(8,128)(2,1)S(1)}, bf16[1,120,768]...) custom-call(s32[4]{0:T(128)S(1)} %copy-done.6, ...), custom_call_target="tpu_custom_call" | custom-call | tf_op jit(solution)/shard_map/project_back/pallas_call | solution.py:672
  212.6 2.3 collective-permute-start.20
  216.1 1.6 collective-permute-start.12
  218.2 6.8 %collective-permute-done.18 = bf16[1,120,768]{2,1,0:T(8,128)(2,1)S(1)} collective-permute-done((bf16[1,120,768]{2,1,0:T(8,128)(2,1)S(1)}, bf16[1,120,768]{2,1,0:T(8,128)(2,1)S(1)}, u32[]{:S(2)}, u32[]{:S(2)}) %collective-permute-start.18) | collective-permute-done | bytes 184352 | tf_op jit(solution)/shard_map/ppermute | solution.py:791
  225.8 3.7 %token_grads.1 = f32[512,768]{1,0:T(8,128)} custom-call(f32[512,768]{1,0:T(8,128)S(1)} %copy-done.2, bf16[3,512,768]{2,1,0:T(8,128)(2,1)S(1)} %copy-done.1, bf16[3,32,24,768]{3,2,1,0:T(8,128)(2,1)S(1)} %copy-done), custom_call_target="tpu_custom_call" | custom-call | flops 2147483648 | bytes 10485760 | tf_op jit(solution)/shard_map/token_grads/pallas_call | solution.py:699
  229.5 3.3 %collective-permute-done.19 = bf16[1,120,768]{2,1,0:T(8,128)(2,1)S(1)} collective-permute-done((bf16[1,120,768]{2,1,0:T(8,128)(2,1)S(1)}, bf16[1,120,768]{2,1,0:T(8,128)(2,1)S(1)}, u32[]{:S(2)}, u32[]{:S(2)}) %collective-permute-start.19) | collective-permute-done | bytes 184352 | tf_op jit(solution)/shard_map/ppermute | solution.py:791
  233.5 9.6 %collective-permute-done.14.refs_3_ = bf16[4,88,768]{2,1,0:T(8,128)(2,1)S(1)} collective-permute-done((bf16[4,88,768]{2,1,0:T(8,128)(2,1)S(1)}, bf16[4,88,768]{2,1,0:T(8,128)(2,1)S(1)}, u32[]{:S(2)}, u32[]{:S(2)}) %collective-permute-start.14) | collective-permute-done | bytes 540704 | tf_op jit(solution)/shard_map/ppermute | solution.py:791
  246.4 2.0 collective-permute-start.17
  249.1 9.3 %reduce-scatter.2.cloned.1.call-done.refs_4_ = bf16[1,96,768]{2,1,0:T(8,128)(2,1)} async-done(((bf16[32,96,768]{2,1,0:T(8,128)(2,1)}), bf16[1,96,768]{2,1,0:T(8,128)(2,1)}) %reduce-scatter.2.cloned.1.call-update) | async-done | bytes 147472 | tf_op jit(solution)/shard_map/reduce_scatter | solution.py:787
  (76 shorter events, 26.9 us)
Async XLA Ops:
  7.2 101.9 %all-gather.3.cloned.1.call-start = ((), (), s32[]{:S(2)}) async-start(), calls=%async_computation.2 | async-start | bytes 10948608 | tf_op jit(solution)/shard_map/all_gather | solution.py:783
  9.2 249.2 %reduce-scatter.2.cloned.1.call-start = ((), (), s32[]{:S(2)}) async-start(), calls=%async_computation.1 | async-start | bytes 4866048 | tf_op jit(solution)/shard_map/reduce_scatter | solution.py:787
  9.3 9.8 %collective-permute-start.2 = (bf16[1,88,768]{2,1,0:T(8,128)(2,1)}, bf16[1,88,768]{2,1,0:T(8,128)(2,1)S(1)}, u32[]{:S(2)}, u32[]{:S(2)}) collective-permute-start(bf16[1,88,768]{2,1,0:T(8,128)(2,1)} %bitcast.32), channel_id=1, source_target_pairs={{0,24},{1,25},{2,26},{3,27},{4,28},{5,29},{6,30},{7,31},{8,16},{9,... | collective-permute-start | bytes 405512 | tf_op jit(solution)/shard_map/ppermute | solution.py:791
  14.4 11.7 %collective-permute-start.1 = (bf16[1,88,768]{2,1,0:T(8,128)(2,1)}, bf16[1,88,768]{2,1,0:T(8,128)(2,1)S(1)}, u32[]{:S(2)}, u32[]{:S(2)}) collective-permute-start(bf16[1,88,768]{2,1,0:T(8,128)(2,1)} %bitcast.33), channel_id=1, source_target_pairs={{0,16},{1,17},{2,18},{3,19},{4,20},{5,21},{6,22},{7,23},{8,24},{9,... | collective-permute-start | bytes 405512 | tf_op jit(solution)/shard_map/ppermute | solution.py:791
  14.4 11.7 %collective-permute-start = (bf16[1,88,768]{2,1,0:T(8,128)(2,1)}, bf16[1,88,768]{2,1,0:T(8,128)(2,1)S(1)}, u32[]{:S(2)}, u32[]{:S(2)}) collective-permute-start(bf16[1,88,768]{2,1,0:T(8,128)(2,1)} %bitcast.34), channel_id=1, source_target_pairs={{0,8},{1,9},{2,10},{3,11},{4,12},{5,13},{6,14},{7,15},{8,0},{9,1},... | collective-permute-start | bytes 405512 | tf_op jit(solution)/shard_map/ppermute | solution.py:791
  27.1 21.9 %collective-permute-start.4 = (bf16[4,88,768]{2,1,0:T(8,128)(2,1)S(1)}, bf16[4,88,768]{2,1,0:T(8,128)(2,1)S(1)}, u32[]{:S(2)}, u32[]{:S(2)}) collective-permute-start(bf16[4,88,768]{2,1,0:T(8,128)(2,1)S(1)} %pad_maximum_fusion), channel_id=1, source_target_pairs={{0,4},{1,5},{2,6},{3,7},{4,0},{5,1},{6,2},{7,3},{8,12},{9,13},{10,... | collective-permute-start | bytes 1622024 | tf_op jit(solution)/shard_map/ppermute | solution.py:791
  28.7 20.3 %collective-permute-start.3 = (bf16[4,88,768]{2,1,0:T(8,128)(2,1)S(1)}, bf16[4,88,768]{2,1,0:T(8,128)(2,1)S(1)}, u32[]{:S(2)}, u32[]{:S(2)}) collective-permute-start(bf16[4,88,768]{2,1,0:T(8,128)(2,1)S(1)} %pad_maximum_fusion), channel_id=1, source_target_pairs={{0,2},{1,3},{2,0},{3,1},{4,6},{5,7},{6,4},{7,5},{8,10},{9,11},{10,... | collective-permute-start | bytes 1622024 | tf_op jit(solution)/shard_map/ppermute | solution.py:791
  31.1 31.4 %collective-permute-start.5 = (bf16[4,88,768]{2,1,0:T(8,128)(2,1)S(1)}, bf16[4,88,768]{2,1,0:T(8,128)(2,1)S(1)}, u32[]{:S(2)}, u32[]{:S(2)}) collective-permute-start(bf16[4,88,768]{2,1,0:T(8,128)(2,1)S(1)} %pad_maximum_fusion), channel_id=1, source_target_pairs={{0,6},{1,7},{2,4},{3,5},{4,2},{5,3},{6,0},{7,1},{8,14},{9,15},{10,... | collective-permute-start | bytes 1622024 | tf_op jit(solution)/shard_map/ppermute | solution.py:791
  62.6 4.5 %collective-permute-start.6 = (bf16[16,88,768]{2,1,0:T(8,128)(2,1)S(1)}, bf16[16,88,768]{2,1,0:T(8,128)(2,1)}, u32[]{:S(2)}, u32[]{:S(2)}) collective-permute-start(bf16[16,88,768]{2,1,0:T(8,128)(2,1)S(1)} %constant_dynamic-update-slice_fusion.refs_1_.refs_3_.refs_5_.refs_7_.refs_9_), channel_id=1, source_target_pairs={{0,1},{1,0},{2,3},{3,2},{4,5},{5,4},{6,7},{7,6},{8,9},{9,8},{10,11... | collective-permute-start | bytes 6488072 | tf_op jit(solution)/shard_map/ppermute | solution.py:791
  147.8 5.8 %collective-permute-start.7 = (bf16[16,120,768]{2,1,0:T(8,128)(2,1)}, bf16[16,120,768]{2,1,0:T(8,128)(2,1)S(1)}, u32[]{:S(2)}, u32[]{:S(2)}) collective-permute-start(bf16[16,120,768]{2,1,0:T(8,128)(2,1)} %get-tuple-element.111), channel_id=1, source_target_pairs={{0,1},{1,0},{2,3},{3,2},{4,5},{5,4},{6,7},{7,6},{8,9},{9,8},{10,11... | collective-permute-start | bytes 8847368 | tf_op jit(solution)/shard_map/ppermute | solution.py:791
  157.4 35.6 %collective-permute-start.8 = (bf16[4,120,768]{2,1,0:T(8,128)(2,1)}, bf16[4,120,768]{2,1,0:T(8,128)(2,1)S(1)}, u32[]{:S(2)}, u32[]{:S(2)}) collective-permute-start(bf16[4,120,768]{2,1,0:T(8,128)(2,1)} %get-tuple-element.114), channel_id=1, source_target_pairs={{0,2},{1,3},{2,0},{3,1},{4,6},{5,7},{6,4},{7,5},{8,10},{9,11},{10,... | collective-permute-start | bytes 2211848 | tf_op jit(solution)/shard_map/ppermute | solution.py:791
  158.9 34.1 %collective-permute-start.9 = (bf16[4,120,768]{2,1,0:T(8,128)(2,1)S(1)}, bf16[4,120,768]{2,1,0:T(8,128)(2,1)S(1)}, u32[]{:S(2)}, u32[]{:S(2)}) collective-permute-start(bf16[4,120,768]{2,1,0:T(8,128)(2,1)S(1)} %get-tuple-element.115), channel_id=1, source_target_pairs={{0,4},{1,5},{2,6},{3,7},{4,0},{5,1},{6,2},{7,3},{8,12},{9,13},{10,... | collective-permute-start | bytes 2211848 | tf_op jit(solution)/shard_map/ppermute | solution.py:791
  159.5 42.1 %collective-permute-start.10 = (bf16[4,120,768]{2,1,0:T(8,128)(2,1)S(1)}, bf16[4,120,768]{2,1,0:T(8,128)(2,1)S(1)}, u32[]{:S(2)}, u32[]{:S(2)}) collective-permute-start(bf16[4,120,768]{2,1,0:T(8,128)(2,1)S(1)} %get-tuple-element.116), channel_id=1, source_target_pairs={{0,6},{1,7},{2,4},{3,5},{4,2},{5,3},{6,0},{7,1},{8,14},{9,15},{10,... | collective-permute-start | bytes 2211848 | tf_op jit(solution)/shard_map/ppermute | solution.py:791
  160.9 40.6 %copy-start.4 = (bf16[768,256]{1,0:T(8,128)(2,1)S(1)}, bf16[768,256]{1,0:T(8,128)(2,1)}, u32[]{:S(2)}) copy-start(bf16[768,256]{1,0:T(8,128)(2,1)} %get-tuple-element.123.refs_4_) | copy-start | bytes 1179652
  210.4 4.5 %collective-permute-start.11 = (bf16[16,88,768]{2,1,0:T(8,128)(2,1)S(1)}, bf16[16,88,768]{2,1,0:T(8,128)(2,1)S(1)}, u32[]{:S(2)}, u32[]{:S(2)}) collective-permute-start(bf16[16,88,768]{2,1,0:T(8,128)(2,1)S(1)} %get-tuple-element.127), channel_id=1, source_target_pairs={{0,1},{1,0},{2,3},{3,2},{4,5},{5,4},{6,7},{7,6},{8,9},{9,8},{10,11... | collective-permute-start | bytes 6488072 | tf_op jit(solution)/shard_map/ppermute | solution.py:791
  210.5 14.5 %collective-permute-start.18 = (bf16[1,120,768]{2,1,0:T(8,128)(2,1)S(1)}, bf16[1,120,768]{2,1,0:T(8,128)(2,1)S(1)}, u32[]{:S(2)}, u32[]{:S(2)}) collective-permute-start(bf16[1,120,768]{2,1,0:T(8,128)(2,1)S(1)} %get-tuple-element.148), channel_id=1, source_target_pairs={{0,8},{1,9},{2,10},{3,11},{4,12},{5,13},{6,14},{7,15},{8,0},{9,1},... | collective-permute-start | bytes 552968 | tf_op jit(solution)/shard_map/ppermute | solution.py:791
  211.8 21.0 %collective-permute-start.19 = (bf16[1,120,768]{2,1,0:T(8,128)(2,1)S(1)}, bf16[1,120,768]{2,1,0:T(8,128)(2,1)S(1)}, u32[]{:S(2)}, u32[]{:S(2)}) collective-permute-start(bf16[1,120,768]{2,1,0:T(8,128)(2,1)S(1)} %get-tuple-element.149), channel_id=1, source_target_pairs={{0,16},{1,17},{2,18},{3,19},{4,20},{5,21},{6,22},{7,23},{8,24},{9,... | collective-permute-start | bytes 552968 | tf_op jit(solution)/shard_map/ppermute | solution.py:791
  212.6 20.1 %collective-permute-start.20 = (bf16[1,120,768]{2,1,0:T(8,128)(2,1)S(1)}, bf16[1,120,768]{2,1,0:T(8,128)(2,1)S(1)}, u32[]{:S(2)}, u32[]{:S(2)}) collective-permute-start(bf16[1,120,768]{2,1,0:T(8,128)(2,1)S(1)} %get-tuple-element.150), channel_id=1, source_target_pairs={{0,24},{1,25},{2,26},{3,27},{4,28},{5,29},{6,30},{7,31},{8,16},{9,... | collective-permute-start | bytes 552968 | tf_op jit(solution)/shard_map/ppermute | solution.py:791
  216.1 17.5 %collective-permute-start.12 = (bf16[4,88,768]{2,1,0:T(8,128)(2,1)S(1)}, bf16[4,88,768]{2,1,0:T(8,128)(2,1)S(1)}, u32[]{:S(2)}, u32[]{:S(2)}) collective-permute-start(bf16[4,88,768]{2,1,0:T(8,128)(2,1)S(1)} %get-tuple-element.128), channel_id=1, source_target_pairs={{0,2},{1,3},{2,0},{3,1},{4,6},{5,7},{6,4},{7,5},{8,10},{9,11},{10,... | collective-permute-start | bytes 1622024 | tf_op jit(solution)/shard_map/ppermute | solution.py:791
  217.7 15.9 %collective-permute-start.13 = (bf16[4,88,768]{2,1,0:T(8,128)(2,1)S(1)}, bf16[4,88,768]{2,1,0:T(8,128)(2,1)S(1)}, u32[]{:S(2)}, u32[]{:S(2)}) collective-permute-start(bf16[4,88,768]{2,1,0:T(8,128)(2,1)S(1)} %get-tuple-element.129), channel_id=1, source_target_pairs={{0,4},{1,5},{2,6},{3,7},{4,0},{5,1},{6,2},{7,3},{8,12},{9,13},{10,... | collective-permute-start | bytes 1622024 | tf_op jit(solution)/shard_map/ppermute | solution.py:791
  225.0 18.1 %collective-permute-start.14 = (bf16[4,88,768]{2,1,0:T(8,128)(2,1)S(1)}, bf16[4,88,768]{2,1,0:T(8,128)(2,1)S(1)}, u32[]{:S(2)}, u32[]{:S(2)}) collective-permute-start(bf16[4,88,768]{2,1,0:T(8,128)(2,1)S(1)} %get-tuple-element.130), channel_id=1, source_target_pairs={{0,6},{1,7},{2,4},{3,5},{4,2},{5,3},{6,0},{7,1},{8,14},{9,15},{10,... | collective-permute-start | bytes 1622024 | tf_op jit(solution)/shard_map/ppermute | solution.py:791
  243.9 14.5 %collective-permute-start.15 = (bf16[1,88,768]{2,1,0:T(8,128)(2,1)S(1)}, bf16[1,88,768]{2,1,0:T(8,128)(2,1)S(1)}, u32[]{:S(2)}, u32[]{:S(2)}) collective-permute-start(bf16[1,88,768]{2,1,0:T(8,128)(2,1)S(1)} %get-tuple-element.137), channel_id=1, source_target_pairs={{0,8},{1,9},{2,10},{3,11},{4,12},{5,13},{6,14},{7,15},{8,0},{9,1},... | collective-permute-start | bytes 405512 | tf_op jit(solution)/shard_map/ppermute | solution.py:791
  245.2 14.0 %collective-permute-start.16 = (bf16[1,88,768]{2,1,0:T(8,128)(2,1)S(1)}, bf16[1,88,768]{2,1,0:T(8,128)(2,1)S(1)}, u32[]{:S(2)}, u32[]{:S(2)}) collective-permute-start(bf16[1,88,768]{2,1,0:T(8,128)(2,1)S(1)} %get-tuple-element.138), channel_id=1, source_target_pairs={{0,16},{1,17},{2,18},{3,19},{4,20},{5,21},{6,22},{7,23},{8,24},{9,... | collective-permute-start | bytes 405512 | tf_op jit(solution)/shard_map/ppermute | solution.py:791
  246.4 12.7 %collective-permute-start.17 = (bf16[1,88,768]{2,1,0:T(8,128)(2,1)S(1)}, bf16[1,88,768]{2,1,0:T(8,128)(2,1)S(1)}, u32[]{:S(2)}, u32[]{:S(2)}) collective-permute-start(bf16[1,88,768]{2,1,0:T(8,128)(2,1)S(1)} %get-tuple-element.139), channel_id=1, source_target_pairs={{0,24},{1,25},{2,26},{3,27},{4,28},{5,29},{6,30},{7,31},{8,16},{9,... | collective-permute-start | bytes 405512 | tf_op jit(solution)/shard_map/ppermute | solution.py:791
  (10 other events, 181.6 us)
Sparse Core Ops, SparseCore 0:
  10.9 98.0 all-gather.2
  128.6 129.8 reduce-scatter.1

commit v2 on v1

--- a/solution.py
+++ b/solution.py
@@ -39,17 +39,22 @@
         return pltpu.roll(grid_scores, span - (tile - 1), 1, stride=1, stride_axis=0)[:, :rows]
 
     values = stacked(v_ref[...])
-    for b in range(rows // tile):
-        sl = slice(b * tile, (b + 1) * tile)
-        low = rows - tile - b * tile
-        grid_scores = dot(stacked(k_ref[sl, :]), qr_ref[low : low + span, :], NT)
+
+    def places(b):
+        sl = pl.ds(pl.multiple_of(b * tile, tile), tile)
+        return sl, pl.ds(pl.multiple_of(rows - tile - b * tile, tile), span)
+
+    def rows_of_keys(b, carry):
+        sl, window = places(b)
+        grid_scores = dot(stacked(k_ref[sl, :]), qr_ref[window, :], NT)
         for head in range(2):
             t_ref[head, sl, :] = skewed(grid_scores[head * tile : (head + 1) * tile])
-    for b in range(rows // tile):
-        sl = slice(b * tile, (b + 1) * tile)
-        low = rows - tile - b * tile
+        return carry
+
+    def rows_of_queries(b, carry):
+        sl, window = places(b)
         q = stacked(q_ref[sl, :])
-        grid_scores = dot(q, kr_ref[low : low + span, :], NT)
+        grid_scores = dot(q, kr_ref[window, :], NT)
         raw = (
             dot(q, k_ref[...], NT)
             + jnp.concatenate([skewed(grid_scores[:tile]), skewed(grid_scores[tile:])], axis=0)
@@ -63,6 +68,10 @@
         p_ref[1, sl, :] = probs[tile:]
         both = jnp.concatenate([probs[:tile], probs[tile:]], axis=1)
         c_ref[sl, :] = dot(both, values, NN).astype(BF)
+        return carry
+
+    lax.fori_loop(0, rows // tile, rows_of_keys, 0)
+    lax.fori_loop(0, rows // tile, rows_of_queries, 0)
 
 
 def attend(total, q, k, v, kr, qr):
@@ -621,43 +630,53 @@
 
 def project_back_kernel(where_ref, vec_in_ref, w, xt, tt, d_hbm, pos_hbm, *refs, fan, hops):
     keep_ref, send_ref = refs[hops : hops + 2]
-    d, pos, vec_ref, chunk_fetch = refs[-4:]
+    d, pos, vec_ref, grad_ref, line_ref, table_ref, chunk_fetch = refs[-7:]
     width, rows = xt.shape
     buckets = tt.shape[1]
     part = width // STRIPES
     own = where_ref[1]
     copy = pltpu.make_async_copy
 
-    def chunk(i):
-        some = [copy(d_hbm.at[i], d.at[i], chunk_fetch.at[0, i])]
-        if i < 2:
-            some += [copy(pos_hbm.at[i], pos.at[i], chunk_fetch.at[1, i])]
-        return some
-
-    for one in chunk(0) + chunk(1) + chunk(2):
+    def fetch_d(i):
+        return copy(d_hbm.at[i], d.at[i], chunk_fetch.at[0, i])
+
+    def fetch_pos(i):
+        return copy(pos_hbm.at[i], pos.at[i], chunk_fetch.at[1, i])
+
+    for one in (fetch_d(0), fetch_pos(0), fetch_d(1), fetch_pos(1), fetch_d(2)):
         one.start()
-    for r, out in enumerate(refs[hops + 2 : -4]):
+    for r, out in enumerate(refs[hops + 2 : -7]):
         at = where_ref[3] ^ r
-        out[0] = sum(ref[at].astype(F32) for ref in refs[:hops]).astype(BF)
+        row = 0
+        for ref, got in (refs[0:2], refs[2:4])[: hops // 2]:
+            rows_here = ref.shape[1]
+            out[0, row : row + rows_here] = (ref[at].astype(F32) + got[at].astype(F32)).astype(BF)
+            row += rows_here
     vec_ref[...] = vec_in_ref[...]
+    table_ref[...] = jnp.zeros_like(table_ref)
+
+    def project(i, carry):
+        fetch_d(i).wait()
+        grad_ref[...] = dot(xt[...], d[i], NN)
+        line_ref[i] = dot(jnp.ones((8, rows), BF), d[i], NN)
+
+        @pl.when(i < 2)
+        def _():
+            fetch_pos(i).wait()
+            grad_ref[...] += dot(tt[...], pos[i], NT)
+            line_ref[i] += dot(jnp.ones((8, buckets), BF), pos[i], NT)
+            table_ref[...] += dot(w.at[i].reshape(width, width)[...], pos[i], NN)
+
+        place = pl.ds(pl.multiple_of(i * part, 8), part)
+        halves_to(keep_ref.at[:, place], send_ref.at[:, place], grad_ref[...], own)
+        return carry
+
+    lax.fori_loop(0, 3, project, 0)
     marks = stripe_marks(width, BF)
-    table = jnp.zeros((width, buckets), F32)
-    ones = jnp.ones((8, rows), BF)
     for i in range(3):
-        for one in chunk(i):
-            one.wait()
-        line = dot(ones, d[i], NN)
-        grad = dot(xt[...], d[i], NN)
-        if i < 2:
-            low = pos[i]
-            table = table + dot(w.at[i].reshape(width, width)[...], low, NN)
-            line = line + dot(jnp.ones((8, buckets), BF), low, NT)
-            grad = grad + dot(tt[...], low, NT)
-        place = slice(i * part, (i + 1) * part)
-        halves_to(keep_ref.at[:, place], send_ref.at[:, place], grad, own)
-        vec_ref[:, i, 0:128] = cut(line[0:1], *marks)
+        vec_ref[:, i, 0:128] = cut(line_ref[i, 0:1], *marks)
     table_at, vector_at = slice(3 * part, 3 * part + 8), slice(3 * part + 8, 3 * part + 16)
-    halves_to(keep_ref.at[:, table_at], send_ref.at[:, table_at], table.T, own)
+    halves_to(keep_ref.at[:, table_at], send_ref.at[:, table_at], table_ref[...].T, own)
     halves_to(keep_ref.at[:, vector_at], send_ref.at[:, vector_at], vec_ref[...].reshape(STRIPES * 8, width), own)
 
 
@@ -674,9 +693,10 @@
         in_specs=[pl.BlockSpec(memory_space=pltpu.SMEM)] + [vmem] * 4 + [hbm] * 2 + [vmem] * len(parts),
         out_specs=[vmem, vmem] + [vmem] * len(parts),
         out_shape=[pltpu.VMEM(half.shape, half.dtype), pltpu.VMEM(half.shape, half.dtype)]
-        + [jax.ShapeDtypeStruct((1,) + part_.shape[1:], BF) for part_ in parts],
+        + [jax.ShapeDtypeStruct((1, sum(part_.shape[1] for part_ in parts[::2]), width), BF)] * len(parts),
         scratch_shapes=[pltpu.VMEM((3, rows, width), BF), pltpu.VMEM((2, width, buckets), BF),
-                        pltpu.VMEM((STRIPES, 8, width), F32), sem((2, 3))],
+                        pltpu.VMEM((STRIPES, 8, width), F32), pltpu.VMEM((width, width), F32),
+                        pltpu.VMEM((3, 8, width), F32), pltpu.VMEM((width, buckets), F32), sem((2, 3))],
         compiler_params=big(32),
         name="project_back",
     )(where, vec, *[pltpu.with_memory_space_constraint(a, pltpu.VMEM) for a in (mats, xt, tt)],
@@ -759,6 +779,53 @@
         compiler_params=big(16),
         name="finish",
     )(*parts, outer)
+
+
+def first_turn_kernel(where_ref, keep_ref, got_ref, a_keep, a_send, b_keep, b_send):
+    y, x = where_ref[2] & 1, where_ref[2] >> 1
+    cut = a_keep.shape[1]
+    first, second = slice(0, cut), slice(cut, keep_ref.shape[1])
+    add = lambda at, rows: (keep_ref[at, rows, :].astype(F32) + got_ref[at, rows, :].astype(F32)).astype(BF)
+    for i in range(2):
+        a_keep[i] = add(i * 2 + y, first)
+        a_send[i] = add(i * 2 + 1 - y, first)
+        b_keep[i] = add(x * 2 + i, second)
+        b_send[i] = add((1 - x) * 2 + i, second)
+
+
+def first_turn(where, keep, got, cut):
+    count, rows, width = keep.shape
+    group = pl.BlockSpec((4, rows, width), lambda z: (z, 0, 0))
+    parts = (cut, cut, rows - cut, rows - cut)
+    return pl.pallas_call(
+        first_turn_kernel,
+        grid=(count // 4,),
+        in_specs=[pl.BlockSpec(memory_space=pltpu.SMEM), group, group],
+        out_specs=[pl.BlockSpec((2, part, width), lambda z: (z, 0, 0)) for part in parts],
+        out_shape=[jax.ShapeDtypeStruct((count // 2, part, width), BF) for part in parts],
+        compiler_params=big(16),
+        name="first_turn",
+    )(where, keep, got)
+
+
+def second_turn_kernel(where_ref, a_ref, a_got, b_ref, b_got, a_keep, a_send, b_keep, b_send):
+    y, x = where_ref[2] & 1, where_ref[2] >> 1
+    for ref, got, own, keep, send in ((a_ref, a_got, x, a_keep, a_send), (b_ref, b_got, y, b_keep, b_send)):
+        for z in range(keep.shape[0]):
+            for out, at in ((keep, z * 2 + own), (send, z * 2 + 1 - own)):
+                out[z] = (ref[at].astype(F32) + got[at].astype(F32)).astype(BF)
+
+
+def second_turn(where, a_keep, a_got, b_keep, b_got):
+    vmem = pl.BlockSpec(memory_space=pltpu.VMEM)
+    shape = lambda block: jax.ShapeDtypeStruct((block.shape[0] // 2,) + block.shape[1:], BF)
+    return pl.pallas_call(
+        second_turn_kernel,
+        in_specs=[pl.BlockSpec(memory_space=pltpu.SMEM)] + [vmem] * 4,
+        out_shape=[shape(a_keep)] * 2 + [shape(b_keep)] * 2,
+        compiler_params=big(16),
+        name="second_turn",
+    )(where, a_keep, a_got, b_keep, b_got)
 
 
 def far_hop_kernel(where_ref, *refs):
@@ -911,15 +978,27 @@
         vec = cut_vectors(vg, fan)
         if direct:
             inner = Scatter(where, count, pltpu.HBM)
-            inner.add(inner_keep, inner_send)
-            inner.near(vec)
-            context_grad = tie(context_grad, inner.sent)
-        d, pos = attend_back(q, k, v, kr, qr, context_grad, probs, onehot, 0, width // 128, ())
+            inner_got = tie(xor_permute(inner_send, 1, count), vec)
+            inner_keep = pltpu.with_memory_space_constraint(inner_keep, pltpu.HBM)
+            a_keep, a_send, b_keep, b_send = first_turn(where, inner_keep, in_vmem(inner_got), 64)
+            a_got, b_got = xor_permute(a_send, 2, count), xor_permute(b_send, 4, count)
+            context_grad = tie(context_grad, (a_send, b_send))
+        most = width // 128 * 2 // 3
+        back = lambda dc, first, pairs, before: attend_back(
+            q, k, v, kr, qr, dc, probs, onehot, first, pairs, before
+        )
+        grads = back(context_grad, 0, most, ())
         if direct:
-            parts = [inner.keep] + [in_vmem(got) for got in inner.got]
+            a_got, b_got = tie((a_got, b_got), grads[0])
+            a_keep, a_send, b_keep, b_send = second_turn(where, a_keep, in_vmem(a_got), b_keep, in_vmem(b_got))
+            a_got, b_got = xor_permute(a_send, 4, count), xor_permute(b_send, 2, count)
+            context_grad = tie(context_grad, (a_send, b_send))
+        d, pos = back(context_grad, most, width // 128 - most, grads)
+        if direct:
+            parts = [a_keep, in_vmem(a_got), b_keep, in_vmem(b_got)]
             last_keep, last_send, *parts = project_back(where, d, pos, mats, xt, tt, vec, fan, parts)
             inner.keep = parts[0]
-            inner.got = [xor_permute(part, 8 * r, count) for r, part in enumerate(parts[1:], 1)]
+            inner_sent = parts[1:]
         else:
             last_keep, last_send = project_back(where, d, pos, mats, xt, tt, vec, fan)
 
@@ -928,6 +1007,8 @@
             last = Scatter(where, count, pltpu.VMEM)
             last.add(last_keep, last_send)
             last.near()
+            inner_sent[2] = tie(inner_sent[2], last.sent)
+            inner.got = [xor_permute(part, 8 * r, count) for r, part in enumerate(inner_sent, 1)]
             tokens_grad = token_grads(fg, tie(d, last.sent), mats)
             last.far(tokens_grad)
             inner.got = tie(inner.got, tokens_grad)

time: 268 us -> 266 us (level)
  waiting for transfers between devices: 93.1 us -> 81.3 us
  Pallas kernels: 126 us -> 132 us
  starting transfers between devices: 25.2 us -> 28.5 us
    reduce_scatter x1, waiting for transfers between devices: 9.34 us -> 4.03 us  [scatter_rows(): return lax.psum_scatter(blocks, AXES, scatter_dimension=0, tiled=False)]
    all_gather x1, waiting for transfers between devices: 8.75 us -> 4.49 us  [gather_rows(): return lax.all_gather(block, AXES, axis=0, tiled=False)]
    pallas_call x1, Pallas kernels: 23.2 us -> 27.5 us  [attend(): pl.pallas_call(lambda *refs: attend_kernel(*refs, rows=rows, tile=rows //...]
    pallas_call x2 -> x1, Pallas kernels: 4.99 us -> 1.13 us  [near_hop(): pl.pallas_call(lambda *refs: near_hop_kernel(*refs, groups=len(keep)), gr...]
    pallas_call x0 -> x2, Pallas kernels: none -> 3.83 us  [the longest x1 2.95 us: first_turn(): pl.pallas_call(first_turn_kernel, grid=(count // 4,), in_specs=[pl.BlockS...]
    ppermute x21 -> x22, starting transfers between devices: 25.1 us -> 28.5 us  [xor_permute(): return lax.ppermute(block, AXES, [(d, d ^ mask) for d in range(count)])]
    pallas_call x1 -> x2, Pallas kernels: 32.1 us -> 34.9 us  [attend_back(): pl.pallas_call(lambda *refs: attend_back_kernel(*refs, rows=rows, tile=ro...]
    ppermute x21 -> x22, waiting for transfers between devices: 75 us -> 72.8 us  [xor_permute(): return lax.ppermute(block, AXES, [(d, d ^ mask) for d in range(count)])]
  transfers between devices with their start and end apart: 23 -> 24, of which waited for: 13 -> 16; matrix products, arithmetic and copies ran while one was open for 2% -> 2% of each run, Pallas kernels for 39% -> 41%
where the time goes in v2:
time: 266 us; the launch traced here: 265 us
  Pallas kernels  132 us (50%)
  waiting for transfers between devices  81.3 us (31%)
  starting transfers between devices  28.5 us (11%)
  between operations  15.6 us (6%)
  local copies, waits for them, and re-layouts  5.45 us (2%)
    ppermute x22, waiting for transfers between devices, xor_permute(): return lax.ppermute(block, AXES, [(d, d ^ mask) for d in range(count)])  72.8 us
    pallas_call x2, Pallas kernels, attend_back(): pl.pallas_call(lambda *refs: attend_back_kernel(*refs, rows=rows, tile=ro...  34.9 us
    ppermute x22, starting transfers between devices, xor_permute(): return lax.ppermute(block, AXES, [(d, d ^ mask) for d in range(count)])  28.5 us
    pallas_call x1, Pallas kernels, attend(): pl.pallas_call(lambda *refs: attend_kernel(*refs, rows=rows, tile=rows //...  27.5 us
    pallas_call x1, Pallas kernels, feed_back(): pl.pallas_call(lambda *refs: feed_back_kernel(*refs, fan=fan), in_specs=[...  19.5 us
    pallas_call x1, Pallas kernels, feed_forward(): pl.pallas_call(lambda *refs: feed_forward_kernel(*refs, fan=fan), in_spec...  19.4 us
    pallas_call x1, Pallas kernels, project_all(): pl.pallas_call(lambda *refs: project_kernel(*refs, fan=fan), grid=(width...  10.1 us
    pallas_call x1, Pallas kernels, project_back(): pl.pallas_call(lambda *refs: project_back_kernel(*refs, fan=fan, hops=len...  7.63 us
  transfers between devices with their start and end apart: 24, of which 16 were waited for; matrix products, arithmetic and copies ran while one was open for 2% of the time, Pallas kernels for 41%

profile of v2, /device:TPU:0, one launch (start us, length us, event | category | flops | bytes accessed | tf_op | source)
XLA Modules:
  0.0 265.4 jit_solution(3168051169864301837)
XLA Ops:
  9.3 5.1 %collective-permute-start.2 = (bf16[1,88,768]{2,1,0:T(8,128)(2,1)}, bf16[1,88,768]{2,1,0:T(8,128)(2,1)S(1)}, u32[]{:S(2)}, u32[]{:S(2)}) collective-permute-start(bf16[1,88,768]{2,1,0:T(8,128)(2,1)} %bitcast.32), channel_id=1, source_target_pairs={{0,24},{1,25},{2,26},{3,27},{4,28},{5,29},{6,30},{7,31},{8,16},{9,... | collective-permute-start | bytes 405512 | tf_op jit(solution)/shard_map/ppermute | solution.py:858
  15.1 4.1 %collective-permute-done.2 = bf16[1,88,768]{2,1,0:T(8,128)(2,1)S(1)} collective-permute-done((bf16[1,88,768]{2,1,0:T(8,128)(2,1)}, bf16[1,88,768]{2,1,0:T(8,128)(2,1)S(1)}, u32[]{:S(2)}, u32[]{:S(2)}) %collective-permute-start.2) | collective-permute-done | bytes 135200 | tf_op jit(solution)/shard_map/ppermute | solution.py:858
  19.1 7.0 %collective-permute-done.1 = bf16[1,88,768]{2,1,0:T(8,128)(2,1)S(1)} collective-permute-done((bf16[1,88,768]{2,1,0:T(8,128)(2,1)}, bf16[1,88,768]{2,1,0:T(8,128)(2,1)S(1)}, u32[]{:S(2)}, u32[]{:S(2)}) %collective-permute-start.1) | collective-permute-done | bytes 135200 | tf_op jit(solution)/shard_map/ppermute | solution.py:858
  31.7 17.3 %collective-permute-done.3 = bf16[4,88,768]{2,1,0:T(8,128)(2,1)S(1)} collective-permute-done((bf16[4,88,768]{2,1,0:T(8,128)(2,1)S(1)}, bf16[4,88,768]{2,1,0:T(8,128)(2,1)S(1)}, u32[]{:S(2)}, u32[]{:S(2)}) %collective-permute-start.3) | collective-permute-done | bytes 540704 | tf_op jit(solution)/shard_map/ppermute | solution.py:858
  49.1 13.4 %collective-permute-done.5 = bf16[4,88,768]{2,1,0:T(8,128)(2,1)S(1)} collective-permute-done((bf16[4,88,768]{2,1,0:T(8,128)(2,1)S(1)}, bf16[4,88,768]{2,1,0:T(8,128)(2,1)S(1)}, u32[]{:S(2)}, u32[]{:S(2)}) %collective-permute-start.5) | collective-permute-done | bytes 540704 | tf_op jit(solution)/shard_map/ppermute | solution.py:858
  67.0 10.1 %project.1 = (bf16[512,768]{1,0:T(8,128)(2,1)}, bf16[512,768]{1,0:T(8,128)(2,1)}, bf16[512,768]{1,0:T(8,128)(2,1)}, bf16[1024,768]{1,0:T(8,128)(2,1)}, bf16[1024...) custom-call(s32[4]{0:T(128)} %pad_add_fusion.refs_0_.where_ref, ...), custom_call_target="tpu_custom_call" | custom-call | flops 4294967296 | bytes 12582912 | tf_op jit(solution)/shard_map/project/pallas_call | solution.py:323
  77.1 27.5 %attend.1 = (bf16[512,768]{1,0:T(8,128)(2,1)}, bf16[12,512,512]{2,1,0:T(8,128)(2,1)}) custom-call(s32[1]{0:T(128)} %bitcast.7.refs_0_, bf16[512,768]{1,0:T(8,128)(2,1)} %get-tuple-element.103.refs_1_.refs_0_, bf16[512,768]{1,0:T(8,128)(2,1)} %get-tuple-element.104.refs_2_.refs_1_, bf16[512,768]{1,0:T(8,128)(2,1)} %get-tuple-element.105.refs_3_.refs_2_, ...), custom_call_target="tpu_custom_call" | custom-call | flops 26843545600 | bytes 12582912 | tf_op jit(solution)/shard_map/attend/pallas_call | solution.py:81
  104.6 4.5 %all-gather.3.cloned.1.call-done = bf16[6912,768]{1,0:T(8,128)(2,1)} async-done(((bf16[216,768]{1,0:T(8,128)(2,1)}), bf16[6912,768]{1,0:T(8,128)(2,1)}) %all-gather.3.cloned.1.call-update) | async-done | bytes 10616848 | tf_op jit(solution)/shard_map/all_gather | solution.py:850
  109.1 19.4 %feed_forward.1 = (bf16[512,768]{1,0:T(8,128)(2,1)}, bf16[3072,768]{1,0:T(8,128)(2,1)}, bf16[4,512,768]{2,1,0:T(8,128)(2,1)}, bf16[512,768]{1,0:T(8,128)(2,1)}, ...) custom-call(f32[16,768]{1,0:T(8,128)} %get-tuple-element.102.refs_0_, ...), custom_call_target="tpu_custom_call" | custom-call | tf_op jit(solution)/shard_map/feed_forward/pallas_call | solution.py:474
  128.5 19.5 %feed_back.1 = (bf16[16,120,768]{2,1,0:T(8,128)(2,1)}, bf16[16,120,768]{2,1,0:T(8,128)(2,1)}, bf16[512,768]{1,0:T(8,128)(2,1)}, f32[512,768]{1,0:T(8,128)}, f32[16,768]{1,0:T(8,128)}) custom-call(s32[4]{0:T(128)} %pad_add_fusion.refs_0_.where_ref, f32[16,768]{1,0:T(8,128)} %get-tuple-element.102.refs_0_.refs_1_, f32[16,768]{1,0:T(8,128)} %get-tuple-element.111.refs_2_, ...), custom_call_target="tpu_custom_call" | custom-call | tf_op jit(solution)/shard_map/feed_back/pallas_call | solution.py:581
  149.9 3.7 %collective-permute-done.7.got_ref = bf16[16,120,768]{2,1,0:T(8,128)(2,1)S(1)} collective-permute-done((bf16[16,120,768]{2,1,0:T(8,128)(2,1)}, bf16[16,120,768]{2,1,0:T(8,128)(2,1)S(1)}, u32[]{:S(2)}, u32[]{:S(2)}) %collective-permute-start.7) | collective-permute-done | bytes 2949152 | tf_op jit(solution)/shard_map/ppermute | solution.py:858
  153.6 2.9 %first_turn.1 = (bf16[8,64,768]{2,1,0:T(8,128)(2,1)S(1)}, bf16[8,64,768]{2,1,0:T(8,128)(2,1)S(1)}, bf16[8,56,768]{2,1,0:T(8,128)(2,1)S(1)}, bf16[8,56,768]{2,1,0:T(8,128)(2,1)S(1)}) custom-call(s32[4]{0:T(128)S(1)} %copy-done.6, bf16[16,120,768]{2,1,0:T(8,128)(2,1)} %get-tuple-element.120.keep_ref, bf16[16,120,768]{2,1,0:T(8,128)(2,1)S(1)} %collective-permute-done.7.got_ref), custom_call_target="tpu_custom_call" | custom-call | tf_op jit(solution)/shard_map/first_turn/pallas_call | solution.py:800
  158.8 22.3 %attend_back.2 = (bf16[3,512,768]{2,1,0:T(8,128)(2,1)}, bf16[2,768,256]{2,1,0:T(8,128)(2,1)}) custom-call(bf16[512,768]{1,0:T(8,128)(2,1)} %get-tuple-element.103.refs_1_.refs_0_, bf16[512,768]{1,0:T(8,128)(2,1)} %get-tuple-element.104.refs_2_.refs_1_, bf16[512,768]{1,0:T(8,128)(2,1)} %get-tuple-element.105.refs_3_.refs_2_, ...), custom_call_target="tpu_custom_call" | custom-call | flops 26666665984 | bytes 12000000 | tf_op jit(solution)/shard_map/attend_back/pallas_call | solution.py:173
  183.9 12.6 %attend_back.3 = (bf16[3,512,768]{2,1,0:T(8,128)(2,1)}, bf16[2,768,256]{2,1,0:T(8,128)(2,1)}) custom-call(bf16[512,768]{1,0:T(8,128)(2,1)} %get-tuple-element.103.refs_1_.refs_0_, bf16[512,768]{1,0:T(8,128)(2,1)} %get-tuple-element.104.refs_2_.refs_1_, ...), custom_call_target="tpu_custom_call", output_to_operand_aliasing={{0}: (8, {}), {1}: (9, {})} | custom-call | flops 13333332992 | bytes 6000000 | tf_op jit(solution)/shard_map/attend_back/pallas_call | solution.py:173
  197.7 7.6 %project_back.1 = (bf16[16,88,768]{2,1,0:T(8,128)(2,1)S(1)}, bf16[16,88,768]{2,1,0:T(8,128)(2,1)S(1)}, bf16[1,120,768]{2,1,0:T(8,128)(2,1)S(1)}, bf16[1,120,768]...) custom-call(s32[4]{0:T(128)S(1)} %copy-done.6, ...), custom_call_target="tpu_custom_call" | custom-call | tf_op jit(solution)/shard_map/project_back/pallas_call | solution.py:691
  206.9 2.4 collective-permute-start.20
  214.3 4.3 %collective-permute-done.19 = bf16[1,120,768]{2,1,0:T(8,128)(2,1)S(1)} collective-permute-done((bf16[1,120,768]{2,1,0:T(8,128)(2,1)S(1)}, bf16[1,120,768]{2,1,0:T(8,128)(2,1)S(1)}, u32[]{:S(2)}, u32[]{:S(2)}) %collective-permute-start.19) | collective-permute-done | bytes 184352 | tf_op jit(solution)/shard_map/ppermute | solution.py:858
  218.6 2.5 collective-permute-start.21
  221.1 3.7 %token_grads.1 = f32[512,768]{1,0:T(8,128)} custom-call(f32[512,768]{1,0:T(8,128)S(1)} %copy-done.2, bf16[3,512,768]{2,1,0:T(8,128)(2,1)S(1)} %copy-done.1, bf16[3,32,24,768]{3,2,1,0:T(8,128)(2,1)S(1)} %copy-done), custom_call_target="tpu_custom_call" | custom-call | flops 2147483648 | bytes 10485760 | tf_op jit(solution)/shard_map/token_grads/pallas_call | solution.py:719
  225.1 3.7 %collective-permute-done.21 = bf16[1,120,768]{2,1,0:T(8,128)(2,1)S(1)} collective-permute-done((bf16[1,120,768]{2,1,0:T(8,128)(2,1)S(1)}, bf16[1,120,768]{2,1,0:T(8,128)(2,1)S(1)}, u32[]{:S(2)}, u32[]{:S(2)}) %collective-permute-start.21) | collective-permute-done | bytes 184352 | tf_op jit(solution)/shard_map/ppermute | solution.py:858
  229.5 10.9 %collective-permute-done.13.refs_1_ = bf16[4,88,768]{2,1,0:T(8,128)(2,1)S(1)} collective-permute-done((bf16[4,88,768]{2,1,0:T(8,128)(2,1)S(1)}, bf16[4,88,768]{2,1,0:T(8,128)(2,1)S(1)}, u32[]{:S(2)}, u32[]{:S(2)}) %collective-permute-start.13) | collective-permute-done | bytes 540704 | tf_op jit(solution)/shard_map/ppermute | solution.py:858
  242.9 2.4 collective-permute-start.17
  246.5 4.0 %reduce-scatter.2.cloned.1.call-done.refs_4_ = bf16[1,96,768]{2,1,0:T(8,128)(2,1)} async-done(((bf16[32,96,768]{2,1,0:T(8,128)(2,1)}), bf16[1,96,768]{2,1,0:T(8,128)(2,1)}) %reduce-scatter.2.cloned.1.call-update) | async-done | bytes 147472 | tf_op jit(solution)/shard_map/reduce_scatter | solution.py:854
  250.5 6.2 %collective-permute-done.17.refs_2_ = bf16[1,88,768]{2,1,0:T(8,128)(2,1)S(1)} collective-permute-done((bf16[1,88,768]{2,1,0:T(8,128)(2,1)S(1)}, bf16[1,88,768]{2,1,0:T(8,128)(2,1)S(1)}, u32[]{:S(2)}, u32[]{:S(2)}) %collective-permute-start.17) | collective-permute-done | bytes 135200 | tf_op jit(solution)/shard_map/ppermute | solution.py:858
  (80 shorter events, 32.7 us)
Async XLA Ops:
  7.2 101.9 %all-gather.3.cloned.1.call-start = ((), (), s32[]{:S(2)}) async-start(), calls=%async_computation.2 | async-start | bytes 10948608 | tf_op jit(solution)/shard_map/all_gather | solution.py:850
  9.2 241.3 %reduce-scatter.2.cloned.1.call-start = ((), (), s32[]{:S(2)}) async-start(), calls=%async_computation.1 | async-start | bytes 4866048 | tf_op jit(solution)/shard_map/reduce_scatter | solution.py:854
  9.3 9.8 %collective-permute-start.2 = (bf16[1,88,768]{2,1,0:T(8,128)(2,1)}, bf16[1,88,768]{2,1,0:T(8,128)(2,1)S(1)}, u32[]{:S(2)}, u32[]{:S(2)}) collective-permute-start(bf16[1,88,768]{2,1,0:T(8,128)(2,1)} %bitcast.32), channel_id=1, source_target_pairs={{0,24},{1,25},{2,26},{3,27},{4,28},{5,29},{6,30},{7,31},{8,16},{9,... | collective-permute-start | bytes 405512 | tf_op jit(solution)/shard_map/ppermute | solution.py:858
  14.4 11.7 %collective-permute-start.1 = (bf16[1,88,768]{2,1,0:T(8,128)(2,1)}, bf16[1,88,768]{2,1,0:T(8,128)(2,1)S(1)}, u32[]{:S(2)}, u32[]{:S(2)}) collective-permute-start(bf16[1,88,768]{2,1,0:T(8,128)(2,1)} %bitcast.33), channel_id=1, source_target_pairs={{0,16},{1,17},{2,18},{3,19},{4,20},{5,21},{6,22},{7,23},{8,24},{9,... | collective-permute-start | bytes 405512 | tf_op jit(solution)/shard_map/ppermute | solution.py:858
  14.4 11.7 %collective-permute-start = (bf16[1,88,768]{2,1,0:T(8,128)(2,1)}, bf16[1,88,768]{2,1,0:T(8,128)(2,1)S(1)}, u32[]{:S(2)}, u32[]{:S(2)}) collective-permute-start(bf16[1,88,768]{2,1,0:T(8,128)(2,1)} %bitcast.34), channel_id=1, source_target_pairs={{0,8},{1,9},{2,10},{3,11},{4,12},{5,13},{6,14},{7,15},{8,0},{9,1},... | collective-permute-start | bytes 405512 | tf_op jit(solution)/shard_map/ppermute | solution.py:858
  27.1 21.9 %collective-permute-start.4 = (bf16[4,88,768]{2,1,0:T(8,128)(2,1)S(1)}, bf16[4,88,768]{2,1,0:T(8,128)(2,1)S(1)}, u32[]{:S(2)}, u32[]{:S(2)}) collective-permute-start(bf16[4,88,768]{2,1,0:T(8,128)(2,1)S(1)} %pad_maximum_fusion), channel_id=1, source_target_pairs={{0,4},{1,5},{2,6},{3,7},{4,0},{5,1},{6,2},{7,3},{8,12},{9,13},{10,... | collective-permute-start | bytes 1622024 | tf_op jit(solution)/shard_map/ppermute | solution.py:858
  28.7 20.3 %collective-permute-start.3 = (bf16[4,88,768]{2,1,0:T(8,128)(2,1)S(1)}, bf16[4,88,768]{2,1,0:T(8,128)(2,1)S(1)}, u32[]{:S(2)}, u32[]{:S(2)}) collective-permute-start(bf16[4,88,768]{2,1,0:T(8,128)(2,1)S(1)} %pad_maximum_fusion), channel_id=1, source_target_pairs={{0,2},{1,3},{2,0},{3,1},{4,6},{5,7},{6,4},{7,5},{8,10},{9,11},{10,... | collective-permute-start | bytes 1622024 | tf_op jit(solution)/shard_map/ppermute | solution.py:858
  31.1 31.4 %collective-permute-start.5 = (bf16[4,88,768]{2,1,0:T(8,128)(2,1)S(1)}, bf16[4,88,768]{2,1,0:T(8,128)(2,1)S(1)}, u32[]{:S(2)}, u32[]{:S(2)}) collective-permute-start(bf16[4,88,768]{2,1,0:T(8,128)(2,1)S(1)} %pad_maximum_fusion), channel_id=1, source_target_pairs={{0,6},{1,7},{2,4},{3,5},{4,2},{5,3},{6,0},{7,1},{8,14},{9,15},{10,... | collective-permute-start | bytes 1622024 | tf_op jit(solution)/shard_map/ppermute | solution.py:858
  62.6 4.5 %collective-permute-start.6 = (bf16[16,88,768]{2,1,0:T(8,128)(2,1)S(1)}, bf16[16,88,768]{2,1,0:T(8,128)(2,1)}, u32[]{:S(2)}, u32[]{:S(2)}) collective-permute-start(bf16[16,88,768]{2,1,0:T(8,128)(2,1)S(1)} %constant_dynamic-update-slice_fusion.refs_1_.refs_3_.refs_5_.refs_7_.refs_9_), channel_id=1, source_target_pairs={{0,1},{1,0},{2,3},{3,2},{4,5},{5,4},{6,7},{7,6},{8,9},{9,8},{10,11... | collective-permute-start | bytes 6488072 | tf_op jit(solution)/shard_map/ppermute | solution.py:858
  148.0 5.7 %collective-permute-start.7 = (bf16[16,120,768]{2,1,0:T(8,128)(2,1)}, bf16[16,120,768]{2,1,0:T(8,128)(2,1)S(1)}, u32[]{:S(2)}, u32[]{:S(2)}) collective-permute-start(bf16[16,120,768]{2,1,0:T(8,128)(2,1)} %get-tuple-element.121), channel_id=1, source_target_pairs={{0,1},{1,0},{2,3},{3,2},{4,5},{5,4},{6,7},{7,6},{8,9},{9,8},{10,11... | collective-permute-start | bytes 8847368 | tf_op jit(solution)/shard_map/ppermute | solution.py:858
  156.6 24.5 %collective-permute-start.9 = (bf16[8,56,768]{2,1,0:T(8,128)(2,1)S(1)}, bf16[8,56,768]{2,1,0:T(8,128)(2,1)S(1)}, u32[]{:S(2)}, u32[]{:S(2)}) collective-permute-start(bf16[8,56,768]{2,1,0:T(8,128)(2,1)S(1)} %get-tuple-element.125), channel_id=1, source_target_pairs={{0,4},{1,5},{2,6},{3,7},{4,0},{5,1},{6,2},{7,3},{8,12},{9,13},{10,... | collective-permute-start | bytes 2064392 | tf_op jit(solution)/shard_map/ppermute | solution.py:858
  158.3 22.8 %collective-permute-start.8 = (bf16[8,64,768]{2,1,0:T(8,128)(2,1)S(1)}, bf16[8,64,768]{2,1,0:T(8,128)(2,1)S(1)}, u32[]{:S(2)}, u32[]{:S(2)}) collective-permute-start(bf16[8,64,768]{2,1,0:T(8,128)(2,1)S(1)} %get-tuple-element.124), channel_id=1, source_target_pairs={{0,2},{1,3},{2,0},{3,1},{4,6},{5,7},{6,4},{7,5},{8,10},{9,11},{10,... | collective-permute-start | bytes 2359304 | tf_op jit(solution)/shard_map/ppermute | solution.py:858
  182.0 14.6 %collective-permute-start.11 = (bf16[4,56,768]{2,1,0:T(8,128)(2,1)S(1)}, bf16[4,56,768]{2,1,0:T(8,128)(2,1)S(1)}, u32[]{:S(2)}, u32[]{:S(2)}) collective-permute-start(bf16[4,56,768]{2,1,0:T(8,128)(2,1)S(1)} %get-tuple-element.135), channel_id=1, source_target_pairs={{0,2},{1,3},{2,0},{3,1},{4,6},{5,7},{6,4},{7,5},{8,10},{9,11},{10,... | collective-permute-start | bytes 1032200 | tf_op jit(solution)/shard_map/ppermute | solution.py:858
  183.5 14.1 %collective-permute-start.10 = (bf16[4,64,768]{2,1,0:T(8,128)(2,1)S(1)}, bf16[4,64,768]{2,1,0:T(8,128)(2,1)S(1)}, u32[]{:S(2)}, u32[]{:S(2)}) collective-permute-start(bf16[4,64,768]{2,1,0:T(8,128)(2,1)S(1)} %get-tuple-element.134), channel_id=1, source_target_pairs={{0,4},{1,5},{2,6},{3,7},{4,0},{5,1},{6,2},{7,3},{8,12},{9,13},{10,... | collective-permute-start | bytes 1179656 | tf_op jit(solution)/shard_map/ppermute | solution.py:858
  205.3 4.3 %collective-permute-start.12 = (bf16[16,88,768]{2,1,0:T(8,128)(2,1)S(1)}, bf16[16,88,768]{2,1,0:T(8,128)(2,1)S(1)}, u32[]{:S(2)}, u32[]{:S(2)}) collective-permute-start(bf16[16,88,768]{2,1,0:T(8,128)(2,1)S(1)} %get-tuple-element.146), channel_id=1, source_target_pairs={{0,1},{1,0},{2,3},{3,2},{4,5},{5,4},{6,7},{7,6},{8,9},{9,8},{10,11... | collective-permute-start | bytes 6488072 | tf_op jit(solution)/shard_map/ppermute | solution.py:858
  205.4 13.2 %collective-permute-start.19 = (bf16[1,120,768]{2,1,0:T(8,128)(2,1)S(1)}, bf16[1,120,768]{2,1,0:T(8,128)(2,1)S(1)}, u32[]{:S(2)}, u32[]{:S(2)}) collective-permute-start(bf16[1,120,768]{2,1,0:T(8,128)(2,1)S(1)} %get-tuple-element.167), channel_id=1, source_target_pairs={{0,8},{1,9},{2,10},{3,11},{4,12},{5,13},{6,14},{7,15},{8,0},{9,1},... | collective-permute-start | bytes 552968 | tf_op jit(solution)/shard_map/ppermute | solution.py:858
  206.9 18.1 %collective-permute-start.20 = (bf16[1,120,768]{2,1,0:T(8,128)(2,1)S(1)}, bf16[1,120,768]{2,1,0:T(8,128)(2,1)S(1)}, u32[]{:S(2)}, u32[]{:S(2)}) collective-permute-start(bf16[1,120,768]{2,1,0:T(8,128)(2,1)S(1)} %get-tuple-element.168), channel_id=1, source_target_pairs={{0,16},{1,17},{2,18},{3,19},{4,20},{5,21},{6,22},{7,23},{8,24},{9,... | collective-permute-start | bytes 552968 | tf_op jit(solution)/shard_map/ppermute | solution.py:858
  210.8 29.7 %collective-permute-start.13 = (bf16[4,88,768]{2,1,0:T(8,128)(2,1)S(1)}, bf16[4,88,768]{2,1,0:T(8,128)(2,1)S(1)}, u32[]{:S(2)}, u32[]{:S(2)}) collective-permute-start(bf16[4,88,768]{2,1,0:T(8,128)(2,1)S(1)} %get-tuple-element.147), channel_id=1, source_target_pairs={{0,2},{1,3},{2,0},{3,1},{4,6},{5,7},{6,4},{7,5},{8,10},{9,11},{10,... | collective-permute-start | bytes 1622024 | tf_op jit(solution)/shard_map/ppermute | solution.py:858
  212.3 28.2 %collective-permute-start.14 = (bf16[4,88,768]{2,1,0:T(8,128)(2,1)S(1)}, bf16[4,88,768]{2,1,0:T(8,128)(2,1)S(1)}, u32[]{:S(2)}, u32[]{:S(2)}) collective-permute-start(bf16[4,88,768]{2,1,0:T(8,128)(2,1)S(1)} %get-tuple-element.148), channel_id=1, source_target_pairs={{0,4},{1,5},{2,6},{3,7},{4,0},{5,1},{6,2},{7,3},{8,12},{9,13},{10,... | collective-permute-start | bytes 1622024 | tf_op jit(solution)/shard_map/ppermute | solution.py:858
  212.9 27.6 %collective-permute-start.15 = (bf16[4,88,768]{2,1,0:T(8,128)(2,1)S(1)}, bf16[4,88,768]{2,1,0:T(8,128)(2,1)S(1)}, u32[]{:S(2)}, u32[]{:S(2)}) collective-permute-start(bf16[4,88,768]{2,1,0:T(8,128)(2,1)S(1)} %get-tuple-element.149), channel_id=1, source_target_pairs={{0,6},{1,7},{2,4},{3,5},{4,2},{5,3},{6,0},{7,1},{8,14},{9,15},{10,... | collective-permute-start | bytes 1622024 | tf_op jit(solution)/shard_map/ppermute | solution.py:858
  218.6 10.2 %collective-permute-start.21 = (bf16[1,120,768]{2,1,0:T(8,128)(2,1)S(1)}, bf16[1,120,768]{2,1,0:T(8,128)(2,1)S(1)}, u32[]{:S(2)}, u32[]{:S(2)}) collective-permute-start(bf16[1,120,768]{2,1,0:T(8,128)(2,1)S(1)} %get-tuple-element.170), channel_id=1, source_target_pairs={{0,24},{1,25},{2,26},{3,27},{4,28},{5,29},{6,30},{7,31},{8,16},{9,... | collective-permute-start | bytes 552968 | tf_op jit(solution)/shard_map/ppermute | solution.py:858
  241.3 9.2 %collective-permute-start.16 = (bf16[1,88,768]{2,1,0:T(8,128)(2,1)S(1)}, bf16[1,88,768]{2,1,0:T(8,128)(2,1)S(1)}, u32[]{:S(2)}, u32[]{:S(2)}) collective-permute-start(bf16[1,88,768]{2,1,0:T(8,128)(2,1)S(1)} %get-tuple-element.156), channel_id=1, source_target_pairs={{0,8},{1,9},{2,10},{3,11},{4,12},{5,13},{6,14},{7,15},{8,0},{9,1},... | collective-permute-start | bytes 405512 | tf_op jit(solution)/shard_map/ppermute | solution.py:858
  242.9 13.9 %collective-permute-start.17 = (bf16[1,88,768]{2,1,0:T(8,128)(2,1)S(1)}, bf16[1,88,768]{2,1,0:T(8,128)(2,1)S(1)}, u32[]{:S(2)}, u32[]{:S(2)}) collective-permute-start(bf16[1,88,768]{2,1,0:T(8,128)(2,1)S(1)} %get-tuple-element.157), channel_id=1, source_target_pairs={{0,16},{1,17},{2,18},{3,19},{4,20},{5,21},{6,22},{7,23},{8,24},{9,... | collective-permute-start | bytes 405512 | tf_op jit(solution)/shard_map/ppermute | solution.py:858
  245.3 11.5 %collective-permute-start.18 = (bf16[1,88,768]{2,1,0:T(8,128)(2,1)S(1)}, bf16[1,88,768]{2,1,0:T(8,128)(2,1)S(1)}, u32[]{:S(2)}, u32[]{:S(2)}) collective-permute-start(bf16[1,88,768]{2,1,0:T(8,128)(2,1)S(1)} %get-tuple-element.158), channel_id=1, source_target_pairs={{0,24},{1,25},{2,26},{3,27},{4,28},{5,29},{6,30},{7,31},{8,16},{9,... | collective-permute-start | bytes 405512 | tf_op jit(solution)/shard_map/ppermute | solution.py:858
  (11 other events, 142.6 us)
Sparse Core Ops, SparseCore 0:
  10.9 98.0 all-gather.2
  128.6 121.8 reduce-scatter.1

commit v3 on v2

--- a/solution.py
+++ b/solution.py
@@ -490,9 +490,9 @@
 
 
 def feed_back_kernel(where_ref, vecs_ref, vg_in_ref, og_hbm, low_hbm, slope_hbm, second_hbm, n1_hbm, inv_hbm,
-                     ctx_hbm, packed_hbm, keep_hbm, send_hbm, cg_hbm, fg_hbm, vg_ref,
-                     og, low, slope, acc, n1, inv, ctx, wo, wi, w2, turned, cg, fg, keep, send,
-                     fetch, chunk_fetch, flush, keep_flush, *, fan):
+                     ctx_hbm, packed_hbm, keep_ref, send_ref, cg_hbm, fg_hbm, vg_ref,
+                     og, low, slope, acc, n1, inv, ctx, wo, wi, w2, turned, cg, fg,
+                     fetch, chunk_fetch, flush, *, fan):
     rows, width = ctx.shape
     part = width // STRIPES
     own = where_ref[1]
@@ -522,20 +522,9 @@
     ins[0].wait()
     ins[2].wait()
 
-    def keep_copies(f):
+    def leave(f, grad):
         place = pl.ds(pl.multiple_of(f * part, 8), part)
-        return (copy(keep.at[f % 2], keep_hbm.at[:, place, :], keep_flush.at[0, f % 2]),
-                copy(send.at[f % 2], send_hbm.at[:, place, :], keep_flush.at[1, f % 2]))
-
-    def leave(f, grad):
-        @pl.when(f >= 2)
-        def _():
-            for one in keep_copies(f - 2):
-                one.wait()
-
-        halves_to(keep.at[f % 2], send.at[f % 2], grad, own)
-        for one in keep_copies(f):
-            one.start()
+        halves_to(keep_ref.at[:, place], send_ref.at[:, place], grad, own)
 
     def backward(f, carry):
         for one in chunk_copies(f):
@@ -564,9 +553,6 @@
     vg_ref[6:7, :] = column(ag.astype(F32))
     for one in outs:
         one.wait()
-    for f in (fan - 1, fan):
-        for one in keep_copies(f):
-            one.wait()
 
 
 def feed_back(where, vecs, vg, og, low, slope, second, n1, inv, ctx, packed, fan):
@@ -581,18 +567,18 @@
     return pl.pallas_call(
         lambda *refs: feed_back_kernel(*refs, fan=fan),
         in_specs=[pl.BlockSpec(memory_space=pltpu.SMEM), vmem, vmem] + [hbm] * 8,
-        out_specs=[hbm] * 4 + [vmem],
-        out_shape=[half, half, shape((rows, width), BF), shape((rows, width), F32), shape(vg.shape, F32)],
+        out_specs=[vmem, vmem, hbm, hbm, vmem],
+        out_shape=[pltpu.VMEM(half.shape, half.dtype)] * 2 + [shape((rows, width), BF), shape((rows, width), F32), shape(vg.shape, F32)],
         scratch_shapes=[thin, thin, pltpu.VMEM((fan, rows, width), BF), wide, wide,
                         pltpu.VMEM((rows, 128), F32), thin, pltpu.VMEM((STRIPES, part, width), BF),
                         pltpu.VMEM((fan, STRIPES, part, width), BF),
                         pltpu.VMEM((fan, STRIPES // fan, part * fan, width), BF),
                         pltpu.VMEM((width, rows), BF), thin, wide]
-        + [pltpu.VMEM((2, STRIPES // 2, part, width), BF)] * 2
-        + [sem((7,)), sem((3, fan)), sem((2,)), sem((2, 2))],
-        compiler_params=big(),
+        + [sem((7,)), sem((3, fan)), sem((2,))],
+        compiler_params=big(44),
         name="feed_back",
-    )(where, vecs, vg, og, low, slope, second, n1, inv, ctx, packed)
+    )(where, vecs, vg, *[pltpu.with_memory_space_constraint(a, pltpu.HBM)
+                         for a in (og, low, slope, second, n1, inv, ctx, packed)])
 
 
 def cut(row, mine, marks):
@@ -979,11 +965,11 @@
         if direct:
             inner = Scatter(where, count, pltpu.HBM)
             inner_got = tie(xor_permute(inner_send, 1, count), vec)
-            inner_keep = pltpu.with_memory_space_constraint(inner_keep, pltpu.HBM)
+            inner_keep = in_vmem(inner_keep)
             a_keep, a_send, b_keep, b_send = first_turn(where, inner_keep, in_vmem(inner_got), 64)
             a_got, b_got = xor_permute(a_send, 2, count), xor_permute(b_send, 4, count)
             context_grad = tie(context_grad, (a_send, b_send))
-        most = width // 128 * 2 // 3
+        most = width // 128 // 2
         back = lambda dc, first, pairs, before: attend_back(
             q, k, v, kr, qr, dc, probs, onehot, first, pairs, before
         )

time: 266 us -> 264 us (level)
  waiting for transfers between devices: 81.3 us -> 84.5 us
  Pallas kernels: 132 us -> 129 us
    ppermute x22, waiting for transfers between devices: 72.8 us -> 77.2 us  [xor_permute(): return lax.ppermute(block, AXES, [(d, d ^ mask) for d in range(count)])]
  transfers between devices with their start and end apart: 24 -> 24, of which waited for: 16 -> 14; matrix products, arithmetic and copies ran while one was open for 2% -> 2% of each run, Pallas kernels for 41% -> 41%
where the time goes in v3:
time: 264 us; the launch traced here: 263 us
  Pallas kernels  129 us (49%)
  waiting for transfers between devices  84.5 us (32%)
  starting transfers between devices  26.2 us (10%)
  between operations  15.7 us (6%)
  local copies, waits for them, and re-layouts  5.42 us (2%)
    ppermute x22, waiting for transfers between devices, xor_permute(): return lax.ppermute(block, AXES, [(d, d ^ mask) for d in range(count)])  77.2 us
    pallas_call x2, Pallas kernels, attend_back(): pl.pallas_call(lambda *refs: attend_back_kernel(*refs, rows=rows, tile=ro...  35.4 us
    pallas_call x1, Pallas kernels, attend(): pl.pallas_call(lambda *refs: attend_kernel(*refs, rows=rows, tile=rows //...  27.5 us
    ppermute x22, starting transfers between devices, xor_permute(): return lax.ppermute(block, AXES, [(d, d ^ mask) for d in range(count)])  26.1 us
    pallas_call x1, Pallas kernels, feed_forward(): pl.pallas_call(lambda *refs: feed_forward_kernel(*refs, fan=fan), in_spec...  19.4 us
    pallas_call x1, Pallas kernels, feed_back(): pl.pallas_call(lambda *refs: feed_back_kernel(*refs, fan=fan), in_specs=[...  17.6 us
    pallas_call x1, Pallas kernels, project_all(): pl.pallas_call(lambda *refs: project_kernel(*refs, fan=fan), grid=(width...  10.2 us
    pallas_call x1, Pallas kernels, project_back(): pl.pallas_call(lambda *refs: project_back_kernel(*refs, fan=fan, hops=len...  7.45 us
  transfers between devices with their start and end apart: 24, of which 14 were waited for; matrix products, arithmetic and copies ran while one was open for 2% of the time, Pallas kernels for 41%

profile of v3, /device:TPU:0, one launch (start us, length us, event | category | flops | bytes accessed | tf_op | source)
XLA Modules:
  0.0 263.2 jit_solution(11206551862752683995)
XLA Ops:
  9.3 5.1 %collective-permute-start.2 = (bf16[1,88,768]{2,1,0:T(8,128)(2,1)}, bf16[1,88,768]{2,1,0:T(8,128)(2,1)S(1)}, u32[]{:S(2)}, u32[]{:S(2)}) collective-permute-start(bf16[1,88,768]{2,1,0:T(8,128)(2,1)} %bitcast.32), channel_id=1, source_target_pairs={{0,24},{1,25},{2,26},{3,27},{4,28},{5,29},{6,30},{7,31},{8,16},{9,... | collective-permute-start | bytes 405512 | tf_op jit(solution)/shard_map/ppermute | solution.py:844
  15.1 4.1 %collective-permute-done.2 = bf16[1,88,768]{2,1,0:T(8,128)(2,1)S(1)} collective-permute-done((bf16[1,88,768]{2,1,0:T(8,128)(2,1)}, bf16[1,88,768]{2,1,0:T(8,128)(2,1)S(1)}, u32[]{:S(2)}, u32[]{:S(2)}) %collective-permute-start.2) | collective-permute-done | bytes 135200 | tf_op jit(solution)/shard_map/ppermute | solution.py:844
  19.1 7.0 %collective-permute-done.1 = bf16[1,88,768]{2,1,0:T(8,128)(2,1)S(1)} collective-permute-done((bf16[1,88,768]{2,1,0:T(8,128)(2,1)}, bf16[1,88,768]{2,1,0:T(8,128)(2,1)S(1)}, u32[]{:S(2)}, u32[]{:S(2)}) %collective-permute-start.1) | collective-permute-done | bytes 135200 | tf_op jit(solution)/shard_map/ppermute | solution.py:844
  31.8 17.3 %collective-permute-done.3 = bf16[4,88,768]{2,1,0:T(8,128)(2,1)S(1)} collective-permute-done((bf16[4,88,768]{2,1,0:T(8,128)(2,1)S(1)}, bf16[4,88,768]{2,1,0:T(8,128)(2,1)S(1)}, u32[]{:S(2)}, u32[]{:S(2)}) %collective-permute-start.3) | collective-permute-done | bytes 540704 | tf_op jit(solution)/shard_map/ppermute | solution.py:844
  49.2 13.4 %collective-permute-done.5 = bf16[4,88,768]{2,1,0:T(8,128)(2,1)S(1)} collective-permute-done((bf16[4,88,768]{2,1,0:T(8,128)(2,1)S(1)}, bf16[4,88,768]{2,1,0:T(8,128)(2,1)S(1)}, u32[]{:S(2)}, u32[]{:S(2)}) %collective-permute-start.5) | collective-permute-done | bytes 540704 | tf_op jit(solution)/shard_map/ppermute | solution.py:844
  67.0 10.2 %project.1 = (bf16[512,768]{1,0:T(8,128)(2,1)}, bf16[512,768]{1,0:T(8,128)(2,1)}, bf16[512,768]{1,0:T(8,128)(2,1)}, bf16[1024,768]{1,0:T(8,128)(2,1)}, bf16[1024...) custom-call(s32[4]{0:T(128)} %pad_add_fusion.refs_0_.where_ref, ...), custom_call_target="tpu_custom_call" | custom-call | flops 4294967296 | bytes 12582912 | tf_op jit(solution)/shard_map/project/pallas_call | solution.py:323
  77.2 27.5 %attend.1 = (bf16[512,768]{1,0:T(8,128)(2,1)}, bf16[12,512,512]{2,1,0:T(8,128)(2,1)}) custom-call(s32[1]{0:T(128)} %bitcast.7.refs_0_, bf16[512,768]{1,0:T(8,128)(2,1)} %get-tuple-element.103.refs_1_.refs_0_, bf16[512,768]{1,0:T(8,128)(2,1)} %get-tuple-element.104.refs_2_.refs_1_, bf16[512,768]{1,0:T(8,128)(2,1)} %get-tuple-element.105.refs_3_.refs_2_, ...), custom_call_target="tpu_custom_call" | custom-call | flops 26843545600 | bytes 12582912 | tf_op jit(solution)/shard_map/attend/pallas_call | solution.py:81
  104.7 4.4 %all-gather.3.cloned.1.call-done = bf16[6912,768]{1,0:T(8,128)(2,1)} async-done(((bf16[216,768]{1,0:T(8,128)(2,1)}), bf16[6912,768]{1,0:T(8,128)(2,1)}) %all-gather.3.cloned.1.call-update) | async-done | bytes 10616848 | tf_op jit(solution)/shard_map/all_gather | solution.py:836
  109.1 19.4 %feed_forward.1 = (bf16[512,768]{1,0:T(8,128)(2,1)}, bf16[3072,768]{1,0:T(8,128)(2,1)}, bf16[4,512,768]{2,1,0:T(8,128)(2,1)}, bf16[512,768]{1,0:T(8,128)(2,1)}, ...) custom-call(f32[16,768]{1,0:T(8,128)} %get-tuple-element.102.refs_0_, ...), custom_call_target="tpu_custom_call" | custom-call | tf_op jit(solution)/shard_map/feed_forward/pallas_call | solution.py:474
  129.3 17.6 %feed_back.1 = (bf16[16,120,768]{2,1,0:T(8,128)(2,1)S(1)}, bf16[16,120,768]{2,1,0:T(8,128)(2,1)S(1)}, bf16[512,768]{1,0:T(8,128)(2,1)S(1)}, f32[512,768]{1,0:T(8,128)S(1)}, f32[16,768]{1,0:T(8,128)S(1)}) custom-call(s32[4]{0:T(128)S(1)} %copy-done.7, f32[16,768]{1,0:T(8,128)S(1)} %copy-done.4, f32[16,768]{1,0:T(8,128)S(1)} %copy-done.6, ...), custom_call_target="tpu_custom_call" | custom-call | tf_op jit(solution)/shard_map/feed_back/pallas_call | solution.py:567
  148.0 4.3 %collective-permute-done.7.got_ref = bf16[16,120,768]{2,1,0:T(8,128)(2,1)S(1)} collective-permute-done((bf16[16,120,768]{2,1,0:T(8,128)(2,1)S(1)}, bf16[16,120,768]{2,1,0:T(8,128)(2,1)S(1)}, u32[]{:S(2)}, u32[]{:S(2)}) %collective-permute-start.7) | collective-permute-done | bytes 2949152 | tf_op jit(solution)/shard_map/ppermute | solution.py:844
  155.8 17.4 %attend_back.2 = (bf16[3,512,768]{2,1,0:T(8,128)(2,1)}, bf16[2,768,256]{2,1,0:T(8,128)(2,1)}) custom-call(bf16[512,768]{1,0:T(8,128)(2,1)} %get-tuple-element.103.refs_1_.refs_0_, bf16[512,768]{1,0:T(8,128)(2,1)} %get-tuple-element.104.refs_2_.refs_1_, bf16[512,768]{1,0:T(8,128)(2,1)} %get-tuple-element.105.refs_3_.refs_2_, ...), custom_call_target="tpu_custom_call" | custom-call | flops 20000000000 | bytes 9000000 | tf_op jit(solution)/shard_map/attend_back/pallas_call | solution.py:173
  177.8 18.0 %attend_back.3 = (bf16[3,512,768]{2,1,0:T(8,128)(2,1)}, bf16[2,768,256]{2,1,0:T(8,128)(2,1)}) custom-call(bf16[512,768]{1,0:T(8,128)(2,1)} %get-tuple-element.103.refs_1_.refs_0_, bf16[512,768]{1,0:T(8,128)(2,1)} %get-tuple-element.104.refs_2_.refs_1_, ...), custom_call_target="tpu_custom_call", output_to_operand_aliasing={{0}: (8, {}), {1}: (9, {})} | custom-call | flops 20000000000 | bytes 9000000 | tf_op jit(solution)/shard_map/attend_back/pallas_call | solution.py:173
  195.9 7.4 %project_back.1 = (bf16[16,88,768]{2,1,0:T(8,128)(2,1)S(1)}, bf16[16,88,768]{2,1,0:T(8,128)(2,1)S(1)}, bf16[1,120,768]{2,1,0:T(8,128)(2,1)S(1)}, bf16[1,120,768]...) custom-call(s32[4]{0:T(128)S(1)} %copy-done.7, ...), custom_call_target="tpu_custom_call" | custom-call | tf_op jit(solution)/shard_map/project_back/pallas_call | solution.py:677
  205.1 2.6 collective-permute-done.12.refs_2_
  210.2 2.1 collective-permute-start.15
  212.3 2.5 collective-permute-done.19
  214.8 2.3 collective-permute-start.21
  217.1 3.7 %token_grads.1 = f32[512,768]{1,0:T(8,128)} custom-call(f32[512,768]{1,0:T(8,128)S(1)} %get-tuple-element.118.fg_ref, bf16[3,512,768]{2,1,0:T(8,128)(2,1)S(1)} %copy-done.1, bf16[3,32,24,768]{3,2,1,0:T(8,128)(2,1)S(1)} %copy-done), custom_call_target="tpu_custom_call" | custom-call | flops 2147483648 | bytes 10485760 | tf_op jit(solution)/shard_map/token_grads/pallas_call | solution.py:705
  220.8 3.5 %collective-permute-done.20 = bf16[1,120,768]{2,1,0:T(8,128)(2,1)S(1)} collective-permute-done((bf16[1,120,768]{2,1,0:T(8,128)(2,1)S(1)}, bf16[1,120,768]{2,1,0:T(8,128)(2,1)S(1)}, u32[]{:S(2)}, u32[]{:S(2)}) %collective-permute-start.20) | collective-permute-done | bytes 184352 | tf_op jit(solution)/shard_map/ppermute | solution.py:844
  225.1 14.1 %collective-permute-done.13.refs_1_ = bf16[4,88,768]{2,1,0:T(8,128)(2,1)S(1)} collective-permute-done((bf16[4,88,768]{2,1,0:T(8,128)(2,1)S(1)}, bf16[4,88,768]{2,1,0:T(8,128)(2,1)S(1)}, u32[]{:S(2)}, u32[]{:S(2)}) %collective-permute-start.13) | collective-permute-done | bytes 540704 | tf_op jit(solution)/shard_map/ppermute | solution.py:844
  241.9 2.5 collective-permute-start.18
  245.2 2.9 %reduce-scatter.2.cloned.1.call-done.refs_4_ = bf16[1,96,768]{2,1,0:T(8,128)(2,1)} async-done(((bf16[32,96,768]{2,1,0:T(8,128)(2,1)}), bf16[1,96,768]{2,1,0:T(8,128)(2,1)}) %reduce-scatter.2.cloned.1.call-update) | async-done | bytes 147472 | tf_op jit(solution)/shard_map/reduce_scatter | solution.py:840
  248.1 6.4 %collective-permute-done.17.refs_2_ = bf16[1,88,768]{2,1,0:T(8,128)(2,1)S(1)} collective-permute-done((bf16[1,88,768]{2,1,0:T(8,128)(2,1)S(1)}, bf16[1,88,768]{2,1,0:T(8,128)(2,1)S(1)}, u32[]{:S(2)}, u32[]{:S(2)}) %collective-permute-start.17) | collective-permute-done | bytes 135200 | tf_op jit(solution)/shard_map/ppermute | solution.py:844
  (82 shorter events, 31.8 us)
Async XLA Ops:
  7.2 101.9 %all-gather.3.cloned.1.call-start = ((), (), s32[]{:S(2)}) async-start(), calls=%async_computation.2 | async-start | bytes 10948608 | tf_op jit(solution)/shard_map/all_gather | solution.py:836
  9.3 238.9 %reduce-scatter.2.cloned.1.call-start = ((), (), s32[]{:S(2)}) async-start(), calls=%async_computation.1 | async-start | bytes 4866048 | tf_op jit(solution)/shard_map/reduce_scatter | solution.py:840
  9.3 9.8 %collective-permute-start.2 = (bf16[1,88,768]{2,1,0:T(8,128)(2,1)}, bf16[1,88,768]{2,1,0:T(8,128)(2,1)S(1)}, u32[]{:S(2)}, u32[]{:S(2)}) collective-permute-start(bf16[1,88,768]{2,1,0:T(8,128)(2,1)} %bitcast.32), channel_id=1, source_target_pairs={{0,24},{1,25},{2,26},{3,27},{4,28},{5,29},{6,30},{7,31},{8,16},{9,... | collective-permute-start | bytes 405512 | tf_op jit(solution)/shard_map/ppermute | solution.py:844
  14.4 11.7 %collective-permute-start.1 = (bf16[1,88,768]{2,1,0:T(8,128)(2,1)}, bf16[1,88,768]{2,1,0:T(8,128)(2,1)S(1)}, u32[]{:S(2)}, u32[]{:S(2)}) collective-permute-start(bf16[1,88,768]{2,1,0:T(8,128)(2,1)} %bitcast.33), channel_id=1, source_target_pairs={{0,16},{1,17},{2,18},{3,19},{4,20},{5,21},{6,22},{7,23},{8,24},{9,... | collective-permute-start | bytes 405512 | tf_op jit(solution)/shard_map/ppermute | solution.py:844
  14.4 11.7 %collective-permute-start = (bf16[1,88,768]{2,1,0:T(8,128)(2,1)}, bf16[1,88,768]{2,1,0:T(8,128)(2,1)S(1)}, u32[]{:S(2)}, u32[]{:S(2)}) collective-permute-start(bf16[1,88,768]{2,1,0:T(8,128)(2,1)} %bitcast.34), channel_id=1, source_target_pairs={{0,8},{1,9},{2,10},{3,11},{4,12},{5,13},{6,14},{7,15},{8,0},{9,1},... | collective-permute-start | bytes 405512 | tf_op jit(solution)/shard_map/ppermute | solution.py:844
  27.1 22.0 %collective-permute-start.4 = (bf16[4,88,768]{2,1,0:T(8,128)(2,1)S(1)}, bf16[4,88,768]{2,1,0:T(8,128)(2,1)S(1)}, u32[]{:S(2)}, u32[]{:S(2)}) collective-permute-start(bf16[4,88,768]{2,1,0:T(8,128)(2,1)S(1)} %pad_maximum_fusion), channel_id=1, source_target_pairs={{0,4},{1,5},{2,6},{3,7},{4,0},{5,1},{6,2},{7,3},{8,12},{9,13},{10,... | collective-permute-start | bytes 1622024 | tf_op jit(solution)/shard_map/ppermute | solution.py:844
  28.7 20.4 %collective-permute-start.3 = (bf16[4,88,768]{2,1,0:T(8,128)(2,1)S(1)}, bf16[4,88,768]{2,1,0:T(8,128)(2,1)S(1)}, u32[]{:S(2)}, u32[]{:S(2)}) collective-permute-start(bf16[4,88,768]{2,1,0:T(8,128)(2,1)S(1)} %pad_maximum_fusion), channel_id=1, source_target_pairs={{0,2},{1,3},{2,0},{3,1},{4,6},{5,7},{6,4},{7,5},{8,10},{9,11},{10,... | collective-permute-start | bytes 1622024 | tf_op jit(solution)/shard_map/ppermute | solution.py:844
  31.1 31.4 %collective-permute-start.5 = (bf16[4,88,768]{2,1,0:T(8,128)(2,1)S(1)}, bf16[4,88,768]{2,1,0:T(8,128)(2,1)S(1)}, u32[]{:S(2)}, u32[]{:S(2)}) collective-permute-start(bf16[4,88,768]{2,1,0:T(8,128)(2,1)S(1)} %pad_maximum_fusion), channel_id=1, source_target_pairs={{0,6},{1,7},{2,4},{3,5},{4,2},{5,3},{6,0},{7,1},{8,14},{9,15},{10,... | collective-permute-start | bytes 1622024 | tf_op jit(solution)/shard_map/ppermute | solution.py:844
  62.6 4.5 %collective-permute-start.6 = (bf16[16,88,768]{2,1,0:T(8,128)(2,1)S(1)}, bf16[16,88,768]{2,1,0:T(8,128)(2,1)}, u32[]{:S(2)}, u32[]{:S(2)}) collective-permute-start(bf16[16,88,768]{2,1,0:T(8,128)(2,1)S(1)} %constant_dynamic-update-slice_fusion.refs_1_.refs_3_.refs_5_.refs_7_.refs_9_), channel_id=1, source_target_pairs={{0,1},{1,0},{2,3},{3,2},{4,5},{5,4},{6,7},{7,6},{8,9},{9,8},{10,11... | collective-permute-start | bytes 6488072 | tf_op jit(solution)/shard_map/ppermute | solution.py:844
  146.9 5.5 %collective-permute-start.7 = (bf16[16,120,768]{2,1,0:T(8,128)(2,1)S(1)}, bf16[16,120,768]{2,1,0:T(8,128)(2,1)S(1)}, u32[]{:S(2)}, u32[]{:S(2)}) collective-permute-start(bf16[16,120,768]{2,1,0:T(8,128)(2,1)S(1)} %get-tuple-element.121), channel_id=1, source_target_pairs={{0,1},{1,0},{2,3},{3,2},{4,5},{5,4},{6,7},{7,6},{8,9},{9,8},{10,11... | collective-permute-start | bytes 8847368 | tf_op jit(solution)/shard_map/ppermute | solution.py:844
  153.7 19.6 %collective-permute-start.9 = (bf16[8,56,768]{2,1,0:T(8,128)(2,1)S(1)}, bf16[8,56,768]{2,1,0:T(8,128)(2,1)S(1)}, u32[]{:S(2)}, u32[]{:S(2)}) collective-permute-start(bf16[8,56,768]{2,1,0:T(8,128)(2,1)S(1)} %get-tuple-element.125), channel_id=1, source_target_pairs={{0,4},{1,5},{2,6},{3,7},{4,0},{5,1},{6,2},{7,3},{8,12},{9,13},{10,... | collective-permute-start | bytes 2064392 | tf_op jit(solution)/shard_map/ppermute | solution.py:844
  155.3 19.5 %collective-permute-start.8 = (bf16[8,64,768]{2,1,0:T(8,128)(2,1)S(1)}, bf16[8,64,768]{2,1,0:T(8,128)(2,1)S(1)}, u32[]{:S(2)}, u32[]{:S(2)}) collective-permute-start(bf16[8,64,768]{2,1,0:T(8,128)(2,1)S(1)} %get-tuple-element.124), channel_id=1, source_target_pairs={{0,2},{1,3},{2,0},{3,1},{4,6},{5,7},{6,4},{7,5},{8,10},{9,11},{10,... | collective-permute-start | bytes 2359304 | tf_op jit(solution)/shard_map/ppermute | solution.py:844
  175.6 20.2 %collective-permute-start.11 = (bf16[4,56,768]{2,1,0:T(8,128)(2,1)S(1)}, bf16[4,56,768]{2,1,0:T(8,128)(2,1)S(1)}, u32[]{:S(2)}, u32[]{:S(2)}) collective-permute-start(bf16[4,56,768]{2,1,0:T(8,128)(2,1)S(1)} %get-tuple-element.135), channel_id=1, source_target_pairs={{0,2},{1,3},{2,0},{3,1},{4,6},{5,7},{6,4},{7,5},{8,10},{9,11},{10,... | collective-permute-start | bytes 1032200 | tf_op jit(solution)/shard_map/ppermute | solution.py:844
  176.2 19.6 %collective-permute-start.10 = (bf16[4,64,768]{2,1,0:T(8,128)(2,1)S(1)}, bf16[4,64,768]{2,1,0:T(8,128)(2,1)S(1)}, u32[]{:S(2)}, u32[]{:S(2)}) collective-permute-start(bf16[4,64,768]{2,1,0:T(8,128)(2,1)S(1)} %get-tuple-element.134), channel_id=1, source_target_pairs={{0,4},{1,5},{2,6},{3,7},{4,0},{5,1},{6,2},{7,3},{8,12},{9,13},{10,... | collective-permute-start | bytes 1179656 | tf_op jit(solution)/shard_map/ppermute | solution.py:844
  203.3 4.3 %collective-permute-start.12 = (bf16[16,88,768]{2,1,0:T(8,128)(2,1)S(1)}, bf16[16,88,768]{2,1,0:T(8,128)(2,1)S(1)}, u32[]{:S(2)}, u32[]{:S(2)}) collective-permute-start(bf16[16,88,768]{2,1,0:T(8,128)(2,1)S(1)} %get-tuple-element.146), channel_id=1, source_target_pairs={{0,1},{1,0},{2,3},{3,2},{4,5},{5,4},{6,7},{7,6},{8,9},{9,8},{10,11... | collective-permute-start | bytes 6488072 | tf_op jit(solution)/shard_map/ppermute | solution.py:844
  203.4 11.4 %collective-permute-start.19 = (bf16[1,120,768]{2,1,0:T(8,128)(2,1)S(1)}, bf16[1,120,768]{2,1,0:T(8,128)(2,1)S(1)}, u32[]{:S(2)}, u32[]{:S(2)}) collective-permute-start(bf16[1,120,768]{2,1,0:T(8,128)(2,1)S(1)} %get-tuple-element.167), channel_id=1, source_target_pairs={{0,8},{1,9},{2,10},{3,11},{4,12},{5,13},{6,14},{7,15},{8,0},{9,1},... | collective-permute-start | bytes 552968 | tf_op jit(solution)/shard_map/ppermute | solution.py:844
  204.3 20.0 %collective-permute-start.20 = (bf16[1,120,768]{2,1,0:T(8,128)(2,1)S(1)}, bf16[1,120,768]{2,1,0:T(8,128)(2,1)S(1)}, u32[]{:S(2)}, u32[]{:S(2)}) collective-permute-start(bf16[1,120,768]{2,1,0:T(8,128)(2,1)S(1)} %get-tuple-element.168), channel_id=1, source_target_pairs={{0,16},{1,17},{2,18},{3,19},{4,20},{5,21},{6,22},{7,23},{8,24},{9,... | collective-permute-start | bytes 552968 | tf_op jit(solution)/shard_map/ppermute | solution.py:844
  208.8 30.4 %collective-permute-start.13 = (bf16[4,88,768]{2,1,0:T(8,128)(2,1)S(1)}, bf16[4,88,768]{2,1,0:T(8,128)(2,1)S(1)}, u32[]{:S(2)}, u32[]{:S(2)}) collective-permute-start(bf16[4,88,768]{2,1,0:T(8,128)(2,1)S(1)} %get-tuple-element.147), channel_id=1, source_target_pairs={{0,2},{1,3},{2,0},{3,1},{4,6},{5,7},{6,4},{7,5},{8,10},{9,11},{10,... | collective-permute-start | bytes 1622024 | tf_op jit(solution)/shard_map/ppermute | solution.py:844
  208.9 30.4 %collective-permute-start.14 = (bf16[4,88,768]{2,1,0:T(8,128)(2,1)S(1)}, bf16[4,88,768]{2,1,0:T(8,128)(2,1)S(1)}, u32[]{:S(2)}, u32[]{:S(2)}) collective-permute-start(bf16[4,88,768]{2,1,0:T(8,128)(2,1)S(1)} %get-tuple-element.148), channel_id=1, source_target_pairs={{0,4},{1,5},{2,6},{3,7},{4,0},{5,1},{6,2},{7,3},{8,12},{9,13},{10,... | collective-permute-start | bytes 1622024 | tf_op jit(solution)/shard_map/ppermute | solution.py:844
  210.2 29.0 %collective-permute-start.15 = (bf16[4,88,768]{2,1,0:T(8,128)(2,1)S(1)}, bf16[4,88,768]{2,1,0:T(8,128)(2,1)S(1)}, u32[]{:S(2)}, u32[]{:S(2)}) collective-permute-start(bf16[4,88,768]{2,1,0:T(8,128)(2,1)S(1)} %get-tuple-element.149), channel_id=1, source_target_pairs={{0,6},{1,7},{2,4},{3,5},{4,2},{5,3},{6,0},{7,1},{8,14},{9,15},{10,... | collective-permute-start | bytes 1622024 | tf_op jit(solution)/shard_map/ppermute | solution.py:844
  214.8 9.5 %collective-permute-start.21 = (bf16[1,120,768]{2,1,0:T(8,128)(2,1)S(1)}, bf16[1,120,768]{2,1,0:T(8,128)(2,1)S(1)}, u32[]{:S(2)}, u32[]{:S(2)}) collective-permute-start(bf16[1,120,768]{2,1,0:T(8,128)(2,1)S(1)} %get-tuple-element.170), channel_id=1, source_target_pairs={{0,24},{1,25},{2,26},{3,27},{4,28},{5,29},{6,30},{7,31},{8,16},{9,... | collective-permute-start | bytes 552968 | tf_op jit(solution)/shard_map/ppermute | solution.py:844
  240.0 8.1 %collective-permute-start.16 = (bf16[1,88,768]{2,1,0:T(8,128)(2,1)S(1)}, bf16[1,88,768]{2,1,0:T(8,128)(2,1)S(1)}, u32[]{:S(2)}, u32[]{:S(2)}) collective-permute-start(bf16[1,88,768]{2,1,0:T(8,128)(2,1)S(1)} %get-tuple-element.156), channel_id=1, source_target_pairs={{0,8},{1,9},{2,10},{3,11},{4,12},{5,13},{6,14},{7,15},{8,0},{9,1},... | collective-permute-start | bytes 405512 | tf_op jit(solution)/shard_map/ppermute | solution.py:844
  241.6 13.0 %collective-permute-start.17 = (bf16[1,88,768]{2,1,0:T(8,128)(2,1)S(1)}, bf16[1,88,768]{2,1,0:T(8,128)(2,1)S(1)}, u32[]{:S(2)}, u32[]{:S(2)}) collective-permute-start(bf16[1,88,768]{2,1,0:T(8,128)(2,1)S(1)} %get-tuple-element.157), channel_id=1, source_target_pairs={{0,16},{1,17},{2,18},{3,19},{4,20},{5,21},{6,22},{7,23},{8,24},{9,... | collective-permute-start | bytes 405512 | tf_op jit(solution)/shard_map/ppermute | solution.py:844
  241.9 12.6 %collective-permute-start.18 = (bf16[1,88,768]{2,1,0:T(8,128)(2,1)S(1)}, bf16[1,88,768]{2,1,0:T(8,128)(2,1)S(1)}, u32[]{:S(2)}, u32[]{:S(2)}) collective-permute-start(bf16[1,88,768]{2,1,0:T(8,128)(2,1)S(1)} %get-tuple-element.158), channel_id=1, source_target_pairs={{0,24},{1,25},{2,26},{3,27},{4,28},{5,29},{6,30},{7,31},{8,16},{9,... | collective-permute-start | bytes 405512 | tf_op jit(solution)/shard_map/ppermute | solution.py:844
  (12 other events, 140.5 us)
Sparse Core Ops, SparseCore 0:
  10.9 98.1 all-gather.2
  128.7 119.4 reduce-scatter.1
